TPU v7x, 256 devices: a whole 4x4x8 slice. The times are simulated.
256 devices in a mesh: bt: 16 (over y, x), freq: 16 (over z, core).
Axes of the slice: x: 4, y: 4, z: 8, core: 2. Of those that a mesh axis runs over, the one named last changes fastest.
Arguments:
- uv_grid: bfloat16 [16, 8, 1024, 1024], P('freq', None, 'bt'), may hold values from -6 to 6
- screens: bfloat16 [2, 256, 4, 1024], P(None, ('bt', 'freq')), may hold values from -6 to 6
- residual: bfloat16 [16, 1024, 8, 256], P('freq', 'bt'), may hold values from -0.033935547 to 0.033935547
- uv_coords: float32 [16, 1024, 2, 256], P('freq', 'bt'), may hold values from 0 to 32
- owner_tile: int32 [16, 1024, 1], P('freq', 'bt'), may hold values from 0 to 15; in each aligned block of 64 rows (0 to 63, 64 to 127, ..., all dimensions but the last counted through in order) at most 8 rows name the same one
- row_offset: int32 [16, 1024], P('freq', 'bt'), may hold values from 0 to 32
- column: int32 [16, 1024], P('freq', 'bt'), may hold values from 0 to 992
- stations: int32 [16, 1024, 2], P('freq', 'bt'), may hold values from 0 to 255
- time_slot: int32 [16, 1024], P('freq', 'bt'), may hold values from 0 to 1
Outputs:
- grid_grad: float32 [16, 8, 1024, 1024], P('freq', None, 'bt')
- screen_grad: float32 [2, 256, 4, 1024], P(None, ('bt', 'freq'))
Inputs may be any that keep to these rules, and one draw needn't show every extreme that they name: Among the 64 subgrids of one device at most 8 have the same owner_tile, and in some device exactly 8 do.
All inputs are finite; a program needn't handle non-finite values.
Results may differ from a plain program's by a relative error of at most 0.0077.
Values may be sent and summed in bfloat16 or wider, within the bound.
No kernel may reach another device: no remote copies, remote signals or barrier semaphores. Data moves between devices by JAX's collectives and lax.ppermute only.
A program may use at most 128 MiB of HBM per device.

v0:
```python
import math

import jax
import jax.numpy as jnp
from jax import lax
from jax.sharding import PartitionSpec as P

PIX = 32
TSLOTS = 2


def dft_tables(side_len):
    ramp = jnp.arange(side_len, dtype=jnp.int32)
    product_index = ramp[:, None] * ramp[None, :] % side_len
    angle = product_index.astype(jnp.float32) * (2.0 * math.pi / side_len)
    norm_factor = 1.0 / math.sqrt(side_len)
    return (
        (jnp.cos(angle) * norm_factor).astype(jnp.bfloat16),
        (jnp.sin(angle) * norm_factor).astype(jnp.bfloat16),
    )


def subgrid_terms(patches, vis_rows, uv_rows, screen_p, screen_q, cos_table, sin_table):
    batch_size = vis_rows.shape[0]
    side_len = cos_table.shape[0]
    pixels = side_len * side_len
    samples = vis_rows.shape[2]
    positions = jnp.arange(side_len, dtype=jnp.int32).astype(jnp.float32)
    phase_x = 2.0 * math.pi / side_len * positions[None, :, None] * uv_rows[:, 0:1, :]
    phase_y = 2.0 * math.pi / side_len * positions[None, :, None] * uv_rows[:, 1:2, :]
    wave_x = jnp.stack([jnp.cos(phase_x), jnp.sin(phase_x)], 1).astype(jnp.bfloat16)
    wave_y = jnp.stack([jnp.cos(phase_y), jnp.sin(phase_y)], 1).astype(jnp.bfloat16)
    wave_y = lax.optimization_barrier(wave_y)
    vis_f32 = vis_rows.astype(jnp.float32).reshape(batch_size, 2, 4, 1, samples)
    wave_f32 = wave_y.astype(jnp.float32)[:, :, None, :, :]
    weight_re = vis_f32[:, 0] * wave_f32[:, 0] - vis_f32[:, 1] * wave_f32[:, 1]
    weight_im = vis_f32[:, 0] * wave_f32[:, 1] + vis_f32[:, 1] * wave_f32[:, 0]
    weighted = jnp.stack([weight_re, weight_im], 1).astype(jnp.bfloat16)
    products = jnp.einsum(
        "baxk,bpcyk->bapcxy", wave_x, weighted, preferred_element_type=jnp.float32
    )
    adj_re = (products[:, 0, 0] - products[:, 1, 1]).reshape(batch_size, 4, pixels)
    adj_im = (products[:, 0, 1] + products[:, 1, 0]).reshape(batch_size, 4, pixels)
    grid_re = patches[0:4].reshape(4, batch_size, side_len, side_len)
    grid_im = patches[4:8].reshape(4, batch_size, side_len, side_len)

    def first_left(table, values):
        return jnp.einsum("xu,cbuv->bcxv", table, values, preferred_element_type=jnp.float32)

    def first_right(values, table):
        return jnp.einsum("bcxv,yv->bcxy", values, table, preferred_element_type=jnp.float32)

    def back_left(table, values):
        return jnp.einsum("xu,bcxy->bcuy", table, values, preferred_element_type=jnp.float32)

    def back_right(values, table):
        return jnp.einsum("bcuy,yv->cbuv", values, table, preferred_element_type=jnp.float32)

    mid_re = (first_left(cos_table, grid_re) - first_left(sin_table, grid_im)).astype(jnp.bfloat16)
    mid_im = (first_left(cos_table, grid_im) + first_left(sin_table, grid_re)).astype(jnp.bfloat16)
    sky_re = (first_right(mid_re, cos_table) - first_right(mid_im, sin_table)).reshape(
        batch_size, 4, pixels
    )
    sky_im = (first_right(mid_re, sin_table) + first_right(mid_im, cos_table)).reshape(
        batch_size, 4, pixels
    )
    scr_first = screen_p.astype(jnp.float32)
    scr_second = screen_q.astype(jnp.float32)
    first_re = jnp.repeat(scr_first[:, 0:2], 2, axis=1)
    first_im = jnp.repeat(scr_first[:, 2:4], 2, axis=1)
    second_re = jnp.tile(scr_second[:, 0:2], (1, 2, 1))
    second_im = jnp.tile(scr_second[:, 2:4], (1, 2, 1))
    both_re = first_re * second_re + first_im * second_im
    both_im = first_re * second_im - first_im * second_re
    back_re = (
        (both_re * adj_re - both_im * adj_im)
        .astype(jnp.bfloat16)
        .reshape(batch_size, 4, side_len, side_len)
    )
    back_im = (
        (both_re * adj_im + both_im * adj_re)
        .astype(jnp.bfloat16)
        .reshape(batch_size, 4, side_len, side_len)
    )
    carry_re = second_re * adj_re - second_im * adj_im
    carry_im = second_re * adj_im + second_im * adj_re
    grad_first_re = (sky_re * carry_re + sky_im * carry_im).reshape(batch_size, 2, 2, pixels).sum(2)
    grad_first_im = (sky_re * carry_im - sky_im * carry_re).reshape(batch_size, 2, 2, pixels).sum(2)
    model_re = first_re * sky_re - first_im * sky_im
    model_im = first_re * sky_im + first_im * sky_re
    grad_second_re = (
        (adj_re * model_re + adj_im * model_im).reshape(batch_size, 2, 2, pixels).sum(1)
    )
    grad_second_im = (
        (adj_re * model_im - adj_im * model_re).reshape(batch_size, 2, 2, pixels).sum(1)
    )
    low_re = (back_left(cos_table, back_re) + back_left(sin_table, back_im)).astype(jnp.bfloat16)
    low_im = (back_left(cos_table, back_im) - back_left(sin_table, back_re)).astype(jnp.bfloat16)
    out_re = back_right(low_re, cos_table) + back_right(low_im, sin_table)
    out_im = back_right(low_im, cos_table) - back_right(low_re, sin_table)
    patch_grad = (
        jnp.concatenate([out_re, out_im], 0).reshape(8, batch_size, pixels).astype(jnp.bfloat16)
    )
    grad_first = jnp.concatenate([grad_first_re, grad_first_im], 1)
    grad_second = jnp.concatenate([grad_second_re, grad_second_im], 1)
    return (patch_grad, grad_first, grad_second)


def process(patches, vis_rows, uv_rows, first_row, second_row, tables, cos_table, sin_table, count):
    pixels = patches.shape[2]
    block_len = math.gcd(count, 32)

    def block_step(block_id, state):
        patch_out, screen_acc = state
        block_start = block_id * block_len
        patch_piece = lax.dynamic_slice_in_dim(patches, block_start, block_len, 1)
        vis_piece = lax.dynamic_slice_in_dim(vis_rows, block_start, block_len, 0)
        uv_piece = lax.dynamic_slice_in_dim(uv_rows, block_start, block_len, 0)
        first_piece = lax.dynamic_slice_in_dim(first_row, block_start, block_len, 0)
        second_piece = lax.dynamic_slice_in_dim(second_row, block_start, block_len, 0)
        patch_grad, grad_first, grad_second = subgrid_terms(
            patch_piece,
            vis_piece,
            uv_piece,
            tables[first_piece],
            tables[second_piece],
            cos_table,
            sin_table,
        )
        patch_out = lax.dynamic_update_slice_in_dim(patch_out, patch_grad, block_start, 1)
        screen_acc = screen_acc.at[first_piece].add(grad_first).at[second_piece].add(grad_second)
        return (patch_out, screen_acc)

    start_state = (
        jnp.zeros((8, count, pixels), jnp.bfloat16),
        jnp.zeros((tables.shape[0], 4, pixels), jnp.float32),
    )
    return lax.fori_loop(0, count // block_len, block_step, start_state)


def cut_windows(tile, row_starts, col_starts, count):
    zero = jnp.zeros((), jnp.int32)

    def cut_step(slot, acc):
        window = lax.dynamic_slice(tile, (zero, row_starts[slot], col_starts[slot]), (8, PIX, PIX))
        return lax.dynamic_update_slice(acc, window.reshape(8, 1, PIX * PIX), (zero, slot, zero))

    start = jnp.zeros((8, count, PIX * PIX), tile.dtype)
    return lax.fori_loop(0, count, cut_step, start)


def add_windows(tile_grad, grads, row_starts, col_starts, count):
    zero = jnp.zeros((), jnp.int32)

    def add_step(slot, acc):
        corner = (zero, row_starts[slot], col_starts[slot])
        window = lax.dynamic_slice(acc, corner, (8, PIX, PIX))
        piece = lax.dynamic_slice_in_dim(grads, slot, 1, 1).reshape(8, PIX, PIX).astype(jnp.float32)
        return lax.dynamic_update_slice(acc, window + piece, corner)

    return lax.fori_loop(0, count, add_step, tile_grad)


def per_device(
    uv_grid, screens, residual, uv_coords, owner_tile, row_offset, column, stations, time_slot
):
    n_owners = lax.axis_size("bt")
    sub_count = residual.shape[1]
    capacity = max(2, 2 * sub_count // n_owners)
    slots_all = n_owners * capacity
    tile_rows = uv_grid.shape[2]
    columns = uv_grid.shape[3]
    pixels = PIX * PIX
    tile = uv_grid[0]
    cos_table, sin_table = dft_tables(PIX)
    gathered = lax.all_gather(screens, ("bt", "freq"), axis=1, tiled=True)
    station_total = gathered.shape[1]
    tables = gathered.reshape(TSLOTS * station_total, 4, pixels)
    owners = owner_tile[0, :, 0]
    ordinal = jnp.arange(sub_count, dtype=jnp.int32)
    before = (owners[:, None] == owners[None, :]) & (ordinal[None, :] < ordinal[:, None])
    slot_rank = jnp.sum(before.astype(jnp.int32), axis=1)
    send_slot = owners * capacity + slot_rank
    empty_grad = jnp.zeros((8, tile_rows, columns), jnp.float32)
    request = (
        jnp.zeros((slots_all, 2), jnp.int32)
        .at[send_slot]
        .set(jnp.stack([row_offset[0], column[0]], 1))
    )
    asked_for = lax.all_to_all(
        request.reshape(n_owners, capacity, 2), "bt", split_axis=0, concat_axis=0, tiled=True
    )
    asked_for = asked_for.reshape(slots_all, 2)
    cut_patches = cut_windows(tile, asked_for[:, 0], asked_for[:, 1], slots_all).reshape(
        8, n_owners, capacity, pixels
    )
    fetched = lax.all_to_all(cut_patches, "bt", split_axis=1, concat_axis=1, tiled=True).reshape(
        8, slots_all, pixels
    )
    patches = jnp.take(fetched, send_slot, axis=1)
    first_row = time_slot[0] * station_total + stations[0, :, 0]
    second_row = time_slot[0] * station_total + stations[0, :, 1]
    patch_grad, screen_acc = process(
        patches,
        residual[0],
        uv_coords[0],
        first_row,
        second_row,
        tables,
        cos_table,
        sin_table,
        sub_count,
    )
    outgoing = jnp.zeros((8, slots_all, pixels), jnp.bfloat16).at[:, send_slot].set(patch_grad)
    returned = lax.all_to_all(
        outgoing.reshape(8, n_owners, capacity, pixels),
        "bt",
        split_axis=1,
        concat_axis=1,
        tiled=True,
    )
    returned = returned.reshape(8, slots_all, pixels)
    tile_grad = add_windows(empty_grad, returned, asked_for[:, 0], asked_for[:, 1], slots_all)
    screen_grad = lax.psum_scatter(
        screen_acc.reshape(TSLOTS, station_total, 4, pixels),
        ("bt", "freq"),
        scatter_dimension=1,
        tiled=True,
    )
    return (tile_grad.reshape(1, 8, tile_rows, columns), screen_grad)


def solution(mesh):
    in_specs = (
        P("freq", None, "bt", None),
        P(None, ("bt", "freq"), None, None),
        P("freq", "bt", None, None),
        P("freq", "bt", None, None),
        P("freq", "bt", None),
        P("freq", "bt"),
        P("freq", "bt"),
        P("freq", "bt", None),
        P("freq", "bt"),
    )
    out_specs = (P("freq", None, "bt", None), P(None, ("bt", "freq"), None, None))
    return jax.shard_map(
        per_device, mesh=mesh, in_specs=in_specs, out_specs=out_specs, check_vma=False
    )
```

profile of v0, /device:TPU:211, one launch (start us, length us, event | category | flops | bytes accessed | tf_op | source)
XLA Modules:
  0.0 2425.6 jit_solution(16052809922389562258)
XLA Ops:
  11.1 6.7 all-to-all-start
  23.0 875.8 %while.43 = (s32[]{:T(128)}, bf16[8,128,1024]{2,0,1:T(8,128)(2,1)}, s32[128]{0:T(128)S(1)}, s32[128]{0:T(128)S(1)}, bf16[8,64,1024]{2,1,0:T(8,128)(2,1)}, /*index=5*/s32[]{:T(128)}, s32[]{:T(128)}, s32[]{:T(128)}, s32[]{:T(128)}) while((s32[]{:T(128)}, bf16[8,128,1024]{2,0,1:T(8,128)(2,1)}, s32[128]{0:T(128)S(1)}, s32[128]{0:T(128)S(1)}, ...), condition=%wide.region_3.4_spmd, body=%wide.region_2.3_spmd.sunk | while | flops 8 | bytes 99009 | solution.py:149
  899.4 6.4 all-to-all-start.1
  905.9 26.2 %all-to-all-done.1 = bf16[8,16,8,1024]{3,0,2,1:T(8,128)(2,1)S(1)} async-done(((bf16[8,16,8,1024]{3,0,2,1:T(8,128)(2,1)}), bf16[8,16,8,1024]{3,0,2,1:T(8,128)(2,1)S(1)}, u32[]{:S(2)}, u32[]{:S(2)}) %all-to-all-start.1) | async-done | bytes 2097184 | tf_op jit(solution)/shard_map/all_to_all | solution.py:197
  933.9 5.4 broadcast_in_dim.75
  940.4 236.9 %while.45 = (s32[]{:T(128)}, bf16[8,64,1024]{2,0,1:T(8,128)(2,1)}, f32[512,4,1024]{2,1,0:T(4,128)}, s32[64]{0:T(128)S(1)}, bf16[512,4,1024]{2,1,0:T(4,128)(2,1)}...) while((s32[]{:T(128)}, bf16[8,64,1024]{2,0,1:T(8,128)(2,1)}, ...), condition=%wide.region_11.12_spmd.clone.clone, body=%wide.region_4.11_spmd.clone.clone.sunk | while | flops 432605440 | bytes 96282664 | solution.py:138
  962.2 7.8 fusion.247
  974.9 4.5 fusion.248
  991.9 7.9 fusion.249
  1047.3 5.2 scatter_fusion
  1052.6 5.2 scatter_fusion.1
  1069.8 7.8 fusion.247
  1082.4 4.5 fusion.248
  1099.4 7.9 fusion.249
  1154.8 5.3 scatter_fusion
  1160.1 5.2 scatter_fusion.1
  1178.9 8.1 scatter_fusion.2
  1187.0 7.4 all-to-all-start.2
  1195.3 27.8 %all-to-all-done.2 = bf16[8,16,8,1024]{3,0,2,1:T(8,128)(2,1)S(1)} async-done(((bf16[8,16,8,1024]{3,0,2,1:T(8,128)(2,1)}), bf16[8,16,8,1024]{3,0,2,1:T(8,128)(2,1)S(1)}, u32[]{:S(2)}, u32[]{:S(2)}) %all-to-all-start.2) | async-done | bytes 2097184 | tf_op jit(solution)/shard_map/all_to_all | solution.py:215
  1224.6 1192.3 %while.44 = (s32[]{:T(128)}, f32[8,64,1024]{2,1,0:T(8,128)S(1)}, s32[128]{0:T(128)S(1)}, s32[128]{0:T(128)S(1)}, bf16[8,128,1024]{2,0,1:T(8,128)(2,1)}, /*index=5*/s32[]{:T(128)}, s32[]{:T(128)}, s32[]{:T(128)}, s32[]{:T(128)}) while((s32[]{:T(128)}, f32[8,64,1024]{2,1,0:T(8,128)S(1)}, s32[128]{0:T(128)S(1)}, s32[128]{0:T(128)S(1)}, ...), condition=%wide.region_14.15_spmd, body=%wide.region_13.14_spmd.sunk | while | flops 16392 | bytes 278729 | solution.py:161
  1351.6 3.4 dynamic_update_slice.29
  1361.0 3.4 dynamic_update_slice.29
  1407.7 3.4 dynamic_update_slice.29
  1417.0 3.4 dynamic_update_slice.29
  1501.0 3.4 dynamic_update_slice.29
  1566.1 3.4 dynamic_update_slice.29
  1584.8 3.4 dynamic_update_slice.29
  1659.1 3.4 dynamic_update_slice.29
  1761.5 3.4 dynamic_update_slice.29
  1780.2 3.4 dynamic_update_slice.29
  1919.7 3.4 dynamic_update_slice.29
  1929.1 3.4 dynamic_update_slice.29
  (1611 shorter events, 1211.5 us)
Async XLA Ops:
  8.7 897.1 %copy-start.14 = (s32[64]{0:T(128)}, s32[64]{0:T(128)S(1)}, u32[]{:S(2)}) copy-start(s32[64]{0:T(128)S(1)} %fusion.145) | copy-start | bytes 772
  11.1 10.3 all-to-all-start
  17.8 916.2 %all-gather.2.cloned.1.call-start = ((), (), s32[]{:S(2)}) async-start(), calls=%async_computation.3 | async-start | bytes 4210688 | tf_op jit(solution)/shard_map/all_gather | solution.py:176
  898.8 7.0 copy-start.13
  898.8 7.1 copy-start.22
  898.8 7.1 copy-start.16
  898.8 7.1 copy-start.17
  899.4 32.7 %all-to-all-start.1 = ((bf16[8,16,8,1024]{3,0,2,1:T(8,128)(2,1)}), bf16[8,16,8,1024]{3,0,2,1:T(8,128)(2,1)S(1)}, u32[]{:S(2)}, u32[]{:S(2)}) async-start(bf16[8,16,8,1024]{3,0,2,1:T(8,128)(2,1)} %bitcast.20), calls=%async_computation.1 | async-start | bytes 4194304 | tf_op jit(solution)/shard_map/all_to_all | solution.py:197
  986.1 0.7 copy-start.7
  1016.2 3.1 copy-start.9
  1025.3 1.0 copy-start.2
  1026.2 1.2 copy-start.5
  1027.5 1.2 copy-start.1
  1029.2 1.0 copy-start.3
  1035.3 1.8 copy-start.4
  1057.8 1.6 copy-start
  1093.6 0.7 copy-start.7
  1123.7 3.1 copy-start.9
  1132.7 1.0 copy-start.2
  1133.7 1.2 copy-start.5
  1134.9 1.2 copy-start.1
  1136.7 1.0 copy-start.3
  1142.8 1.8 copy-start.4
  1165.3 1.6 copy-start
  1177.3 1.6 copy-start.10
  1177.3 1.6 copy-start.15
  1187.0 36.0 %all-to-all-start.2 = ((bf16[8,16,8,1024]{3,0,2,1:T(8,128)(2,1)}), bf16[8,16,8,1024]{3,0,2,1:T(8,128)(2,1)S(1)}, u32[]{:S(2)}, u32[]{:S(2)}) async-start(bf16[8,16,8,1024]{3,0,2,1:T(8,128)(2,1)} %bitcast.24), calls=%async_computation.2 | async-start | bytes 4194304 | tf_op jit(solution)/shard_map/all_to_all | solution.py:215
  1194.5 1222.4 %all-reduce.3.cloned.1.call-start = ((), (), s32[]{:S(2)}) async-start(), calls=%async_computation.4 | async-start | bytes 16777216
  1195.2 29.3 %copy-start.19 = (s32[128]{0:T(128)S(1)}, s32[128]{0:T(128)}, u32[]{:S(2)}) copy-start(s32[128]{0:T(128)} %copy-done.18) | copy-start | bytes 1540
  1195.2 29.3 %copy-start.21 = (s32[128]{0:T(128)S(1)}, s32[128]{0:T(128)}, u32[]{:S(2)}) copy-start(s32[128]{0:T(128)} %copy-done.20) | copy-start | bytes 1540
  1223.0 1.3 copy-start.12
  2416.9 1.5 copy-start.11
  (6 other events, 3.9 us)
Sparse Core Ops, SparseCore 0:
  22.4 107.4 all-gather.1
  1200.8 282.0 all-reduce.2
where the time goes:
time: 2460 us; the launch traced here: 2430 us
  local copies, waits for them, and re-layouts  1100 us (45%)
  loops' own time  1010 us (41%)
  other arithmetic  184 us (7%)
  waiting for transfers between devices  58.1 us (2%)
  matrix products  42.5 us (2%)
    another operation x1, loops' own time, cut_windows(): return lax.fori_loop(0, count, cut_step, start)  498 us
    another operation x1, loops' own time, add_windows(): return lax.fori_loop(0, count, add_step, tile_grad)  489 us
    dynamic_update_slice x128, local copies, waits for them, and re-layouts, add_step(): return lax.dynamic_update_slice(acc, window + piece, corner)  425 us
    dynamic_slice x256, local copies, waits for them, and re-layouts, add_step(): corner = (zero, row_starts[slot], col_starts[slot])  159 us
    dynamic_slice x128, local copies, waits for them, and re-layouts, cut_step(): lax.dynamic_slice(tile, (zero, row_starts[slot], col_starts[slot]), (8, P...  133 us
    convert_element_type x128, other arithmetic, add_step(): lax.dynamic_slice_in_dim(grads, slot, 1, 1).reshape(8, PIX, PIX)  93.1 us
    dynamic_update_slice x128, local copies, waits for them, and re-layouts, cut_step(): lax.dynamic_update_slice(acc, window.reshape(8, 1, PIX * PIX), (zero, slo...  77.9 us
    dynamic_slice x128, local copies, waits for them, and re-layouts, cut_step(): row_starts[slot]  75.3 us
  transfers between devices with their start and end apart: 5, of which 3 were waited for; matrix products, arithmetic and copies ran while one was open for 45% of the time, Pallas kernels for 0%

commit v1 on v0

v1 whole, which is shorter than its diff:
```python
import math

import jax
import jax.numpy as jnp
import numpy as np
from jax import lax
from jax.experimental import pallas as pl
from jax.experimental.pallas import tpu as pltpu
from jax.sharding import PartitionSpec as P

PIX = 32
TSLOTS = 2
COMPS = 8
LANES = 128
CAP = 8
F32 = jnp.float32
BF16 = jnp.bfloat16


def constant_tables():
    ramp = np.arange(PIX)
    angle = (ramp[:, None] * ramp[None, :] % PIX) * (2.0 * math.pi / PIX)
    cos_part = (np.cos(angle) / math.sqrt(PIX)).astype(np.float32)
    sin_part = (np.sin(angle) / math.sqrt(PIX)).astype(np.float32)
    forward = np.block([[cos_part, -sin_part], [sin_part, cos_part]])
    backward = np.block([[cos_part, sin_part], [-sin_part, cos_part]])
    eye = np.eye(4, dtype=np.float32)
    right = np.concatenate([np.kron(eye, cos_part), np.kron(eye, sin_part)], 1)
    block = np.eye(PIX, dtype=np.float32)

    def spread(picks):
        out = np.zeros((LANES, len(picks) * PIX), np.float32)
        for j, i in enumerate(picks):
            out[i * PIX : (i + 1) * PIX, j * PIX : (j + 1) * PIX] = block
        return out

    spread_first = spread([0, 0, 1, 1, 2, 2, 3, 3])
    spread_second = spread([0, 1, 0, 1, 2, 3, 2, 3])
    as_bf16 = [
        jnp.asarray(v, BF16) for v in (forward, backward, right, spread_first, spread_second)
    ]
    return as_bf16


def dot(a, b):
    return jnp.dot(a, b, preferred_element_type=F32)


def route_kernel(owner, row_offset, column, station_a, station_b, slot_time, request, slot, first, second, fill):
    count = owner.shape[0]

    def clear(i, carry):
        request[i] = -1
        return carry

    lax.fori_loop(0, request.shape[0], clear, 0)

    def zero(i, carry):
        fill[i] = 0
        return carry

    lax.fori_loop(0, fill.shape[0], zero, 0)

    def step(s, carry):
        o = owner[s]
        place = o * CAP + fill[o]
        fill[o] = fill[o] + 1
        slot[s] = place
        request[place] = row_offset[s] * 1024 + column[s]
        first[s] = station_a[s] * TSLOTS + slot_time[s]
        second[s] = station_b[s] * TSLOTS + slot_time[s]
        return carry

    lax.fori_loop(0, count, step, 0)


def route(owners, row_offset, column, station_a, station_b, slot_time, n_owners):
    count = owners.shape[0]
    smem = pl.BlockSpec(memory_space=pltpu.SMEM)
    ints = lambda n: jax.ShapeDtypeStruct((n,), jnp.int32)
    return pl.pallas_call(
        route_kernel,
        out_shape=(ints(n_owners * CAP), ints(count), ints(count), ints(count)),
        in_specs=[smem] * 6,
        out_specs=(smem,) * 4,
        scratch_shapes=[pltpu.SMEM((n_owners,), jnp.int32)],
        name="route",
    )(owners, row_offset, column, station_a, station_b, slot_time)


def listed(asked, order):
    def step(i, n):
        order[n] = i
        return n + (asked[i] >= 0).astype(jnp.int32)

    return lax.fori_loop(0, asked.shape[0], step, jnp.int32(0))


def for_listed(n, group, body):
    def whole(g, carry):
        body([g * group + k for k in range(group)])
        return carry

    lax.fori_loop(0, n // group, whole, 0)

    def rest(i, carry):
        body([i])
        return carry

    lax.fori_loop(n // group * group, n, rest, 0)


def cut_kernel(asked, tile, out, wide, order):
    comps, rows, columns = tile.shape
    panels = columns // LANES
    for j in range(panels):
        wide[j] = tile[:, :, j * LANES : (j + 1) * LANES].astype(F32).reshape(comps * rows, LANES)
    n = listed(asked, order)
    line = lax.broadcasted_iota(jnp.int32, (LANES, LANES), 0)
    lane = lax.broadcasted_iota(jnp.int32, (LANES, LANES), 1)
    ahead = line - lane % PIX
    block = lax.broadcasted_iota(jnp.int32, (PIX, LANES), 1) // PIX

    def body(places):
        for place in places:
            i = order[place]
            code = asked[i]
            r, c0 = code // 1024, code % 1024
            j, shift = c0 // LANES, c0 % LANES
            after = jnp.minimum(j + 1, panels - 1)

            def rows_of(panel):
                return jnp.concatenate(
                    [wide[panel, pl.ds(c * rows + r, PIX), :] for c in range(comps)], 0
                ).astype(BF16)

            both = jnp.concatenate([rows_of(j), rows_of(after)], 1)
            pick = jnp.concatenate([ahead == shift, ahead + LANES == shift], 0)
            moved = dot(both, jnp.where(pick, 1.0, 0.0).astype(BF16))
            parts = []
            for ri in range(2):
                part = moved[ri * 128 : ri * 128 + PIX]
                for m in range(1, 4):
                    start = (ri * 4 + m) * PIX
                    part = jnp.where(block == m, moved[start : start + PIX], part)
                parts.append(part)
            out[i] = jnp.concatenate(parts, 0).astype(BF16)

    for_listed(n, 4, body)


def cut_windows(asked, tile):
    comps, rows, columns = tile.shape
    slots = asked.shape[0]
    return pl.pallas_call(
        cut_kernel,
        out_shape=jax.ShapeDtypeStruct((slots, 2 * PIX, LANES), BF16),
        in_specs=[pl.BlockSpec(memory_space=pltpu.SMEM), pl.BlockSpec(memory_space=pltpu.VMEM)],
        out_specs=pl.BlockSpec(memory_space=pltpu.VMEM),
        scratch_shapes=[
            pltpu.VMEM((columns // LANES, comps * rows, LANES), F32),
            pltpu.SMEM((slots + 1,), jnp.int32),
        ],
        name="cut",
    )(asked, tile)


def add_kernel(asked, pieces, out, wide, order):
    comps, rows, columns = out.shape
    panels = columns // LANES
    for j in range(panels):
        wide[j] = jnp.zeros((comps * rows, LANES), F32)
    n = listed(asked, order)
    line = lax.broadcasted_iota(jnp.int32, (LANES, LANES), 0)
    lane = lax.broadcasted_iota(jnp.int32, (LANES, LANES), 1)
    ahead = lane - line % PIX
    block = lax.broadcasted_iota(jnp.int32, (PIX, LANES), 1) // PIX

    def body(places):
        spread = []
        for place in places:
            i = order[place]
            code = asked[i]
            r, c0 = code // 1024, code % 1024
            j, shift = c0 // LANES, c0 % LANES
            piece = pieces[i].astype(F32)
            lines = []
            for ri in range(2):
                for m in range(4):
                    lines.append(jnp.where(block == m, piece[ri * PIX : (ri + 1) * PIX], 0.0))
            lines = jnp.concatenate(lines, 0).astype(BF16)
            moved = dot(lines, jnp.where(ahead == shift, 1.0, 0.0).astype(BF16))
            spread.append((r, j, shift, lines, moved))
        for r, j, shift, lines, moved in spread:
            for c in range(comps):
                at = pl.ds(c * rows + r, PIX)
                wide[j, at, :] = wide[j, at, :] + moved[c * PIX : (c + 1) * PIX]
        for r, j, shift, lines, moved in spread:

            @pl.when(shift > LANES - PIX)
            def _(r=r, j=j, shift=shift, lines=lines):
                over = dot(lines, jnp.where(ahead + LANES == shift, 1.0, 0.0).astype(BF16))
                for c in range(comps):
                    at = pl.ds(c * rows + r, PIX)
                    wide[j + 1, at, :] = wide[j + 1, at, :] + over[c * PIX : (c + 1) * PIX]

    for_listed(n, 4, body)
    for j in range(panels):
        out[:, :, j * LANES : (j + 1) * LANES] = wide[j].reshape(comps, rows, LANES)


def add_windows(asked, pieces, comps, rows, columns):
    slots = asked.shape[0]
    return pl.pallas_call(
        add_kernel,
        out_shape=jax.ShapeDtypeStruct((comps, rows, columns), F32),
        in_specs=[pl.BlockSpec(memory_space=pltpu.SMEM), pl.BlockSpec(memory_space=pltpu.VMEM)],
        out_specs=pl.BlockSpec(memory_space=pltpu.VMEM),
        scratch_shapes=[
            pltpu.VMEM((columns // LANES, comps * rows, LANES), F32),
            pltpu.SMEM((slots + 1,), jnp.int32),
        ],
        name="add",
    )(asked, pieces)


def turn_waves(turns):
    part = turns - jnp.round(turns)
    z = part * part
    coef_sin = [(-1.0) ** k * math.pi ** (2 * k + 1) / math.factorial(2 * k + 1) for k in range(7)]
    coef_cos = [(-1.0) ** k * math.pi ** (2 * k) / math.factorial(2 * k) for k in range(8)]
    s = jnp.full_like(z, coef_sin[-1])
    for v in coef_sin[-2::-1]:
        s = s * z + v
    s = s * part
    c = jnp.full_like(z, coef_cos[-1])
    for v in coef_cos[-2::-1]:
        c = c * z + v
    return 1.0 - 2.0 * s * s, 2.0 * s * c


def image_kernel(group, vis, uv, out):
    samples = vis.shape[2]
    position = lax.broadcasted_iota(jnp.int32, (PIX, samples), 0).astype(F32) * (1.0 / PIX)

    def step(g, carry):
        for k in range(group):
            s = g * group + k
            uv_rows = uv[s]
            x_cos, x_sin = turn_waves(position * uv_rows[0:1])
            y_cos, y_sin = turn_waves(position * uv_rows[1:2])
            wave_x = jnp.concatenate([x_cos, x_sin], 0).astype(BF16)
            y_cos, y_sin = y_cos.astype(BF16).astype(F32), y_sin.astype(BF16).astype(F32)
            rows = vis[s].astype(F32)
            weight_re, weight_im = [], []
            for m in range(4):
                re, im = rows[m : m + 1], rows[m + 4 : m + 5]
                weight_re.append(re * y_cos - im * y_sin)
                weight_im.append(re * y_sin + im * y_cos)
            weighted = jnp.concatenate(weight_re + weight_im, 0).astype(BF16)
            products = lax.dot_general(
                wave_x, weighted, (((1,), (1,)), ((), ())), preferred_element_type=F32
            )
            low, high = products[:PIX], products[PIX:]
            out[s, 0:PIX] = low[:, :LANES] - high[:, LANES:]
            out[s, PIX:] = low[:, LANES:] + high[:, :LANES]
        return carry

    lax.fori_loop(0, vis.shape[0] // group, step, 0)


def adjoint_images(vis, uv):
    count = vis.shape[0]
    group = math.gcd(count, 4)
    vmem = pl.BlockSpec(memory_space=pltpu.VMEM)
    return pl.pallas_call(
        lambda *refs: image_kernel(group, *refs),
        out_shape=jax.ShapeDtypeStruct((count, 2 * PIX, LANES), F32),
        in_specs=[vmem, vmem],
        out_specs=vmem,
        name="image",
    )(vis, uv)


def screens_of(table, row, spread):
    wide = dot(table[row], spread[...])
    return wide[:, :LANES], wide[:, LANES:]


def patch_kernel(group, slot, first, second, image, table, backward, right, spread_a, spread_b, out):
    def step(g, carry):
        for k in range(group):
            s = g * group + k
            a_re, a_im = screens_of(table, first[s], spread_a)
            b_re, b_im = screens_of(table, second[s], spread_b)
            m_re, m_im = image[s, 0:PIX], image[s, PIX:]
            both_re = a_re * b_re + a_im * b_im
            both_im = a_re * b_im - a_im * b_re
            back_re = both_re * m_re - both_im * m_im
            back_im = both_re * m_im + both_im * m_re
            back = jnp.concatenate([back_re, back_im], 0).astype(BF16)
            low = dot(backward[...], back).astype(BF16)
            grad = dot(low, right[...])
            re, im = grad[:PIX], grad[PIX:]
            grad_re = re[:, :LANES] + im[:, LANES:]
            grad_im = im[:, :LANES] - re[:, LANES:]
            out[slot[s]] = jnp.concatenate([grad_re, grad_im], 0).astype(BF16)
        return carry

    lax.fori_loop(0, image.shape[0] // group, step, 0)


def patch_gradients(slot, first, second, image, table, consts, slots):
    forward, backward, right, spread_a, spread_b = consts
    group = math.gcd(image.shape[0], 4)
    vmem, smem = pl.BlockSpec(memory_space=pltpu.VMEM), pl.BlockSpec(memory_space=pltpu.SMEM)
    return pl.pallas_call(
        lambda *refs: patch_kernel(group, *refs),
        out_shape=jax.ShapeDtypeStruct((slots, 2 * PIX, LANES), BF16),
        in_specs=[smem] * 3 + [vmem] * 6,
        out_specs=vmem,
        name="patch",
    )(slot, first, second, image, table, backward, right, spread_a, spread_b)


def screen_kernel(group, slot, first, second, image, patches, table, forward, right, spread_a, spread_b, out, acc):
    chunk = 32

    def clear(i, carry):
        acc[pl.ds(i * chunk, chunk)] = jnp.zeros((chunk, PIX, LANES), F32)
        return carry

    lax.fori_loop(0, acc.shape[0] // chunk, clear, 0)
    block = lax.broadcasted_iota(jnp.int32, (PIX, LANES), 1) // PIX

    def step(g, carry):
        terms = []
        for k in range(group):
            s = g * group + k
            a_re, a_im = screens_of(table, first[s], spread_a)
            b_re, b_im = screens_of(table, second[s], spread_b)
            m_re, m_im = image[s, 0:PIX], image[s, PIX:]
            mid = dot(forward[...], patches[slot[s]]).astype(BF16)
            wide = dot(mid, right[...])
            re, im = wide[:PIX], wide[PIX:]
            sky_re = re[:, :LANES] - im[:, LANES:]
            sky_im = re[:, LANES:] + im[:, :LANES]
            carry_re = b_re * m_re - b_im * m_im
            carry_im = b_re * m_im + b_im * m_re
            ga_re = sky_re * carry_re + sky_im * carry_im
            ga_im = sky_re * carry_im - sky_im * carry_re
            model_re = a_re * sky_re - a_im * sky_im
            model_im = a_re * sky_im + a_im * sky_re
            gb_re = m_re * model_re + m_im * model_im
            gb_im = m_re * model_im - m_im * model_re
            ta = jnp.where(
                block % 2 == 0,
                ga_re + pltpu.roll(ga_re, LANES - PIX, 1),
                ga_im + pltpu.roll(ga_im, PIX, 1),
            )
            ta = jnp.where(
                block == 1,
                pltpu.roll(ta, LANES - PIX, 1),
                jnp.where(block == 2, pltpu.roll(ta, PIX, 1), ta),
            )
            tb = jnp.where(
                block < 2,
                gb_re + pltpu.roll(gb_re, 2 * PIX, 1),
                gb_im + pltpu.roll(gb_im, 2 * PIX, 1),
            )
            terms.append((s, ta, tb))
        for s, ta, tb in terms:
            acc[first[s]] = acc[first[s]] + ta
            acc[second[s]] = acc[second[s]] + tb
        return carry

    lax.fori_loop(0, image.shape[0] // group, step, 0)

    def give(i, carry):
        at = pl.ds(i * chunk, chunk)
        out[at] = acc[at].astype(BF16)
        return carry

    lax.fori_loop(0, acc.shape[0] // chunk, give, 0)


def screen_gradients(slot, first, second, image, patches, table, consts):
    forward, backward, right, spread_a, spread_b = consts
    group = math.gcd(image.shape[0], 4)
    vmem, smem = pl.BlockSpec(memory_space=pltpu.VMEM), pl.BlockSpec(memory_space=pltpu.SMEM)
    return pl.pallas_call(
        lambda *refs: screen_kernel(group, *refs),
        out_shape=jax.ShapeDtypeStruct(table.shape, BF16),
        in_specs=[smem] * 3 + [vmem] * 7,
        out_specs=vmem,
        scratch_shapes=[pltpu.VMEM(table.shape, F32)],
        name="screen",
    )(slot, first, second, image, patches, table, forward, right, spread_a, spread_b)


def exchange(x, axis):
    return lax.all_to_all(x, axis, split_axis=0, concat_axis=0, tiled=True)


def per_device(
    uv_grid, screens, residual, uv_coords, owner_tile, row_offset, column, stations, time_slot
):
    n_bt, n_freq = lax.axis_size("bt"), lax.axis_size("freq")
    slots = n_bt * CAP
    consts = constant_tables()
    held = screens.shape[1]
    own = screens.reshape(TSLOTS, held, 4, PIX, PIX).transpose(1, 0, 3, 2, 4)
    own = own.reshape(held, TSLOTS, PIX, LANES)
    table = lax.all_gather(own, "freq", axis=0, tiled=True)
    table = lax.all_gather(table, "bt", axis=0, tiled=True)
    table = table.reshape(-1, PIX, LANES)
    request, slot, first, second = route(
        owner_tile[0, :, 0],
        row_offset[0],
        column[0],
        stations[0, :, 0],
        stations[0, :, 1],
        time_slot[0],
        n_bt,
    )
    asked = exchange(request.reshape(n_bt, CAP), "bt").reshape(slots)
    image = adjoint_images(residual[0], uv_coords[0])
    cut = cut_windows(asked, uv_grid[0])
    fetched = exchange(cut.reshape(n_bt, CAP, 2 * PIX, LANES), "bt").reshape(slots, 2 * PIX, LANES)
    grads = patch_gradients(slot, first, second, image, table, consts, slots)
    returned = exchange(grads.reshape(n_bt, CAP, 2 * PIX, LANES), "bt").reshape(slots, 2 * PIX, LANES)
    terms = screen_gradients(slot, first, second, image, fetched, table, consts)
    grid_grad = add_windows(asked, returned, *uv_grid.shape[1:])
    part = exchange(terms.reshape(n_bt, -1, TSLOTS, PIX, LANES), "bt")
    part = jnp.sum(part.astype(F32), 0).astype(BF16)
    part = exchange(part.reshape(n_freq, held, TSLOTS, PIX, LANES), "freq")
    part = jnp.sum(part.astype(F32), 0).reshape(held, TSLOTS, PIX, 4, PIX)
    screen_grad = part.transpose(1, 0, 3, 2, 4).reshape(TSLOTS, held, 4, PIX * PIX)
    return grid_grad[None], screen_grad


def solution(mesh):
    in_specs = (
        P("freq", None, "bt", None),
        P(None, ("bt", "freq"), None, None),
        P("freq", "bt", None, None),
        P("freq", "bt", None, None),
        P("freq", "bt", None),
        P("freq", "bt"),
        P("freq", "bt"),
        P("freq", "bt", None),
        P("freq", "bt"),
    )
    out_specs = (P("freq", None, "bt", None), P(None, ("bt", "freq"), None, None))
    return jax.shard_map(
        per_device, mesh=mesh, in_specs=in_specs, out_specs=out_specs, check_vma=False
    )
```

time: 2460 us -> 254 us (0.10)
  the two profiles are of different devices: /device:TPU:211 before, /device:TPU:1 now
where the time goes in v1:
time: 254 us; the launch traced here: 253 us
  waiting for transfers between devices  95.8 us (38%)
  Pallas kernels  67.7 us (27%)
  blocking collectives  36.4 us (14%)
  starting transfers between devices  28.5 us (11%)
  between operations  14.1 us (6%)
  local copies, waits for them, and re-layouts  6.2 us (2%)
  other arithmetic  4.59 us (2%)
    all_to_all x4, waiting for transfers between devices, exchange(): return lax.all_to_all(x, axis, split_axis=0, concat_axis=0, tiled=True)  95.8 us
    all_to_all x4, starting transfers between devices, exchange(): return lax.all_to_all(x, axis, split_axis=0, concat_axis=0, tiled=True)  28.4 us
    pallas_call x1, Pallas kernels, patch_gradients(): pl.pallas_call(lambda *refs: patch_kernel(group, *refs), out_shape=jax.Sh...  23.6 us
    all_gather x1, blocking collectives, per_device(): table = lax.all_gather(own, 'freq', axis=0, tiled=True)  23.4 us
    pallas_call x1, Pallas kernels, screen_gradients(): pl.pallas_call(lambda *refs: screen_kernel(group, *refs), out_shape=jax.S...  16.3 us
    all_to_all x1, blocking collectives, exchange(): return lax.all_to_all(x, axis, split_axis=0, concat_axis=0, tiled=True)  13 us
    pallas_call x1, Pallas kernels, adjoint_images(): pl.pallas_call(lambda *refs: image_kernel(group, *refs), out_shape=jax.Sh...  11.5 us
    pallas_call x1, Pallas kernels, add_windows(): pl.pallas_call(add_kernel, out_shape=jax.ShapeDtypeStruct((comps, rows, c...  7.3 us
  transfers between devices with their start and end apart: 5, of which 4 were waited for; matrix products, arithmetic and copies ran while one was open for 3% of the time, Pallas kernels for 20%

profile of v1, /device:TPU:1, one launch (start us, length us, event | category | flops | bytes accessed | tf_op | source)
XLA Modules:
  0.0 253.3 jit_solution(10282470199133039065)
XLA Ops:
  7.2 0.0 all-gather.2.cloned.1.call-start
  7.2 0.8 reshape.48
  8.1 0.1 reshape.49
  8.2 23.4 %all_gather.6 = bf16[16,2,32,128]{3,2,1,0:T(8,128)(2,1)} all-gather(bf16[1,2,32,128]{3,2,1,0:T(8,128)(2,1)S(1)} %reshape.49), channel_id=1, replica_groups=mesh['bt'=16,'freq'=16] {'freq'}, dimensions={0}, use_global_device_ids=true | all-gather | bytes 278528 | tf_op jit(solution)/shard_map/all_gather | solution.py:414
  31.6 0.0 all-gather.2.cloned.1.call-update
  31.6 1.3 slice_bitcast_fusion
  32.9 3.0 %route.1 = (s32[128]{0:T(128)}, s32[64]{0:T(128)}, s32[64]{0:T(128)}, s32[64]{0:T(128)}) custom-call(s32[64]{0:T(128)} %bitcast.44, s32[64]{0:T(128)} %bitcast.45, s32[64]{0:T(128)} %bitcast.46, s32[64]{0:T(128)} %get-tuple-element.15.station_a, s32[64]{0:T(128)} %get-tuple-element.14.station_b, s32[64]{0:T(128)} %bitcast.47), custom_call_target="tpu_custom_call" | custom-call | tf_op jit(solution)/shard_map/route/pallas_call | solution.py:81
  35.9 0.7 all_to_all.18
  36.6 13.0 %all_to_all.29 = s32[16,1,8]{2,1,0:T(1,128)S(1)} all-to-all(s32[16,1,8]{2,1,0:T(1,128)S(1)} %bitcast.43), channel_id=1, replica_groups=mesh['bt'=16,'freq'=16] {'bt'}, dimensions={0} | all-to-all | bytes 1024 | tf_op jit(solution)/shard_map/all_to_all | solution.py:402
  49.5 0.5 broadcast.3
  50.1 0.7 reduce.5
  50.7 0.6 reshape.47.asked
  51.3 6.0 %cut.1 = bf16[128,64,128]{2,1,0:T(8,128)(2,1)} custom-call(s32[128]{0:T(128)} %reshape.47.asked, bf16[8,64,1024]{2,1,0:T(8,128)(2,1)} %bitcast.37), custom_call_target="tpu_custom_call" | custom-call | tf_op jit(solution)/shard_map/cut/pallas_call | solution.py:155
  57.3 10.2 %all-to-all-start.2 = ((bf16[16,8,64,128]{3,2,1,0:T(8,128)(2,1)}), bf16[16,8,64,128]{3,2,1,0:T(8,128)(2,1)S(1)}, u32[]{:S(2)}, u32[]{:S(2)}) async-start(bf16[16,8,64,128]{3,2,1,0:T(8,128)(2,1)} %bitcast.34), calls=%async_computation.2 | async-start | bytes 4194304 | tf_op jit(solution)/shard_map/all_to_all | solution.py:402
  67.5 11.5 %image.1.refs_3_ = f32[64,64,128]{2,1,0:T(8,128)} custom-call(bf16[64,8,256]{2,1,0:T(8,128)(2,1)} %bitcast.39, f32[64,2,256]{2,1,0:T(2,128)} %bitcast.41), custom_call_target="tpu_custom_call" | custom-call | tf_op jit(solution)/shard_map/image/pallas_call | solution.py:276
  79.0 32.3 %all-to-all-done.2 = bf16[16,8,64,128]{3,2,1,0:T(8,128)(2,1)S(1)} async-done(((bf16[16,8,64,128]{3,2,1,0:T(8,128)(2,1)}), bf16[16,8,64,128]{3,2,1,0:T(8,128)(2,1)S(1)}, u32[]{:S(2)}, u32[]{:S(2)}) %all-to-all-start.2) | async-done | bytes 2097184 | tf_op jit(solution)/shard_map/all_to_all | solution.py:402
  111.4 0.0 copy-start.1
  111.4 0.0 all-gather.2.cloned.1.call-done
  111.4 1.3 copy-done.1
  112.7 16.3 %screen.1 = bf16[512,32,128]{2,1,0:T(8,128)(2,1)} custom-call(s32[64]{0:T(128)} %get-tuple-element.7.refs_0_, s32[64]{0:T(128)} %get-tuple-element.8.refs_1_, s32[64]{0:T(128)} %get-tuple-element.9.refs_2_, f32[64,64,128]{2,1,0:T(8,128)} %image.1.refs_3_, bf16[128,64,128]{2,1,0:T(8,128)(2,1)} %bitcast.35, bf16[512,32,128]{2,1,0:T(8,128)(2,1)} %bitcast.29, ...), custom_call_target="tpu_custom_call" | custom-call | tf_op jit(solution)/shard_map/screen/pallas_call | solution.py:391
  129.0 4.5 %all-to-all-start.3 = ((bf16[16,16,2,32,128]{4,3,2,1,0:T(8,128)(2,1)}), bf16[16,16,2,32,128]{4,3,2,1,0:T(8,128)(2,1)}, u32[]{:S(2)}, u32[]{:S(2)}) async-start(bf16[16,16,2,32,128]{4,3,2,1,0:T(8,128)(2,1)} %bitcast.31), calls=%async_computation.3 | async-start | bytes 8388608 | tf_op jit(solution)/shard_map/all_to_all | solution.py:402
  133.6 23.6 %patch.1 = bf16[128,64,128]{2,1,0:T(8,128)(2,1)} custom-call(s32[64]{0:T(128)} %get-tuple-element.7.refs_0_, s32[64]{0:T(128)} %get-tuple-element.8.refs_1_, s32[64]{0:T(128)} %get-tuple-element.9.refs_2_, f32[64,64,128]{2,1,0:T(8,128)} %image.1.refs_3_, bf16[512,32,128]{2,1,0:T(8,128)(2,1)} %bitcast.30, bf16[64,64]{1,0:T(8,128)(2,1)} %constant.15.clone.refs_5_, ...), custom_call_target="tpu_custom_call" | custom-call | tf_op jit(solution)/shard_map/patch/pallas_call | solution.py:317
  157.2 37.2 %all-to-all-done.3 = bf16[16,16,2,32,128]{4,3,2,1,0:T(8,128)(2,1)} async-done(((bf16[16,16,2,32,128]{4,3,2,1,0:T(8,128)(2,1)}), bf16[16,16,2,32,128]{4,3,2,1,0:T(8,128)(2,1)}, u32[]{:S(2)}, u32[]{:S(2)}) %all-to-all-start.3) | async-done | bytes 4194336 | tf_op jit(solution)/shard_map/all_to_all | solution.py:402
  194.4 4.7 %all-to-all-start.1 = ((bf16[16,8,64,128]{3,2,1,0:T(8,128)(2,1)}), bf16[16,8,64,128]{3,2,1,0:T(8,128)(2,1)S(1)}, u32[]{:S(2)}, u32[]{:S(2)}) async-start(bf16[16,8,64,128]{3,2,1,0:T(8,128)(2,1)} %bitcast.32), calls=%async_computation.1 | async-start | bytes 4194304 | tf_op jit(solution)/shard_map/all_to_all | solution.py:402
  199.1 3.9 %reduce_sum.21 = bf16[16,2,32,128]{3,2,1,0:T(8,128)(2,1)} reduce(bf16[16,16,2,32,128]{4,3,2,1,0:T(8,128)(2,1)} %all-to-all-done.3, bf16[]{:T(256)} %constant.12.clone.1), dimensions={0}, to_apply=%region_0.0 | reduce | flops 1966080 | bytes 4456450 | tf_op jit(solution)/shard_map/reduce_sum | solution.py:435
  203.0 21.8 %all-to-all-done.1 = bf16[16,8,64,128]{3,2,1,0:T(8,128)(2,1)S(1)} async-done(((bf16[16,8,64,128]{3,2,1,0:T(8,128)(2,1)}), bf16[16,8,64,128]{3,2,1,0:T(8,128)(2,1)S(1)}, u32[]{:S(2)}, u32[]{:S(2)}) %all-to-all-start.1) | async-done | bytes 2097184 | tf_op jit(solution)/shard_map/all_to_all | solution.py:402
  224.8 9.0 %all-to-all-start.4 = ((bf16[16,1,2,32,128]{4,3,2,1,0:T(8,128)(2,1)}), bf16[16,1,2,32,128]{4,3,2,1,0:T(8,128)(2,1)S(1)}, u32[]{:S(2)}, u32[]{:S(2)}) async-start(bf16[16,1,2,32,128]{4,3,2,1,0:T(8,128)(2,1)} %bitcast.18), calls=%async_computation.4 | async-start | bytes 524288 | tf_op jit(solution)/shard_map/all_to_all | solution.py:402
  233.8 0.0 copy-done
  233.8 7.3 %add.5 = f32[8,64,1024]{2,1,0:T(8,128)} custom-call(s32[128]{0:T(128)} %reshape.47.asked, bf16[128,64,128]{2,1,0:T(8,128)(2,1)} %bitcast.33), custom_call_target="tpu_custom_call" | custom-call | tf_op jit(solution)/shard_map/add/pallas_call | solution.py:214
  241.1 4.4 %all-to-all-done.4 = bf16[16,1,2,32,128]{4,3,2,1,0:T(8,128)(2,1)S(1)} async-done(((bf16[16,1,2,32,128]{4,3,2,1,0:T(8,128)(2,1)}), bf16[16,1,2,32,128]{4,3,2,1,0:T(8,128)(2,1)S(1)}, u32[]{:S(2)}, u32[]{:S(2)}) %all-to-all-start.4) | async-done | bytes 262176 | tf_op jit(solution)/shard_map/all_to_all | solution.py:402
  245.5 0.1 reshape.57
  245.7 0.7 reshape.58
  (4 shorter events, 0.1 us)
Async XLA Ops:
  7.2 104.2 %all-gather.2.cloned.1.call-start = ((), (), s32[]{:S(2)}) async-start(), calls=%async_computation.5 | async-start | bytes 4456448 | tf_op jit(solution)/shard_map/all_gather | solution.py:415
  57.3 54.0 %all-to-all-start.2 = ((bf16[16,8,64,128]{3,2,1,0:T(8,128)(2,1)}), bf16[16,8,64,128]{3,2,1,0:T(8,128)(2,1)S(1)}, u32[]{:S(2)}, u32[]{:S(2)}) async-start(bf16[16,8,64,128]{3,2,1,0:T(8,128)(2,1)} %bitcast.34), calls=%async_computation.2 | async-start | bytes 4194304 | tf_op jit(solution)/shard_map/all_to_all | solution.py:402
  111.4 1.3 copy-start.1
  129.0 65.4 %all-to-all-start.3 = ((bf16[16,16,2,32,128]{4,3,2,1,0:T(8,128)(2,1)}), bf16[16,16,2,32,128]{4,3,2,1,0:T(8,128)(2,1)}, u32[]{:S(2)}, u32[]{:S(2)}) async-start(bf16[16,16,2,32,128]{4,3,2,1,0:T(8,128)(2,1)} %bitcast.31), calls=%async_computation.3 | async-start | bytes 8388608 | tf_op jit(solution)/shard_map/all_to_all | solution.py:402
  194.4 30.3 %all-to-all-start.1 = ((bf16[16,8,64,128]{3,2,1,0:T(8,128)(2,1)}), bf16[16,8,64,128]{3,2,1,0:T(8,128)(2,1)S(1)}, u32[]{:S(2)}, u32[]{:S(2)}) async-start(bf16[16,8,64,128]{3,2,1,0:T(8,128)(2,1)} %bitcast.32), calls=%async_computation.1 | async-start | bytes 4194304 | tf_op jit(solution)/shard_map/all_to_all | solution.py:402
  224.8 9.0 %copy-start = (bf16[16,8,64,128]{3,2,1,0:T(8,128)(2,1)}, bf16[16,8,64,128]{3,2,1,0:T(8,128)(2,1)S(1)}, u32[]{:S(2)}) copy-start(bf16[16,8,64,128]{3,2,1,0:T(8,128)(2,1)S(1)} %all-to-all-done.1) | copy-start | bytes 6291460
  224.8 20.7 %all-to-all-start.4 = ((bf16[16,1,2,32,128]{4,3,2,1,0:T(8,128)(2,1)}), bf16[16,1,2,32,128]{4,3,2,1,0:T(8,128)(2,1)S(1)}, u32[]{:S(2)}, u32[]{:S(2)}) async-start(bf16[16,1,2,32,128]{4,3,2,1,0:T(8,128)(2,1)} %bitcast.18), calls=%async_computation.4 | async-start | bytes 524288 | tf_op jit(solution)/shard_map/all_to_all | solution.py:402
Sparse Core Ops, SparseCore 0:
  31.7 75.7 all-gather.1

commit v2 on v1

--- a/solution.py
+++ b/solution.py
@@ -8,9 +8,9 @@
 from jax.experimental.pallas import tpu as pltpu
 from jax.sharding import PartitionSpec as P
 
+
 PIX = 32
 TSLOTS = 2
-COMPS = 8
 LANES = 128
 CAP = 8
 F32 = jnp.float32
@@ -46,20 +46,46 @@
     return jnp.dot(a, b, preferred_element_type=F32)
 
 
-def route_kernel(owner, row_offset, column, station_a, station_b, slot_time, request, slot, first, second, fill):
+def swap_blocks(x):
+    rolled = [x] + [pltpu.roll(x, d * PIX, 1) for d in (1, 2, 3)]
+    line = lax.broadcasted_iota(jnp.int32, x.shape, 0)
+    block = lax.broadcasted_iota(jnp.int32, x.shape, 1) // PIX
+    rows = []
+    for a in range(4):
+        d = (block - a + 4) % 4
+        moved = rolled[0]
+        for k in (1, 2, 3):
+            moved = jnp.where(d == k, rolled[k], moved)
+        rows.append(jnp.sum(jnp.where(block == line, moved, 0.0), 0, keepdims=True))
+    return rows
+
+
+def mail_kernel(
+    n_bt, n_freq, me, owner, row_offset, column, stations, slot_time, screens,
+    mail, slot, first, second, first_sum, second_sum, fill, request, own,
+):
     count = owner.shape[0]
+    n_z = n_freq // 2
+    my_z, my_core = me[0] // 2, me[0] % 2
 
     def clear(i, carry):
         request[i] = -1
         return carry
 
-    lax.fori_loop(0, request.shape[0], clear, 0)
+    lax.fori_loop(0, n_bt * CAP, clear, 0)
 
     def zero(i, carry):
         fill[i] = 0
         return carry
 
-    lax.fori_loop(0, fill.shape[0], zero, 0)
+    lax.fori_loop(0, n_bt, zero, 0)
+
+    def rows(station, t):
+        bt, freq = station // n_freq, station % n_freq
+        z, core = freq // 2, freq % 2
+        half = jnp.where(core == my_core, 0, n_bt * n_z)
+        ahead = (z - my_z + n_z) % n_z
+        return (half + ahead * n_bt + bt) * TSLOTS + t, (half + bt * n_z + z) * TSLOTS + t
 
     def step(s, carry):
         o = owner[s]
@@ -67,33 +93,85 @@
         fill[o] = fill[o] + 1
         slot[s] = place
         request[place] = row_offset[s] * 1024 + column[s]
-        first[s] = station_a[s] * TSLOTS + slot_time[s]
-        second[s] = station_b[s] * TSLOTS + slot_time[s]
+        first[s], first_sum[s] = rows(stations[s * 2], slot_time[s])
+        second[s], second_sum[s] = rows(stations[s * 2 + 1], slot_time[s])
         return carry
 
     lax.fori_loop(0, count, step, 0)
-
-
-def route(owners, row_offset, column, station_a, station_b, slot_time, n_owners):
+    for t in range(TSLOTS):
+        table = screens[t].astype(F32)
+        for high in range(PIX // 4):
+            for a, line in enumerate(swap_blocks(table[:, high * LANES : (high + 1) * LANES])):
+                x = t * PIX + high * 4 + a
+                own[x : x + 1] = line
+    every = own[...].astype(BF16)
+    lane = lax.broadcasted_iota(jnp.int32, (16, LANES), 1)
+
+    def address(j, carry):
+        line = jnp.full((16, LANES), -1, jnp.int32)
+        for k in range(CAP):
+            code = request[j * CAP + k]
+            for part, value in enumerate((code >> 10, (code >> 5) & 31, code & 31)):
+                line = jnp.where(lane == part * CAP + k, value, line)
+        mail[j] = jnp.concatenate([every, line.astype(F32).astype(BF16)], 0)
+        return carry
+
+    lax.fori_loop(0, n_bt, address, 0)
+
+
+def make_mail(me, owners, row_offset, column, stations, slot_time, screens, n_bt, n_freq):
     count = owners.shape[0]
-    smem = pl.BlockSpec(memory_space=pltpu.SMEM)
-    ints = lambda n: jax.ShapeDtypeStruct((n,), jnp.int32)
-    return pl.pallas_call(
-        route_kernel,
-        out_shape=(ints(n_owners * CAP), ints(count), ints(count), ints(count)),
-        in_specs=[smem] * 6,
-        out_specs=(smem,) * 4,
-        scratch_shapes=[pltpu.SMEM((n_owners,), jnp.int32)],
-        name="route",
-    )(owners, row_offset, column, station_a, station_b, slot_time)
+    smem, vmem = pl.BlockSpec(memory_space=pltpu.SMEM), pl.BlockSpec(memory_space=pltpu.VMEM)
+    ints = jax.ShapeDtypeStruct((count,), jnp.int32)
+    rows = TSLOTS * PIX
+    return pl.pallas_call(
+        lambda *refs: mail_kernel(n_bt, n_freq, *refs),
+        out_shape=(jax.ShapeDtypeStruct((n_bt, rows + 16, LANES), BF16),) + (ints,) * 5,
+        in_specs=[smem] * 6 + [vmem],
+        out_specs=(vmem,) + (smem,) * 5,
+        scratch_shapes=[
+            pltpu.SMEM((n_bt,), jnp.int32),
+            pltpu.SMEM((n_bt * CAP,), jnp.int32),
+            pltpu.VMEM((rows, LANES), F32),
+        ],
+        name="mail",
+    )(me, owners, row_offset, column, stations, slot_time, screens)
+
+
+def finish_kernel(parts, out):
+    total = jnp.sum(parts[...].astype(F32), 0)
+    line = lax.broadcasted_iota(jnp.int32, (4, LANES), 0)
+    for t in range(TSLOTS):
+        for high in range(PIX // 4):
+            rows = swap_blocks(total[t, high * 4 : high * 4 + 4])
+            tile = jnp.broadcast_to(rows[0], (4, LANES))
+            for a in (1, 2, 3):
+                tile = jnp.where(line == a, jnp.broadcast_to(rows[a], (4, LANES)), tile)
+            out[t, :, high * LANES : (high + 1) * LANES] = tile
+
+
+def finish(parts):
+    vmem = pl.BlockSpec(memory_space=pltpu.VMEM)
+    return pl.pallas_call(
+        finish_kernel,
+        out_shape=jax.ShapeDtypeStruct((TSLOTS, 4, PIX * PIX), F32),
+        in_specs=[vmem],
+        out_specs=vmem,
+        name="finish",
+    )(parts)
 
 
 def listed(asked, order):
     def step(i, n):
         order[n] = i
-        return n + (asked[i] >= 0).astype(jnp.int32)
-
-    return lax.fori_loop(0, asked.shape[0], step, jnp.int32(0))
+        return n + (asked[i // CAP, i % CAP] >= 0).astype(jnp.int32)
+
+    return lax.fori_loop(0, asked.shape[0] * CAP, step, jnp.int32(0))
+
+
+def corner(asked, i):
+    j, k = i // CAP, i % CAP
+    return asked[j, k], asked[j, CAP + k] * PIX + asked[j, 2 * CAP + k]
 
 
 def for_listed(n, group, body):
@@ -124,8 +202,7 @@
     def body(places):
         for place in places:
             i = order[place]
-            code = asked[i]
-            r, c0 = code // 1024, code % 1024
+            r, c0 = corner(asked, i)
             j, shift = c0 // LANES, c0 % LANES
             after = jnp.minimum(j + 1, panels - 1)
 
@@ -151,7 +228,7 @@
 
 def cut_windows(asked, tile):
     comps, rows, columns = tile.shape
-    slots = asked.shape[0]
+    slots = asked.shape[0] * CAP
     return pl.pallas_call(
         cut_kernel,
         out_shape=jax.ShapeDtypeStruct((slots, 2 * PIX, LANES), BF16),
@@ -180,8 +257,7 @@
         spread = []
         for place in places:
             i = order[place]
-            code = asked[i]
-            r, c0 = code // 1024, code % 1024
+            r, c0 = corner(asked, i)
             j, shift = c0 // LANES, c0 % LANES
             piece = pieces[i].astype(F32)
             lines = []
@@ -210,7 +286,7 @@
 
 
 def add_windows(asked, pieces, comps, rows, columns):
-    slots = asked.shape[0]
+    slots = asked.shape[0] * CAP
     return pl.pallas_call(
         add_kernel,
         out_shape=jax.ShapeDtypeStruct((comps, rows, columns), F32),
@@ -282,12 +358,29 @@
     )(vis, uv)
 
 
+def join_halves(near, far, table, sems):
+    half = near.shape[0]
+    copies = [
+        pltpu.make_async_copy(ref, table.at[pl.ds(i * half, half)], sems.at[i])
+        for i, ref in enumerate((near, far))
+    ]
+    for copy in copies:
+        copy.start()
+    return copies
+
+
 def screens_of(table, row, spread):
     wide = dot(table[row], spread[...])
     return wide[:, :LANES], wide[:, LANES:]
 
 
-def patch_kernel(group, slot, first, second, image, table, backward, right, spread_a, spread_b, out):
+def patch_kernel(
+    group, slot, first, second, image, near, far, backward, right, spread_a, spread_b,
+    out, table, sems,
+):
+    for copy in join_halves(near, far, table, sems):
+        copy.wait()
+
     def step(g, carry):
         for k in range(group):
             s = g * group + k
@@ -310,27 +403,39 @@
     lax.fori_loop(0, image.shape[0] // group, step, 0)
 
 
-def patch_gradients(slot, first, second, image, table, consts, slots):
-    forward, backward, right, spread_a, spread_b = consts
+def table_scratch(near):
+    whole = (2 * near.shape[0],) + near.shape[1:]
+    return [pltpu.VMEM(whole, BF16), pltpu.SemaphoreType.DMA((2,))]
+
+
+def patch_gradients(slot, first, second, image, near, far, consts, slots):
+    _, backward, right, spread_a, spread_b = consts
     group = math.gcd(image.shape[0], 4)
     vmem, smem = pl.BlockSpec(memory_space=pltpu.VMEM), pl.BlockSpec(memory_space=pltpu.SMEM)
     return pl.pallas_call(
         lambda *refs: patch_kernel(group, *refs),
         out_shape=jax.ShapeDtypeStruct((slots, 2 * PIX, LANES), BF16),
-        in_specs=[smem] * 3 + [vmem] * 6,
+        in_specs=[smem] * 3 + [vmem] + [pl.BlockSpec(memory_space=pl.ANY)] * 2 + [vmem] * 4,
         out_specs=vmem,
+        scratch_shapes=table_scratch(near),
         name="patch",
-    )(slot, first, second, image, table, backward, right, spread_a, spread_b)
-
-
-def screen_kernel(group, slot, first, second, image, patches, table, forward, right, spread_a, spread_b, out, acc):
+    )(slot, first, second, image, near, far, backward, right, spread_a, spread_b)
+
+
+def screen_kernel(
+    group, slot, first, second, first_sum, second_sum, image, patches, near, far,
+    forward, right, spread_a, spread_b, out_near, out_far, table, sems, acc,
+):
     chunk = 32
+    copies = join_halves(near, far, table, sems)
 
     def clear(i, carry):
         acc[pl.ds(i * chunk, chunk)] = jnp.zeros((chunk, PIX, LANES), F32)
         return carry
 
     lax.fori_loop(0, acc.shape[0] // chunk, clear, 0)
+    for copy in copies:
+        copy.wait()
     block = lax.broadcasted_iota(jnp.int32, (PIX, LANES), 1) // PIX
 
     def step(g, carry):
@@ -370,73 +475,99 @@
             )
             terms.append((s, ta, tb))
         for s, ta, tb in terms:
-            acc[first[s]] = acc[first[s]] + ta
-            acc[second[s]] = acc[second[s]] + tb
+            acc[first_sum[s]] = acc[first_sum[s]] + ta
+            acc[second_sum[s]] = acc[second_sum[s]] + tb
         return carry
 
     lax.fori_loop(0, image.shape[0] // group, step, 0)
 
-    def give(i, carry):
-        at = pl.ds(i * chunk, chunk)
-        out[at] = acc[at].astype(BF16)
-        return carry
-
-    lax.fori_loop(0, acc.shape[0] // chunk, give, 0)
-
-
-def screen_gradients(slot, first, second, image, patches, table, consts):
-    forward, backward, right, spread_a, spread_b = consts
+    for start, out in ((0, out_near), (out_near.shape[0], out_far)):
+
+        def give(i, carry, start=start, out=out):
+            out[pl.ds(i * chunk, chunk)] = acc[pl.ds(start + i * chunk, chunk)].astype(BF16)
+            return carry
+
+        lax.fori_loop(0, out.shape[0] // chunk, give, 0)
+
+
+def screen_gradients(slot, rows, image, patches, near, far, consts):
+    forward, _, right, spread_a, spread_b = consts
     group = math.gcd(image.shape[0], 4)
     vmem, smem = pl.BlockSpec(memory_space=pltpu.VMEM), pl.BlockSpec(memory_space=pltpu.SMEM)
+    scratch = table_scratch(near)
     return pl.pallas_call(
         lambda *refs: screen_kernel(group, *refs),
-        out_shape=jax.ShapeDtypeStruct(table.shape, BF16),
-        in_specs=[smem] * 3 + [vmem] * 7,
-        out_specs=vmem,
-        scratch_shapes=[pltpu.VMEM(table.shape, F32)],
+        out_shape=(jax.ShapeDtypeStruct(near.shape, BF16),) * 2,
+        in_specs=[smem] * 5 + [vmem] * 2 + [pl.BlockSpec(memory_space=pl.ANY)] * 2 + [vmem] * 4,
+        out_specs=(vmem,) * 2,
+        scratch_shapes=scratch + [pltpu.VMEM(scratch[0].shape, F32)],
         name="screen",
-    )(slot, first, second, image, patches, table, forward, right, spread_a, spread_b)
-
-
-def exchange(x, axis):
-    return lax.all_to_all(x, axis, split_axis=0, concat_axis=0, tiled=True)
+    )(slot, *rows, image, patches, near, far, forward, right, spread_a, spread_b)
+
+
+def exchange(x, axis, groups=None):
+    return lax.all_to_all(
+        x, axis, split_axis=0, concat_axis=0, tiled=True, axis_index_groups=groups
+    )
+
+
+def ring_gather(x, n_z):
+    def by(step):
+        return [(2 * z + c, 2 * ((z + step) % n_z) + c) for z in range(n_z) for c in range(2)]
+
+    blocks = [None] * n_z
+    blocks[0] = up = down = x
+    for k in range(1, n_z // 2 + 1):
+        up = lax.ppermute(up, "freq", by(1))
+        blocks[n_z - k] = up
+        if k < n_z - k:
+            down = lax.ppermute(down, "freq", by(-1))
+            blocks[k] = down
+    return jnp.stack(blocks)
 
 
 def per_device(
     uv_grid, screens, residual, uv_coords, owner_tile, row_offset, column, stations, time_slot
 ):
     n_bt, n_freq = lax.axis_size("bt"), lax.axis_size("freq")
+    n_z = n_freq // 2
     slots = n_bt * CAP
     consts = constant_tables()
-    held = screens.shape[1]
-    own = screens.reshape(TSLOTS, held, 4, PIX, PIX).transpose(1, 0, 3, 2, 4)
-    own = own.reshape(held, TSLOTS, PIX, LANES)
-    table = lax.all_gather(own, "freq", axis=0, tiled=True)
-    table = lax.all_gather(table, "bt", axis=0, tiled=True)
-    table = table.reshape(-1, PIX, LANES)
-    request, slot, first, second = route(
+    swap = [(f, f ^ 1) for f in range(n_freq)]
+    same_core = [[2 * z + c for z in range(n_z)] for c in range(2)]
+    row = TSLOTS * PIX
+    mail, slot, first, second, first_sum, second_sum = make_mail(
+        lax.axis_index("freq").astype(jnp.int32).reshape(1),
         owner_tile[0, :, 0],
         row_offset[0],
         column[0],
-        stations[0, :, 0],
-        stations[0, :, 1],
+        stations[0].reshape(-1),
         time_slot[0],
+        screens[:, 0],
         n_bt,
+        n_freq,
     )
-    asked = exchange(request.reshape(n_bt, CAP), "bt").reshape(slots)
     image = adjoint_images(residual[0], uv_coords[0])
+    mail, image = lax.optimization_barrier((exchange(mail, "bt"), image))
+    asked = mail[:, row].astype(jnp.int32)
     cut = cut_windows(asked, uv_grid[0])
-    fetched = exchange(cut.reshape(n_bt, CAP, 2 * PIX, LANES), "bt").reshape(slots, 2 * PIX, LANES)
-    grads = patch_gradients(slot, first, second, image, table, consts, slots)
+    cut, screens_here = lax.optimization_barrier((cut, mail[:, :row]))
+    fetched = exchange(cut.reshape(n_bt, CAP, 2 * PIX, LANES), "bt")
+    fetched = fetched.reshape(slots, 2 * PIX, LANES)
+    near = ring_gather(screens_here, n_z).reshape(n_z * n_bt * TSLOTS, PIX, LANES)
+    far = lax.ppermute(near, "freq", swap)
+    terms, sent = screen_gradients(
+        slot, (first, second, first_sum, second_sum), image, fetched, near, far, consts
+    )
+    grads = patch_gradients(slot, first, second, image, near, far, consts, slots)
     returned = exchange(grads.reshape(n_bt, CAP, 2 * PIX, LANES), "bt").reshape(slots, 2 * PIX, LANES)
-    terms = screen_gradients(slot, first, second, image, fetched, table, consts)
     grid_grad = add_windows(asked, returned, *uv_grid.shape[1:])
-    part = exchange(terms.reshape(n_bt, -1, TSLOTS, PIX, LANES), "bt")
+    came = lax.ppermute(sent, "freq", swap)
+    part = (terms.astype(F32) + came.astype(F32)).astype(BF16)
+    part = exchange(part.reshape(n_bt, n_z, TSLOTS, PIX, LANES), "bt")
     part = jnp.sum(part.astype(F32), 0).astype(BF16)
-    part = exchange(part.reshape(n_freq, held, TSLOTS, PIX, LANES), "freq")
-    part = jnp.sum(part.astype(F32), 0).reshape(held, TSLOTS, PIX, 4, PIX)
-    screen_grad = part.transpose(1, 0, 3, 2, 4).reshape(TSLOTS, held, 4, PIX * PIX)
-    return grid_grad[None], screen_grad
+    screen_grad = finish(exchange(part, "freq", same_core))
+    return grid_grad[None], screen_grad[:, None]
 
 
 def solution(mesh):
@@ -452,6 +583,7 @@
         P("freq", "bt"),
     )
     out_specs = (P("freq", None, "bt", None), P(None, ("bt", "freq"), None, None))
+
     return jax.shard_map(
         per_device, mesh=mesh, in_specs=in_specs, out_specs=out_specs, check_vma=False
     )

time: 254 us -> 236 us (0.929)
  the two profiles are of different devices: /device:TPU:1 before, /device:TPU:54 now
where the time goes in v2:
time: 236 us; the launch traced here: 235 us
  Pallas kernels  93.7 us (40%)
  waiting for transfers between devices  59.6 us (25%)
  starting transfers between devices  40.1 us (17%)
  blocking collectives  31.9 us (14%)
  other arithmetic  5.14 us (2%)
  local copies, waits for them, and re-layouts  3.76 us (2%)
    all_to_all x4, waiting for transfers between devices, exchange(): lax.all_to_all(x, axis, split_axis=0, concat_axis=0, tiled=True, axis_ind...  32.5 us
    all_to_all x1, blocking collectives, exchange(): lax.all_to_all(x, axis, split_axis=0, concat_axis=0, tiled=True, axis_ind...  31.9 us
    all_to_all x4, starting transfers between devices, exchange(): lax.all_to_all(x, axis, split_axis=0, concat_axis=0, tiled=True, axis_ind...  31.1 us
    pallas_call x1, Pallas kernels, patch_gradients(): pl.pallas_call(lambda *refs: patch_kernel(group, *refs), out_shape=jax.Sh...  24.6 us
    ppermute x4, waiting for transfers between devices, ring_gather(): up = lax.ppermute(up, 'freq', by(1))  21.9 us
    pallas_call x1, Pallas kernels, add_windows(): pl.pallas_call(add_kernel, out_shape=jax.ShapeDtypeStruct((comps, rows, c...  18.6 us
    pallas_call x1, Pallas kernels, screen_gradients(): pl.pallas_call(lambda *refs: screen_kernel(group, *refs), out_shape=(jax....  16.8 us
    pallas_call x1, Pallas kernels, cut_windows(): pl.pallas_call(cut_kernel, out_shape=jax.ShapeDtypeStruct((slots, 2 * PIX...  14.7 us
  transfers between devices with their start and end apart: 13, of which 9 were waited for; matrix products, arithmetic and copies ran while one was open for 1% of the time, Pallas kernels for 23%

profile of v2, /device:TPU:54, one launch (start us, length us, event | category | flops | bytes accessed | tf_op | source)
XLA Modules:
  0.0 235.0 jit_solution(13728621452737180284)
XLA Ops:
  0.6 0.8 copy.24
  1.4 0.7 reshape_squeeze.3.refs_4_
  2.1 5.8 %mail.1 = (bf16[16,80,128]{2,1,0:T(8,128)(2,1)}, s32[64]{0:T(128)}, s32[64]{0:T(128)}, s32[64]{0:T(128)}, s32[64]{0:T(128)}, /*index=5*/s32[64]{0:T(128)}) custom-call(s32[1]{0:T(128)} %bitcast.refs_0_, s32[64]{0:T(128)} %bitcast.52, s32[64]{0:T(128)} %bitcast.53, s32[64]{0:T(128)} %bitcast.54, s32[128]{0:T(128)} %reshape_squeeze.3.refs_4_, s32[64]{0:T(128)} %bitcast.55, ...), custom_call_target="tpu_custom_call" | custom-call | tf_op jit(solution)/shard_map/mail/pallas_call | solution.py:127
  7.9 7.2 %all-to-all-start = ((bf16[16,80,128]{2,1,0:T(8,128)(2,1)}), bf16[16,80,128]{2,1,0:T(8,128)(2,1)S(1)}, u32[]{:S(2)}, u32[]{:S(2)}) async-start(bf16[16,80,128]{2,1,0:T(8,128)(2,1)} %get-tuple-element.14), calls=%async_computation | async-start | bytes 655360 | tf_op jit(solution)/shard_map/all_to_all | solution.py:509
  15.1 11.5 %image.1.refs_3_.refs_5_ = f32[64,64,128]{2,1,0:T(8,128)} custom-call(bf16[64,8,256]{2,1,0:T(8,128)(2,1)} %bitcast.48, f32[64,2,256]{2,1,0:T(2,128)} %bitcast.49), custom_call_target="tpu_custom_call" | custom-call | tf_op jit(solution)/shard_map/image/pallas_call | solution.py:352
  26.7 0.6 fusion.asked
  27.3 14.7 %cut.1 = bf16[128,64,128]{2,1,0:T(8,128)(2,1)} custom-call(s32[16,128]{1,0:T(8,128)} %fusion.asked, bf16[8,64,1024]{2,1,0:T(8,128)(2,1)} %bitcast.47), custom_call_target="tpu_custom_call" | custom-call | tf_op jit(solution)/shard_map/cut/pallas_call | solution.py:232
  42.0 1.9 collective-permute-start.3
  44.0 5.5 %collective-permute-done.3 = bf16[16,64,128]{2,1,0:T(8,128)(2,1)S(1)} collective-permute-done((bf16[16,64,128]{2,1,0:T(8,128)(2,1)S(1)}, bf16[16,64,128]{2,1,0:T(8,128)(2,1)S(1)}, u32[]{:S(2)}, u32[]{:S(2)}) %collective-permute-start.3) | collective-permute-done | bytes 262176 | tf_op jit(solution)/shard_map/ppermute | solution.py:521
  49.5 1.9 collective-permute-start.4
  51.4 2.3 collective-permute-start.1
  53.7 5.2 %collective-permute-done.4 = bf16[16,64,128]{2,1,0:T(8,128)(2,1)S(1)} collective-permute-done((bf16[16,64,128]{2,1,0:T(8,128)(2,1)S(1)}, bf16[16,64,128]{2,1,0:T(8,128)(2,1)S(1)}, u32[]{:S(2)}, u32[]{:S(2)}) %collective-permute-start.4) | collective-permute-done | bytes 262176 | tf_op jit(solution)/shard_map/ppermute | solution.py:521
  58.9 0.5 collective-permute-done.1
  59.3 2.6 %collective-permute-start.2 = (bf16[16,64,128]{2,1,0:T(8,128)(2,1)S(1)}, bf16[16,64,128]{2,1,0:T(8,128)(2,1)S(1)}, u32[]{:S(2)}, u32[]{:S(2)}) collective-permute-start(bf16[16,64,128]{2,1,0:T(8,128)(2,1)S(1)} %collective-permute-done.1), channel_id=1, source_target_pairs={{0,14},{1,15},{2,0},{3,1},{4,2},{5,3},{6,4},{7,5},{8,6},{9,7},{10,... | collective-permute-start | bytes 786440 | tf_op jit(solution)/shard_map/ppermute | solution.py:524
  62.0 4.2 %collective-permute-done.5 = bf16[16,64,128]{2,1,0:T(8,128)(2,1)S(1)} collective-permute-done((bf16[16,64,128]{2,1,0:T(8,128)(2,1)S(1)}, bf16[16,64,128]{2,1,0:T(8,128)(2,1)S(1)}, u32[]{:S(2)}, u32[]{:S(2)}) %collective-permute-start.5) | collective-permute-done | bytes 262176 | tf_op jit(solution)/shard_map/ppermute | solution.py:521
  66.2 0.4 collective-permute-done.2
  66.7 7.1 %collective-permute-done.6 = bf16[16,64,128]{2,1,0:T(8,128)(2,1)S(1)} collective-permute-done((bf16[16,64,128]{2,1,0:T(8,128)(2,1)S(1)}, bf16[16,64,128]{2,1,0:T(8,128)(2,1)S(1)}, u32[]{:S(2)}, u32[]{:S(2)}) %collective-permute-start.6) | collective-permute-done | bytes 262176 | tf_op jit(solution)/shard_map/ppermute | solution.py:521
  74.0 31.9 %all_to_all.25 = bf16[16,8,64,128]{3,2,1,0:T(8,128)(2,1)} all-to-all(bf16[16,8,64,128]{3,2,1,0:T(8,128)(2,1)S(1)} %bitcast.45), channel_id=1, replica_groups=mesh['bt'=16,'freq'=16] {'bt'}, dimensions={0} | all-to-all | bytes 4194304 | tf_op jit(solution)/shard_map/all_to_all | solution.py:509
  106.0 1.3 copy-done.1
  107.3 16.8 %screen.1 = (bf16[256,32,128]{2,1,0:T(8,128)(2,1)}, bf16[256,32,128]{2,1,0:T(8,128)(2,1)}) custom-call(s32[64]{0:T(128)} %get-tuple-element.16.refs_0_, s32[64]{0:T(128)} %get-tuple-element.17.refs_1_, s32[64]{0:T(128)} %get-tuple-element.18.refs_2_, s32[64]{0:T(128)} %get-tuple-element.21.refs_3_, s32[64]{0:T(128)} %get-tuple-element.22.refs_4_, ...), custom_call_target="tpu_custom_call" | custom-call | tf_op jit(solution)/shard_map/screen/pallas_call | solution.py:498
  124.2 4.4 %collective-permute-done.8 = bf16[256,32,128]{2,1,0:T(8,128)(2,1)S(1)} collective-permute-done((bf16[256,32,128]{2,1,0:T(8,128)(2,1)}, bf16[256,32,128]{2,1,0:T(8,128)(2,1)S(1)}, u32[]{:S(2)}, u32[]{:S(2)}) %collective-permute-start.8) | collective-permute-done | bytes 2097184 | tf_op jit(solution)/shard_map/ppermute | solution.py:565
  128.5 3.5 %add_convert_fusion = bf16[256,32,128]{2,1,0:T(8,128)(2,1)} fusion(bf16[256,32,128]{2,1,0:T(8,128)(2,1)S(1)} %collective-permute-done.8, bf16[256,32,128]{2,1,0:T(8,128)(2,1)} %get-tuple-element.24), kind=kLoop, calls=%fused_computation | loop fusion | flops 4194304 | bytes 6291456 | tf_op jit(solution)/shard_map/convert_element_type | solution.py:566
  132.0 7.8 %all-to-all-start.3 = ((bf16[16,8,2,32,128]{4,3,2,1,0:T(8,128)(2,1)}), bf16[16,8,2,32,128]{4,3,2,1,0:T(8,128)(2,1)S(1)}, u32[]{:S(2)}, u32[]{:S(2)}) async-start(bf16[16,8,2,32,128]{4,3,2,1,0:T(8,128)(2,1)} %bitcast.25), calls=%async_computation.3 | async-start | bytes 4194304 | tf_op jit(solution)/shard_map/all_to_all | solution.py:509
  139.8 24.6 %patch.1 = bf16[128,64,128]{2,1,0:T(8,128)(2,1)} custom-call(s32[64]{0:T(128)} %get-tuple-element.16.refs_0_, s32[64]{0:T(128)} %get-tuple-element.17.refs_1_, s32[64]{0:T(128)} %get-tuple-element.18.refs_2_, f32[64,64,128]{2,1,0:T(8,128)} %image.1.refs_3_.refs_5_, bf16[256,32,128]{2,1,0:T(8,128)(2,1)} %bitcast.42, bf16[256,32,128]{2,1,0:T(8,128)(2,1)} %copy-done.1, ...), custom_call_target="tpu_custom_call" | custom-call | tf_op jit(solution)/shard_map/patch/pallas_call | solution.py:415
  164.4 6.0 %all-to-all-done.3 = bf16[16,8,2,32,128]{4,3,2,1,0:T(8,128)(2,1)S(1)} async-done(((bf16[16,8,2,32,128]{4,3,2,1,0:T(8,128)(2,1)}), bf16[16,8,2,32,128]{4,3,2,1,0:T(8,128)(2,1)S(1)}, u32[]{:S(2)}, u32[]{:S(2)}) %all-to-all-start.3) | async-done | bytes 2097184 | tf_op jit(solution)/shard_map/all_to_all | solution.py:509
  170.4 7.6 %all-to-all-start.1 = ((bf16[16,8,64,128]{3,2,1,0:T(8,128)(2,1)}), bf16[16,8,64,128]{3,2,1,0:T(8,128)(2,1)}, u32[]{:S(2)}, u32[]{:S(2)}) async-start(bf16[16,8,64,128]{3,2,1,0:T(8,128)(2,1)} %bitcast.43), calls=%async_computation.1 | async-start | bytes 4194304 | tf_op jit(solution)/shard_map/all_to_all | solution.py:509
  178.0 1.1 reduce_sum.12
  179.0 26.5 %all-to-all-done.1 = bf16[16,8,64,128]{3,2,1,0:T(8,128)(2,1)} async-done(((bf16[16,8,64,128]{3,2,1,0:T(8,128)(2,1)}), bf16[16,8,64,128]{3,2,1,0:T(8,128)(2,1)}, u32[]{:S(2)}, u32[]{:S(2)}) %all-to-all-start.1) | async-done | bytes 2097184 | tf_op jit(solution)/shard_map/all_to_all | solution.py:509
  205.5 8.5 %all-to-all-start.4 = ((bf16[8,2,32,128]{3,2,1,0:T(8,128)(2,1)}), bf16[8,2,32,128]{3,2,1,0:T(8,128)(2,1)S(1)}, u32[]{:S(2)}, u32[]{:S(2)}) async-start(bf16[8,2,32,128]{3,2,1,0:T(8,128)(2,1)} %reduce_sum.12), calls=%async_computation.4 | async-start | bytes 262144 | tf_op jit(solution)/shard_map/all_to_all | solution.py:509
  214.1 18.6 %add.6 = f32[8,64,1024]{2,1,0:T(8,128)} custom-call(s32[16,128]{1,0:T(8,128)} %fusion.asked, bf16[128,64,128]{2,1,0:T(8,128)(2,1)} %bitcast.21.pieces), custom_call_target="tpu_custom_call" | custom-call | tf_op jit(solution)/shard_map/add/pallas_call | solution.py:290
  232.7 0.6 copy-done.3
  233.3 1.7 finish.1
  (25 shorter events, 0.7 us)
Async XLA Ops:
  7.9 18.7 %all-to-all-start = ((bf16[16,80,128]{2,1,0:T(8,128)(2,1)}), bf16[16,80,128]{2,1,0:T(8,128)(2,1)S(1)}, u32[]{:S(2)}, u32[]{:S(2)}) async-start(bf16[16,80,128]{2,1,0:T(8,128)(2,1)} %get-tuple-element.14), calls=%async_computation | async-start | bytes 655360 | tf_op jit(solution)/shard_map/all_to_all | solution.py:509
  42.0 32.0 %copy-start.2 = (bf16[128,64,128]{2,1,0:T(8,128)(2,1)S(1)}, bf16[128,64,128]{2,1,0:T(8,128)(2,1)}, u32[]{:S(2)}) copy-start(bf16[128,64,128]{2,1,0:T(8,128)(2,1)} %cut.1) | copy-start | bytes 6291460
  42.0 7.5 %collective-permute-start.3 = (bf16[16,64,128]{2,1,0:T(8,128)(2,1)S(1)}, bf16[16,64,128]{2,1,0:T(8,128)(2,1)S(1)}, u32[]{:S(2)}, u32[]{:S(2)}) collective-permute-start(bf16[16,64,128]{2,1,0:T(8,128)(2,1)S(1)} %slice.7), channel_id=1, source_target_pairs={{0,2},{1,3},{2,4},{3,5},{4,6},{5,7},{6,8},{7,9},{8,10},{9,11},{10,... | collective-permute-start | bytes 786440 | tf_op jit(solution)/shard_map/ppermute | solution.py:521
  43.9 7.5 %collective-permute-start = (bf16[16,64,128]{2,1,0:T(8,128)(2,1)S(1)}, bf16[16,64,128]{2,1,0:T(8,128)(2,1)S(1)}, u32[]{:S(2)}, u32[]{:S(2)}) collective-permute-start(bf16[16,64,128]{2,1,0:T(8,128)(2,1)S(1)} %slice.7), channel_id=1, source_target_pairs={{0,14},{1,15},{2,0},{3,1},{4,2},{5,3},{6,4},{7,5},{8,6},{9,7},{10,... | collective-permute-start | bytes 786440 | tf_op jit(solution)/shard_map/ppermute | solution.py:524
  49.5 9.4 %collective-permute-start.4 = (bf16[16,64,128]{2,1,0:T(8,128)(2,1)S(1)}, bf16[16,64,128]{2,1,0:T(8,128)(2,1)S(1)}, u32[]{:S(2)}, u32[]{:S(2)}) collective-permute-start(bf16[16,64,128]{2,1,0:T(8,128)(2,1)S(1)} %collective-permute-done.3), channel_id=1, source_target_pairs={{0,2},{1,3},{2,4},{3,5},{4,6},{5,7},{6,8},{7,9},{8,10},{9,11},{10,... | collective-permute-start | bytes 786440 | tf_op jit(solution)/shard_map/ppermute | solution.py:521
  51.4 7.9 %collective-permute-start.1 = (bf16[16,64,128]{2,1,0:T(8,128)(2,1)S(1)}, bf16[16,64,128]{2,1,0:T(8,128)(2,1)S(1)}, u32[]{:S(2)}, u32[]{:S(2)}) collective-permute-start(bf16[16,64,128]{2,1,0:T(8,128)(2,1)S(1)} %collective-permute-done), channel_id=1, source_target_pairs={{0,14},{1,15},{2,0},{3,1},{4,2},{5,3},{6,4},{7,5},{8,6},{9,7},{10,... | collective-permute-start | bytes 786440 | tf_op jit(solution)/shard_map/ppermute | solution.py:524
  58.9 7.3 %collective-permute-start.5 = (bf16[16,64,128]{2,1,0:T(8,128)(2,1)S(1)}, bf16[16,64,128]{2,1,0:T(8,128)(2,1)S(1)}, u32[]{:S(2)}, u32[]{:S(2)}) collective-permute-start(bf16[16,64,128]{2,1,0:T(8,128)(2,1)S(1)} %collective-permute-done.4), channel_id=1, source_target_pairs={{0,2},{1,3},{2,4},{3,5},{4,6},{5,7},{6,8},{7,9},{8,10},{9,11},{10,... | collective-permute-start | bytes 786440 | tf_op jit(solution)/shard_map/ppermute | solution.py:521
  59.3 7.3 %collective-permute-start.2 = (bf16[16,64,128]{2,1,0:T(8,128)(2,1)S(1)}, bf16[16,64,128]{2,1,0:T(8,128)(2,1)S(1)}, u32[]{:S(2)}, u32[]{:S(2)}) collective-permute-start(bf16[16,64,128]{2,1,0:T(8,128)(2,1)S(1)} %collective-permute-done.1), channel_id=1, source_target_pairs={{0,14},{1,15},{2,0},{3,1},{4,2},{5,3},{6,4},{7,5},{8,6},{9,7},{10,... | collective-permute-start | bytes 786440 | tf_op jit(solution)/shard_map/ppermute | solution.py:524
  66.2 7.6 %collective-permute-start.6 = (bf16[16,64,128]{2,1,0:T(8,128)(2,1)S(1)}, bf16[16,64,128]{2,1,0:T(8,128)(2,1)S(1)}, u32[]{:S(2)}, u32[]{:S(2)}) collective-permute-start(bf16[16,64,128]{2,1,0:T(8,128)(2,1)S(1)} %collective-permute-done.5), channel_id=1, source_target_pairs={{0,2},{1,3},{2,4},{3,5},{4,6},{5,7},{6,8},{7,9},{8,10},{9,11},{10,... | collective-permute-start | bytes 786440 | tf_op jit(solution)/shard_map/ppermute | solution.py:521
  73.9 32.0 %copy-start = (bf16[8,16,64,128]{3,2,1,0:T(8,128)(2,1)}, bf16[8,16,64,128]{3,2,1,0:T(8,128)(2,1)S(1)}, u32[]{:S(2)}) copy-start(bf16[8,16,64,128]{3,2,1,0:T(8,128)(2,1)S(1)} %bitcast_dynamic-update-slice_fusion) | copy-start | bytes 6291460
  73.9 32.0 %collective-permute-start.7 = (bf16[256,32,128]{2,1,0:T(8,128)(2,1)S(1)}, bf16[256,32,128]{2,1,0:T(8,128)(2,1)S(1)}, u32[]{:S(2)}, u32[]{:S(2)}) collective-permute-start(bf16[256,32,128]{2,1,0:T(8,128)(2,1)S(1)} %bitcast.40), channel_id=1, source_target_pairs={{0,1},{1,0},{2,3},{3,2},{4,5},{5,4},{6,7},{7,6},{8,9},{9,8},{10,11... | collective-permute-start | bytes 6291464 | tf_op jit(solution)/shard_map/ppermute | solution.py:558
  106.0 1.3 copy-start.1
  124.1 4.5 %collective-permute-start.8 = (bf16[256,32,128]{2,1,0:T(8,128)(2,1)}, bf16[256,32,128]{2,1,0:T(8,128)(2,1)S(1)}, u32[]{:S(2)}, u32[]{:S(2)}) collective-permute-start(bf16[256,32,128]{2,1,0:T(8,128)(2,1)} %get-tuple-element.25), channel_id=1, source_target_pairs={{0,1},{1,0},{2,3},{3,2},{4,5},{5,4},{6,7},{7,6},{8,9},{9,8},{10,11... | collective-permute-start | bytes 6291464 | tf_op jit(solution)/shard_map/ppermute | solution.py:565
  132.0 38.4 %all-to-all-start.3 = ((bf16[16,8,2,32,128]{4,3,2,1,0:T(8,128)(2,1)}), bf16[16,8,2,32,128]{4,3,2,1,0:T(8,128)(2,1)S(1)}, u32[]{:S(2)}, u32[]{:S(2)}) async-start(bf16[16,8,2,32,128]{4,3,2,1,0:T(8,128)(2,1)} %bitcast.25), calls=%async_computation.3 | async-start | bytes 4194304 | tf_op jit(solution)/shard_map/all_to_all | solution.py:509
  170.4 35.1 %all-to-all-start.1 = ((bf16[16,8,64,128]{3,2,1,0:T(8,128)(2,1)}), bf16[16,8,64,128]{3,2,1,0:T(8,128)(2,1)}, u32[]{:S(2)}, u32[]{:S(2)}) async-start(bf16[16,8,64,128]{3,2,1,0:T(8,128)(2,1)} %bitcast.43), calls=%async_computation.1 | async-start | bytes 4194304 | tf_op jit(solution)/shard_map/all_to_all | solution.py:509
  205.5 27.1 %all-to-all-start.4 = ((bf16[8,2,32,128]{3,2,1,0:T(8,128)(2,1)}), bf16[8,2,32,128]{3,2,1,0:T(8,128)(2,1)S(1)}, u32[]{:S(2)}, u32[]{:S(2)}) async-start(bf16[8,2,32,128]{3,2,1,0:T(8,128)(2,1)} %reduce_sum.12), calls=%async_computation.4 | async-start | bytes 262144 | tf_op jit(solution)/shard_map/all_to_all | solution.py:509
  232.7 0.6 copy-start.3

commit v3 on v2

--- a/solution.py
+++ b/solution.py
@@ -93,8 +93,8 @@
         fill[o] = fill[o] + 1
         slot[s] = place
         request[place] = row_offset[s] * 1024 + column[s]
-        first[s], first_sum[s] = rows(stations[s * 2], slot_time[s])
-        second[s], second_sum[s] = rows(stations[s * 2 + 1], slot_time[s])
+        first[s], first_sum[s] = rows(stations[0, s], slot_time[s])
+        second[s], second_sum[s] = rows(stations[1, s], slot_time[s])
         return carry
 
     lax.fori_loop(0, count, step, 0)
@@ -200,6 +200,7 @@
     block = lax.broadcasted_iota(jnp.int32, (PIX, LANES), 1) // PIX
 
     def body(places):
+        done = []
         for place in places:
             i = order[place]
             r, c0 = corner(asked, i)
@@ -221,7 +222,9 @@
                     start = (ri * 4 + m) * PIX
                     part = jnp.where(block == m, moved[start : start + PIX], part)
                 parts.append(part)
-            out[i] = jnp.concatenate(parts, 0).astype(BF16)
+            done.append((i, jnp.concatenate(parts, 0).astype(BF16)))
+        for i, piece in done:
+            out[i] = piece
 
     for_listed(n, 4, body)
 
@@ -265,20 +268,19 @@
                 for m in range(4):
                     lines.append(jnp.where(block == m, piece[ri * PIX : (ri + 1) * PIX], 0.0))
             lines = jnp.concatenate(lines, 0).astype(BF16)
-            moved = dot(lines, jnp.where(ahead == shift, 1.0, 0.0).astype(BF16))
-            spread.append((r, j, shift, lines, moved))
-        for r, j, shift, lines, moved in spread:
+            pick = jnp.concatenate([ahead == shift, ahead + LANES == shift], 1)
+            spread.append((r, j, shift, dot(lines, jnp.where(pick, 1.0, 0.0).astype(BF16))))
+        for r, j, shift, moved in spread:
             for c in range(comps):
                 at = pl.ds(c * rows + r, PIX)
-                wide[j, at, :] = wide[j, at, :] + moved[c * PIX : (c + 1) * PIX]
-        for r, j, shift, lines, moved in spread:
+                wide[j, at, :] = wide[j, at, :] + moved[c * PIX : (c + 1) * PIX, :LANES]
+        for r, j, shift, moved in spread:
 
             @pl.when(shift > LANES - PIX)
-            def _(r=r, j=j, shift=shift, lines=lines):
-                over = dot(lines, jnp.where(ahead + LANES == shift, 1.0, 0.0).astype(BF16))
+            def _(r=r, j=j, moved=moved):
                 for c in range(comps):
                     at = pl.ds(c * rows + r, PIX)
-                    wide[j + 1, at, :] = wide[j + 1, at, :] + over[c * PIX : (c + 1) * PIX]
+                    wide[j + 1, at, :] = wide[j + 1, at, :] + moved[c * PIX : (c + 1) * PIX, LANES:]
 
     for_listed(n, 4, body)
     for j in range(panels):
@@ -320,6 +322,7 @@
     position = lax.broadcasted_iota(jnp.int32, (PIX, samples), 0).astype(F32) * (1.0 / PIX)
 
     def step(g, carry):
+        done = []
         for k in range(group):
             s = g * group + k
             uv_rows = uv[s]
@@ -338,8 +341,10 @@
                 wave_x, weighted, (((1,), (1,)), ((), ())), preferred_element_type=F32
             )
             low, high = products[:PIX], products[PIX:]
-            out[s, 0:PIX] = low[:, :LANES] - high[:, LANES:]
-            out[s, PIX:] = low[:, LANES:] + high[:, :LANES]
+            done.append((s, low[:, :LANES] - high[:, LANES:], low[:, LANES:] + high[:, :LANES]))
+        for s, re, im in done:
+            out[s, 0:PIX] = re
+            out[s, PIX:] = im
         return carry
 
     lax.fori_loop(0, vis.shape[0] // group, step, 0)
@@ -369,9 +374,17 @@
     return copies
 
 
-def screens_of(table, row, spread):
-    wide = dot(table[row], spread[...])
-    return wide[:, :LANES], wide[:, LANES:]
+def screens_of(table, rows, spread):
+    wide = dot(jnp.concatenate([table[row] for row in rows], 0), spread[...])
+    at = [slice(k * PIX, (k + 1) * PIX) for k in range(len(rows))]
+    return [(wide[k, :LANES], wide[k, LANES:]) for k in at]
+
+
+def transforms(left, pieces, right):
+    inner = dot(left[...], jnp.concatenate(pieces, 1)).astype(BF16)
+    lines = [inner[:, k * LANES : (k + 1) * LANES] for k in range(len(pieces))]
+    outer = dot(jnp.concatenate(lines, 0), right[...])
+    return [outer[k * 2 * PIX : (k + 1) * 2 * PIX] for k in range(len(pieces))]
 
 
 def patch_kernel(
@@ -382,22 +395,25 @@
         copy.wait()
 
     def step(g, carry):
-        for k in range(group):
-            s = g * group + k
-            a_re, a_im = screens_of(table, first[s], spread_a)
-            b_re, b_im = screens_of(table, second[s], spread_b)
+        subs = [g * group + k for k in range(group)]
+        first_screens = screens_of(table, [first[s] for s in subs], spread_a)
+        second_screens = screens_of(table, [second[s] for s in subs], spread_b)
+        backs = []
+        for s, (a_re, a_im), (b_re, b_im) in zip(subs, first_screens, second_screens):
             m_re, m_im = image[s, 0:PIX], image[s, PIX:]
             both_re = a_re * b_re + a_im * b_im
             both_im = a_re * b_im - a_im * b_re
             back_re = both_re * m_re - both_im * m_im
             back_im = both_re * m_im + both_im * m_re
-            back = jnp.concatenate([back_re, back_im], 0).astype(BF16)
-            low = dot(backward[...], back).astype(BF16)
-            grad = dot(low, right[...])
+            backs.append(jnp.concatenate([back_re, back_im], 0).astype(BF16))
+        grads = []
+        for grad in transforms(backward, backs, right):
             re, im = grad[:PIX], grad[PIX:]
             grad_re = re[:, :LANES] + im[:, LANES:]
             grad_im = im[:, :LANES] - re[:, LANES:]
-            out[slot[s]] = jnp.concatenate([grad_re, grad_im], 0).astype(BF16)
+            grads.append(jnp.concatenate([grad_re, grad_im], 0).astype(BF16))
+        for s, grad in zip(subs, grads):
+            out[slot[s]] = grad
         return carry
 
     lax.fori_loop(0, image.shape[0] // group, step, 0)
@@ -440,14 +456,13 @@
 
     def step(g, carry):
         terms = []
-        for k in range(group):
-            s = g * group + k
-            a_re, a_im = screens_of(table, first[s], spread_a)
-            b_re, b_im = screens_of(table, second[s], spread_b)
+        subs = [g * group + k for k in range(group)]
+        first_screens = screens_of(table, [first[s] for s in subs], spread_a)
+        second_screens = screens_of(table, [second[s] for s in subs], spread_b)
+        skies = transforms(forward, [patches[slot[s]] for s in subs], right)
+        for s, (a_re, a_im), (b_re, b_im), sky in zip(subs, first_screens, second_screens, skies):
             m_re, m_im = image[s, 0:PIX], image[s, PIX:]
-            mid = dot(forward[...], patches[slot[s]]).astype(BF16)
-            wide = dot(mid, right[...])
-            re, im = wide[:PIX], wide[PIX:]
+            re, im = sky[:PIX], sky[PIX:]
             sky_re = re[:, :LANES] - im[:, LANES:]
             sky_im = re[:, LANES:] + im[:, :LANES]
             carry_re = b_re * m_re - b_im * m_im
@@ -541,7 +556,7 @@
         owner_tile[0, :, 0],
         row_offset[0],
         column[0],
-        stations[0].reshape(-1),
+        stations[0].T,
         time_slot[0],
         screens[:, 0],
         n_bt,
@@ -550,21 +565,21 @@
     image = adjoint_images(residual[0], uv_coords[0])
     mail, image = lax.optimization_barrier((exchange(mail, "bt"), image))
     asked = mail[:, row].astype(jnp.int32)
+    near = ring_gather(mail[:, :row], n_z).reshape(n_z * n_bt * TSLOTS, PIX, LANES)
+    far = lax.ppermute(near, "freq", swap)
     cut = cut_windows(asked, uv_grid[0])
-    cut, screens_here = lax.optimization_barrier((cut, mail[:, :row]))
     fetched = exchange(cut.reshape(n_bt, CAP, 2 * PIX, LANES), "bt")
     fetched = fetched.reshape(slots, 2 * PIX, LANES)
-    near = ring_gather(screens_here, n_z).reshape(n_z * n_bt * TSLOTS, PIX, LANES)
-    far = lax.ppermute(near, "freq", swap)
+    grads = patch_gradients(slot, first, second, image, near, far, consts, slots)
+    returned = exchange(grads.reshape(n_bt, CAP, 2 * PIX, LANES), "bt")
+    returned = returned.reshape(slots, 2 * PIX, LANES)
     terms, sent = screen_gradients(
         slot, (first, second, first_sum, second_sum), image, fetched, near, far, consts
     )
-    grads = patch_gradients(slot, first, second, image, near, far, consts, slots)
-    returned = exchange(grads.reshape(n_bt, CAP, 2 * PIX, LANES), "bt").reshape(slots, 2 * PIX, LANES)
-    grid_grad = add_windows(asked, returned, *uv_grid.shape[1:])
     came = lax.ppermute(sent, "freq", swap)
     part = (terms.astype(F32) + came.astype(F32)).astype(BF16)
     part = exchange(part.reshape(n_bt, n_z, TSLOTS, PIX, LANES), "bt")
+    grid_grad = add_windows(asked, returned, *uv_grid.shape[1:])
     part = jnp.sum(part.astype(F32), 0).astype(BF16)
     screen_grad = finish(exchange(part, "freq", same_core))
     return grid_grad[None], screen_grad[:, None]

time: 236 us -> 229 us (0.970)
  Pallas kernels: 93.7 us -> 78.5 us
  waiting for transfers between devices: 59.6 us -> 70.9 us
  local copies, waits for them, and re-layouts: 3.76 us -> 1.05 us
    pallas_call x1, Pallas kernels: 24.6 us -> 13.2 us  [patch_gradients(): pl.pallas_call(lambda *refs: patch_kernel(group, *refs), out_shape=jax.Sh...]
    all_to_all x4, waiting for transfers between devices: 32.5 us -> 44 us  [exchange(): lax.all_to_all(x, axis, split_axis=0, concat_axis=0, tiled=True, axis_ind...]
  transfers between devices with their start and end apart: 13 -> 13, of which waited for: 9 -> 9; matrix products, arithmetic and copies ran while one was open for 1% -> 1% of each run, Pallas kernels for 23% -> 24%
where the time goes in v3:
time: 229 us
  Pallas kernels  78.5 us (34%)
  waiting for transfers between devices  70.9 us (31%)
  starting transfers between devices  40.2 us (18%)
  blocking collectives  32 us (14%)
  other arithmetic  5.29 us (2%)
    all_to_all x4, waiting for transfers between devices, exchange(): lax.all_to_all(x, axis, split_axis=0, concat_axis=0, tiled=True, axis_ind...  44 us
    all_to_all x1, blocking collectives, exchange(): lax.all_to_all(x, axis, split_axis=0, concat_axis=0, tiled=True, axis_ind...  32 us
    all_to_all x4, starting transfers between devices, exchange(): lax.all_to_all(x, axis, split_axis=0, concat_axis=0, tiled=True, axis_ind...  30.9 us
    ppermute x4, waiting for transfers between devices, ring_gather(): up = lax.ppermute(up, 'freq', by(1))  21.8 us
    pallas_call x1, Pallas kernels, add_windows(): pl.pallas_call(add_kernel, out_shape=jax.ShapeDtypeStruct((comps, rows, c...  16.2 us
    pallas_call x1, Pallas kernels, screen_gradients(): pl.pallas_call(lambda *refs: screen_kernel(group, *refs), out_shape=(jax....  15.3 us
    pallas_call x1, Pallas kernels, cut_windows(): pl.pallas_call(cut_kernel, out_shape=jax.ShapeDtypeStruct((slots, 2 * PIX...  14.7 us
    pallas_call x1, Pallas kernels, patch_gradients(): pl.pallas_call(lambda *refs: patch_kernel(group, *refs), out_shape=jax.Sh...  13.2 us
  transfers between devices with their start and end apart: 13, of which 9 were waited for; matrix products, arithmetic and copies ran while one was open for 1% of the time, Pallas kernels for 24%

profile of v3, /device:TPU:54, one launch (start us, length us, event | category | flops | bytes accessed | tf_op | source)
XLA Modules:
  0.0 228.6 jit_solution(1467945416372357312)
XLA Ops:
  0.6 5.8 %mail.1 = (bf16[16,80,128]{2,1,0:T(8,128)(2,1)}, s32[64]{0:T(128)}, s32[64]{0:T(128)}, s32[64]{0:T(128)}, s32[64]{0:T(128)}, /*index=5*/s32[64]{0:T(128)}) custom-call(s32[1]{0:T(128)} %bitcast.refs_0_, s32[64]{0:T(128)} %bitcast.56, s32[64]{0:T(128)} %bitcast.57, s32[64]{0:T(128)} %bitcast.58, s32[2,64]{1,0:T(2,128)} %bitcast.55, s32[64]{0:T(128)} %bitcast.59, ...), custom_call_target="tpu_custom_call" | custom-call | tf_op jit(solution)/shard_map/mail/pallas_call | solution.py:127
  6.5 7.2 %all-to-all-start = ((bf16[16,80,128]{2,1,0:T(8,128)(2,1)}), bf16[16,80,128]{2,1,0:T(8,128)(2,1)S(1)}, u32[]{:S(2)}, u32[]{:S(2)}) async-start(bf16[16,80,128]{2,1,0:T(8,128)(2,1)} %get-tuple-element.12), calls=%async_computation | async-start | bytes 655360 | tf_op jit(solution)/shard_map/all_to_all | solution.py:524
  13.7 11.5 %image.1.refs_3_.refs_5_ = f32[64,64,128]{2,1,0:T(8,128)} custom-call(bf16[64,8,256]{2,1,0:T(8,128)(2,1)} %bitcast.51, f32[64,2,256]{2,1,0:T(2,128)} %bitcast.52), custom_call_target="tpu_custom_call" | custom-call | tf_op jit(solution)/shard_map/image/pallas_call | solution.py:357
  25.2 2.0 collective-permute-start.3
  27.2 0.1 collective-permute-start
  27.3 5.5 %collective-permute-done.3 = bf16[16,64,128]{2,1,0:T(8,128)(2,1)S(1)} collective-permute-done((bf16[16,64,128]{2,1,0:T(8,128)(2,1)S(1)}, bf16[16,64,128]{2,1,0:T(8,128)(2,1)S(1)}, u32[]{:S(2)}, u32[]{:S(2)}) %collective-permute-start.3) | collective-permute-done | bytes 262176 | tf_op jit(solution)/shard_map/ppermute | solution.py:536
  32.8 1.9 collective-permute-start.4
  34.7 2.3 %collective-permute-start.1 = (bf16[16,64,128]{2,1,0:T(8,128)(2,1)S(1)}, bf16[16,64,128]{2,1,0:T(8,128)(2,1)S(1)}, u32[]{:S(2)}, u32[]{:S(2)}) collective-permute-start(bf16[16,64,128]{2,1,0:T(8,128)(2,1)S(1)} %collective-permute-done), channel_id=1, source_target_pairs={{0,14},{1,15},{2,0},{3,1},{4,2},{5,3},{6,4},{7,5},{8,6},{9,7},{10,... | collective-permute-start | bytes 786440 | tf_op jit(solution)/shard_map/ppermute | solution.py:539
  37.0 5.2 %collective-permute-done.4 = bf16[16,64,128]{2,1,0:T(8,128)(2,1)S(1)} collective-permute-done((bf16[16,64,128]{2,1,0:T(8,128)(2,1)S(1)}, bf16[16,64,128]{2,1,0:T(8,128)(2,1)S(1)}, u32[]{:S(2)}, u32[]{:S(2)}) %collective-permute-start.4) | collective-permute-done | bytes 262176 | tf_op jit(solution)/shard_map/ppermute | solution.py:536
  42.3 0.3 collective-permute-done.1
  42.6 2.7 %collective-permute-start.2 = (bf16[16,64,128]{2,1,0:T(8,128)(2,1)S(1)}, bf16[16,64,128]{2,1,0:T(8,128)(2,1)S(1)}, u32[]{:S(2)}, u32[]{:S(2)}) collective-permute-start(bf16[16,64,128]{2,1,0:T(8,128)(2,1)S(1)} %collective-permute-done.1), channel_id=1, source_target_pairs={{0,14},{1,15},{2,0},{3,1},{4,2},{5,3},{6,4},{7,5},{8,6},{9,7},{10,... | collective-permute-start | bytes 786440 | tf_op jit(solution)/shard_map/ppermute | solution.py:539
  45.4 4.1 %collective-permute-done.5 = bf16[16,64,128]{2,1,0:T(8,128)(2,1)S(1)} collective-permute-done((bf16[16,64,128]{2,1,0:T(8,128)(2,1)S(1)}, bf16[16,64,128]{2,1,0:T(8,128)(2,1)S(1)}, u32[]{:S(2)}, u32[]{:S(2)}) %collective-permute-start.5) | collective-permute-done | bytes 262176 | tf_op jit(solution)/shard_map/ppermute | solution.py:536
  49.5 0.4 collective-permute-done.2
  49.9 7.1 %collective-permute-done.6 = bf16[16,64,128]{2,1,0:T(8,128)(2,1)S(1)} collective-permute-done((bf16[16,64,128]{2,1,0:T(8,128)(2,1)S(1)}, bf16[16,64,128]{2,1,0:T(8,128)(2,1)S(1)}, u32[]{:S(2)}, u32[]{:S(2)}) %collective-permute-start.6) | collective-permute-done | bytes 262176 | tf_op jit(solution)/shard_map/ppermute | solution.py:536
  57.2 0.1 collective-permute-start.7
  57.3 0.7 fusion.asked
  58.1 14.7 %cut.1 = bf16[128,64,128]{2,1,0:T(8,128)(2,1)} custom-call(s32[16,128]{1,0:T(8,128)} %fusion.asked, bf16[8,64,1024]{2,1,0:T(8,128)(2,1)} %bitcast.50), custom_call_target="tpu_custom_call" | custom-call | tf_op jit(solution)/shard_map/cut/pallas_call | solution.py:235
  72.8 32.0 %all_to_all.25 = bf16[16,8,64,128]{3,2,1,0:T(8,128)(2,1)} all-to-all(bf16[16,8,64,128]{3,2,1,0:T(8,128)(2,1)} %bitcast.48), channel_id=1, replica_groups=mesh['bt'=16,'freq'=16] {'bt'}, dimensions={0} | all-to-all | bytes 4194304 | tf_op jit(solution)/shard_map/all_to_all | solution.py:524
  104.8 15.3 %screen.1 = (bf16[256,32,128]{2,1,0:T(8,128)(2,1)}, bf16[256,32,128]{2,1,0:T(8,128)(2,1)}) custom-call(s32[64]{0:T(128)} %get-tuple-element.14.refs_0_, s32[64]{0:T(128)} %get-tuple-element.15.refs_1_, s32[64]{0:T(128)} %get-tuple-element.16.refs_2_, s32[64]{0:T(128)} %get-tuple-element.18.refs_3_, s32[64]{0:T(128)} %get-tuple-element.19.refs_4_, ...), custom_call_target="tpu_custom_call" | custom-call | tf_op jit(solution)/shard_map/screen/pallas_call | solution.py:513
  120.1 0.1 collective-permute-start.8
  120.2 4.4 %collective-permute-done.8 = bf16[256,32,128]{2,1,0:T(8,128)(2,1)S(1)} collective-permute-done((bf16[256,32,128]{2,1,0:T(8,128)(2,1)}, bf16[256,32,128]{2,1,0:T(8,128)(2,1)S(1)}, u32[]{:S(2)}, u32[]{:S(2)}) %collective-permute-start.8) | collective-permute-done | bytes 2097184 | tf_op jit(solution)/shard_map/ppermute | solution.py:579
  124.6 3.5 %add_convert_fusion = bf16[256,32,128]{2,1,0:T(8,128)(2,1)} fusion(bf16[256,32,128]{2,1,0:T(8,128)(2,1)S(1)} %collective-permute-done.8, bf16[256,32,128]{2,1,0:T(8,128)(2,1)} %get-tuple-element.20), kind=kLoop, calls=%fused_computation | loop fusion | flops 4194304 | bytes 6291456 | tf_op jit(solution)/shard_map/convert_element_type | solution.py:580
  128.1 7.8 %all-to-all-start.3 = ((bf16[16,8,2,32,128]{4,3,2,1,0:T(8,128)(2,1)}), bf16[16,8,2,32,128]{4,3,2,1,0:T(8,128)(2,1)S(1)}, u32[]{:S(2)}, u32[]{:S(2)}) async-start(bf16[16,8,2,32,128]{4,3,2,1,0:T(8,128)(2,1)} %bitcast.27), calls=%async_computation.3 | async-start | bytes 4194304 | tf_op jit(solution)/shard_map/all_to_all | solution.py:524
  135.8 13.2 %patch.1 = bf16[128,64,128]{2,1,0:T(8,128)(2,1)} custom-call(s32[64]{0:T(128)} %get-tuple-element.14.refs_0_, s32[64]{0:T(128)} %get-tuple-element.15.refs_1_, s32[64]{0:T(128)} %get-tuple-element.16.refs_2_, f32[64,64,128]{2,1,0:T(8,128)} %image.1.refs_3_.refs_5_, bf16[256,32,128]{2,1,0:T(8,128)(2,1)} %bitcast.45, ...), custom_call_target="tpu_custom_call" | custom-call | tf_op jit(solution)/shard_map/patch/pallas_call | solution.py:431
  149.0 17.5 %all-to-all-done.3 = bf16[16,8,2,32,128]{4,3,2,1,0:T(8,128)(2,1)S(1)} async-done(((bf16[16,8,2,32,128]{4,3,2,1,0:T(8,128)(2,1)}), bf16[16,8,2,32,128]{4,3,2,1,0:T(8,128)(2,1)S(1)}, u32[]{:S(2)}, u32[]{:S(2)}) %all-to-all-start.3) | async-done | bytes 2097184 | tf_op jit(solution)/shard_map/all_to_all | solution.py:524
  166.5 7.6 %all-to-all-start.1 = ((bf16[16,8,64,128]{3,2,1,0:T(8,128)(2,1)}), bf16[16,8,64,128]{3,2,1,0:T(8,128)(2,1)}, u32[]{:S(2)}, u32[]{:S(2)}) async-start(bf16[16,8,64,128]{3,2,1,0:T(8,128)(2,1)} %bitcast.46), calls=%async_computation.1 | async-start | bytes 4194304 | tf_op jit(solution)/shard_map/all_to_all | solution.py:524
  174.1 1.1 reduce_sum.12
  175.1 26.5 %all-to-all-done.1 = bf16[16,8,64,128]{3,2,1,0:T(8,128)(2,1)} async-done(((bf16[16,8,64,128]{3,2,1,0:T(8,128)(2,1)}), bf16[16,8,64,128]{3,2,1,0:T(8,128)(2,1)}, u32[]{:S(2)}, u32[]{:S(2)}) %all-to-all-start.1) | async-done | bytes 2097184 | tf_op jit(solution)/shard_map/all_to_all | solution.py:524
  201.6 8.4 %all-to-all-start.4 = ((bf16[8,2,32,128]{3,2,1,0:T(8,128)(2,1)}), bf16[8,2,32,128]{3,2,1,0:T(8,128)(2,1)S(1)}, u32[]{:S(2)}, u32[]{:S(2)}) async-start(bf16[8,2,32,128]{3,2,1,0:T(8,128)(2,1)} %reduce_sum.12), calls=%async_computation.4 | async-start | bytes 262144 | tf_op jit(solution)/shard_map/all_to_all | solution.py:524
  210.0 16.2 %add.6 = f32[8,64,1024]{2,1,0:T(8,128)} custom-call(s32[16,128]{1,0:T(8,128)} %fusion.asked, bf16[128,64,128]{2,1,0:T(8,128)(2,1)} %bitcast.21.pieces), custom_call_target="tpu_custom_call" | custom-call | tf_op jit(solution)/shard_map/add/pallas_call | solution.py:292
  226.2 0.7 copy-done.1
  226.9 1.7 finish.1
  (19 shorter events, 0.4 us)
Async XLA Ops:
  6.5 18.7 %all-to-all-start = ((bf16[16,80,128]{2,1,0:T(8,128)(2,1)}), bf16[16,80,128]{2,1,0:T(8,128)(2,1)S(1)}, u32[]{:S(2)}, u32[]{:S(2)}) async-start(bf16[16,80,128]{2,1,0:T(8,128)(2,1)} %get-tuple-element.12), calls=%async_computation | async-start | bytes 655360 | tf_op jit(solution)/shard_map/all_to_all | solution.py:524
  25.2 7.6 %collective-permute-start.3 = (bf16[16,64,128]{2,1,0:T(8,128)(2,1)S(1)}, bf16[16,64,128]{2,1,0:T(8,128)(2,1)S(1)}, u32[]{:S(2)}, u32[]{:S(2)}) collective-permute-start(bf16[16,64,128]{2,1,0:T(8,128)(2,1)S(1)} %slice.7), channel_id=1, source_target_pairs={{0,2},{1,3},{2,4},{3,5},{4,6},{5,7},{6,8},{7,9},{8,10},{9,11},{10,... | collective-permute-start | bytes 786440 | tf_op jit(solution)/shard_map/ppermute | solution.py:536
  27.2 7.5 %collective-permute-start = (bf16[16,64,128]{2,1,0:T(8,128)(2,1)S(1)}, bf16[16,64,128]{2,1,0:T(8,128)(2,1)S(1)}, u32[]{:S(2)}, u32[]{:S(2)}) collective-permute-start(bf16[16,64,128]{2,1,0:T(8,128)(2,1)S(1)} %slice.7), channel_id=1, source_target_pairs={{0,14},{1,15},{2,0},{3,1},{4,2},{5,3},{6,4},{7,5},{8,6},{9,7},{10,... | collective-permute-start | bytes 786440 | tf_op jit(solution)/shard_map/ppermute | solution.py:539
  32.8 9.4 %collective-permute-start.4 = (bf16[16,64,128]{2,1,0:T(8,128)(2,1)S(1)}, bf16[16,64,128]{2,1,0:T(8,128)(2,1)S(1)}, u32[]{:S(2)}, u32[]{:S(2)}) collective-permute-start(bf16[16,64,128]{2,1,0:T(8,128)(2,1)S(1)} %collective-permute-done.3), channel_id=1, source_target_pairs={{0,2},{1,3},{2,4},{3,5},{4,6},{5,7},{6,8},{7,9},{8,10},{9,11},{10,... | collective-permute-start | bytes 786440 | tf_op jit(solution)/shard_map/ppermute | solution.py:536
  34.7 7.9 %collective-permute-start.1 = (bf16[16,64,128]{2,1,0:T(8,128)(2,1)S(1)}, bf16[16,64,128]{2,1,0:T(8,128)(2,1)S(1)}, u32[]{:S(2)}, u32[]{:S(2)}) collective-permute-start(bf16[16,64,128]{2,1,0:T(8,128)(2,1)S(1)} %collective-permute-done), channel_id=1, source_target_pairs={{0,14},{1,15},{2,0},{3,1},{4,2},{5,3},{6,4},{7,5},{8,6},{9,7},{10,... | collective-permute-start | bytes 786440 | tf_op jit(solution)/shard_map/ppermute | solution.py:539
  42.2 7.3 %collective-permute-start.5 = (bf16[16,64,128]{2,1,0:T(8,128)(2,1)S(1)}, bf16[16,64,128]{2,1,0:T(8,128)(2,1)S(1)}, u32[]{:S(2)}, u32[]{:S(2)}) collective-permute-start(bf16[16,64,128]{2,1,0:T(8,128)(2,1)S(1)} %collective-permute-done.4), channel_id=1, source_target_pairs={{0,2},{1,3},{2,4},{3,5},{4,6},{5,7},{6,8},{7,9},{8,10},{9,11},{10,... | collective-permute-start | bytes 786440 | tf_op jit(solution)/shard_map/ppermute | solution.py:536
  42.6 7.3 %collective-permute-start.2 = (bf16[16,64,128]{2,1,0:T(8,128)(2,1)S(1)}, bf16[16,64,128]{2,1,0:T(8,128)(2,1)S(1)}, u32[]{:S(2)}, u32[]{:S(2)}) collective-permute-start(bf16[16,64,128]{2,1,0:T(8,128)(2,1)S(1)} %collective-permute-done.1), channel_id=1, source_target_pairs={{0,14},{1,15},{2,0},{3,1},{4,2},{5,3},{6,4},{7,5},{8,6},{9,7},{10,... | collective-permute-start | bytes 786440 | tf_op jit(solution)/shard_map/ppermute | solution.py:539
  49.5 7.6 %collective-permute-start.6 = (bf16[16,64,128]{2,1,0:T(8,128)(2,1)S(1)}, bf16[16,64,128]{2,1,0:T(8,128)(2,1)S(1)}, u32[]{:S(2)}, u32[]{:S(2)}) collective-permute-start(bf16[16,64,128]{2,1,0:T(8,128)(2,1)S(1)} %collective-permute-done.5), channel_id=1, source_target_pairs={{0,2},{1,3},{2,4},{3,5},{4,6},{5,7},{6,8},{7,9},{8,10},{9,11},{10,... | collective-permute-start | bytes 786440 | tf_op jit(solution)/shard_map/ppermute | solution.py:536
  57.2 47.6 %copy-start = (bf16[8,16,64,128]{3,2,1,0:T(8,128)(2,1)}, bf16[8,16,64,128]{3,2,1,0:T(8,128)(2,1)S(1)}, u32[]{:S(2)}) copy-start(bf16[8,16,64,128]{3,2,1,0:T(8,128)(2,1)S(1)} %bitcast_dynamic-update-slice_fusion) | copy-start | bytes 6291460
  57.2 47.6 %collective-permute-start.7 = (bf16[256,32,128]{2,1,0:T(8,128)(2,1)S(1)}, bf16[256,32,128]{2,1,0:T(8,128)(2,1)}, u32[]{:S(2)}, u32[]{:S(2)}) collective-permute-start(bf16[256,32,128]{2,1,0:T(8,128)(2,1)S(1)} %bitcast.43), channel_id=1, source_target_pairs={{0,1},{1,0},{2,3},{3,2},{4,5},{5,4},{6,7},{7,6},{8,9},{9,8},{10,11... | collective-permute-start | bytes 6291464 | tf_op jit(solution)/shard_map/ppermute | solution.py:569
  120.1 4.5 %collective-permute-start.8 = (bf16[256,32,128]{2,1,0:T(8,128)(2,1)}, bf16[256,32,128]{2,1,0:T(8,128)(2,1)S(1)}, u32[]{:S(2)}, u32[]{:S(2)}) collective-permute-start(bf16[256,32,128]{2,1,0:T(8,128)(2,1)} %get-tuple-element.21), channel_id=1, source_target_pairs={{0,1},{1,0},{2,3},{3,2},{4,5},{5,4},{6,7},{7,6},{8,9},{9,8},{10,11... | collective-permute-start | bytes 6291464 | tf_op jit(solution)/shard_map/ppermute | solution.py:579
  128.1 38.4 %all-to-all-start.3 = ((bf16[16,8,2,32,128]{4,3,2,1,0:T(8,128)(2,1)}), bf16[16,8,2,32,128]{4,3,2,1,0:T(8,128)(2,1)S(1)}, u32[]{:S(2)}, u32[]{:S(2)}) async-start(bf16[16,8,2,32,128]{4,3,2,1,0:T(8,128)(2,1)} %bitcast.27), calls=%async_computation.3 | async-start | bytes 4194304 | tf_op jit(solution)/shard_map/all_to_all | solution.py:524
  166.5 35.1 %all-to-all-start.1 = ((bf16[16,8,64,128]{3,2,1,0:T(8,128)(2,1)}), bf16[16,8,64,128]{3,2,1,0:T(8,128)(2,1)}, u32[]{:S(2)}, u32[]{:S(2)}) async-start(bf16[16,8,64,128]{3,2,1,0:T(8,128)(2,1)} %bitcast.46), calls=%async_computation.1 | async-start | bytes 4194304 | tf_op jit(solution)/shard_map/all_to_all | solution.py:524
  201.6 24.6 %all-to-all-start.4 = ((bf16[8,2,32,128]{3,2,1,0:T(8,128)(2,1)}), bf16[8,2,32,128]{3,2,1,0:T(8,128)(2,1)S(1)}, u32[]{:S(2)}, u32[]{:S(2)}) async-start(bf16[8,2,32,128]{3,2,1,0:T(8,128)(2,1)} %reduce_sum.12), calls=%async_computation.4 | async-start | bytes 262144 | tf_op jit(solution)/shard_map/all_to_all | solution.py:524
  226.2 0.7 copy-start.1

commit v4 on v3

--- a/solution.py
+++ b/solution.py
@@ -61,43 +61,22 @@
 
 
 def mail_kernel(
-    n_bt, n_freq, me, owner, row_offset, column, stations, slot_time, screens,
-    mail, slot, first, second, first_sum, second_sum, fill, request, own,
+    n_bt, owner, row_offset, column, screens, mail, slot, fill, request, own,
 ):
     count = owner.shape[0]
-    n_z = n_freq // 2
-    my_z, my_core = me[0] // 2, me[0] % 2
-
-    def clear(i, carry):
-        request[i] = -1
-        return carry
-
-    lax.fori_loop(0, n_bt * CAP, clear, 0)
-
-    def zero(i, carry):
+    for i in range(n_bt):
         fill[i] = 0
-        return carry
-
-    lax.fori_loop(0, n_bt, zero, 0)
-
-    def rows(station, t):
-        bt, freq = station // n_freq, station % n_freq
-        z, core = freq // 2, freq % 2
-        half = jnp.where(core == my_core, 0, n_bt * n_z)
-        ahead = (z - my_z + n_z) % n_z
-        return (half + ahead * n_bt + bt) * TSLOTS + t, (half + bt * n_z + z) * TSLOTS + t
 
     def step(s, carry):
         o = owner[s]
-        place = o * CAP + fill[o]
-        fill[o] = fill[o] + 1
+        n = fill[o]
+        fill[o] = n + 1
+        place = o * CAP + n
         slot[s] = place
         request[place] = row_offset[s] * 1024 + column[s]
-        first[s], first_sum[s] = rows(stations[0, s], slot_time[s])
-        second[s], second_sum[s] = rows(stations[1, s], slot_time[s])
-        return carry
-
-    lax.fori_loop(0, count, step, 0)
+        return carry
+
+    lax.fori_loop(0, count, step, 0, unroll=4)
     for t in range(TSLOTS):
         table = screens[t].astype(F32)
         for high in range(PIX // 4):
@@ -108,9 +87,10 @@
     lane = lax.broadcasted_iota(jnp.int32, (16, LANES), 1)
 
     def address(j, carry):
-        line = jnp.full((16, LANES), -1, jnp.int32)
+        n = fill[j]
+        line = jnp.where(lane == 3 * CAP, n, 0)
         for k in range(CAP):
-            code = request[j * CAP + k]
+            code = jnp.where(k < n, request[j * CAP + k], 0)
             for part, value in enumerate((code >> 10, (code >> 5) & 31, code & 31)):
                 line = jnp.where(lane == part * CAP + k, value, line)
         mail[j] = jnp.concatenate([every, line.astype(F32).astype(BF16)], 0)
@@ -119,23 +99,25 @@
     lax.fori_loop(0, n_bt, address, 0)
 
 
-def make_mail(me, owners, row_offset, column, stations, slot_time, screens, n_bt, n_freq):
+def make_mail(owners, row_offset, column, screens, n_bt):
     count = owners.shape[0]
     smem, vmem = pl.BlockSpec(memory_space=pltpu.SMEM), pl.BlockSpec(memory_space=pltpu.VMEM)
-    ints = jax.ShapeDtypeStruct((count,), jnp.int32)
     rows = TSLOTS * PIX
     return pl.pallas_call(
-        lambda *refs: mail_kernel(n_bt, n_freq, *refs),
-        out_shape=(jax.ShapeDtypeStruct((n_bt, rows + 16, LANES), BF16),) + (ints,) * 5,
-        in_specs=[smem] * 6 + [vmem],
-        out_specs=(vmem,) + (smem,) * 5,
+        lambda *refs: mail_kernel(n_bt, *refs),
+        out_shape=(
+            jax.ShapeDtypeStruct((n_bt, rows + 16, LANES), BF16),
+            jax.ShapeDtypeStruct((count,), jnp.int32),
+        ),
+        in_specs=[smem] * 3 + [vmem],
+        out_specs=(vmem, smem),
         scratch_shapes=[
             pltpu.SMEM((n_bt,), jnp.int32),
             pltpu.SMEM((n_bt * CAP,), jnp.int32),
             pltpu.VMEM((rows, LANES), F32),
         ],
         name="mail",
-    )(me, owners, row_offset, column, stations, slot_time, screens)
+    )(owners, row_offset, column, screens)
 
 
 def finish_kernel(parts, out):
@@ -162,15 +144,16 @@
 
 
 def listed(asked, order):
-    def step(i, n):
-        order[n] = i
-        return n + (asked[i // CAP, i % CAP] >= 0).astype(jnp.int32)
-
-    return lax.fori_loop(0, asked.shape[0] * CAP, step, jnp.int32(0))
+    def step(j, n):
+        for k in range(CAP):
+            order[n + k] = j * CAP + k
+        return n + asked[j, 3 * CAP]
+
+    return lax.fori_loop(0, asked.shape[0], step, jnp.int32(0))
 
 
 def corner(asked, i):
-    j, k = i // CAP, i % CAP
+    j, k = i >> 3, i & 7
     return asked[j, k], asked[j, CAP + k] * PIX + asked[j, 2 * CAP + k]
 
 
@@ -188,7 +171,7 @@
     lax.fori_loop(n // group * group, n, rest, 0)
 
 
-def cut_kernel(asked, tile, out, wide, order):
+def cut_kernel(asked, tile, out, wide, order, stage, sems):
     comps, rows, columns = tile.shape
     panels = columns // LANES
     for j in range(panels):
@@ -204,7 +187,7 @@
         for place in places:
             i = order[place]
             r, c0 = corner(asked, i)
-            j, shift = c0 // LANES, c0 % LANES
+            j, shift = c0 >> 7, c0 & (LANES - 1)
             after = jnp.minimum(j + 1, panels - 1)
 
             def rows_of(panel):
@@ -224,9 +207,18 @@
                 parts.append(part)
             done.append((i, jnp.concatenate(parts, 0).astype(BF16)))
         for i, piece in done:
-            out[i] = piece
+            stage[i] = piece
+        for i, piece in done:
+            pltpu.make_async_copy(stage.at[i], out.at[i], sems.at[i]).start()
 
     for_listed(n, 4, body)
+
+    def finished(g, carry):
+        i = order[g]
+        pltpu.make_async_copy(stage.at[i], out.at[i], sems.at[i]).wait()
+        return carry
+
+    lax.fori_loop(0, n, finished, 0)
 
 
 def cut_windows(asked, tile):
@@ -236,10 +228,12 @@
         cut_kernel,
         out_shape=jax.ShapeDtypeStruct((slots, 2 * PIX, LANES), BF16),
         in_specs=[pl.BlockSpec(memory_space=pltpu.SMEM), pl.BlockSpec(memory_space=pltpu.VMEM)],
-        out_specs=pl.BlockSpec(memory_space=pltpu.VMEM),
+        out_specs=pl.BlockSpec(memory_space=pl.ANY),
         scratch_shapes=[
             pltpu.VMEM((columns // LANES, comps * rows, LANES), F32),
-            pltpu.SMEM((slots + 1,), jnp.int32),
+            pltpu.SMEM((slots + CAP,), jnp.int32),
+            pltpu.VMEM((slots, 2 * PIX, LANES), BF16),
+            pltpu.SemaphoreType.DMA((slots,)),
         ],
         name="cut",
     )(asked, tile)
@@ -261,7 +255,7 @@
         for place in places:
             i = order[place]
             r, c0 = corner(asked, i)
-            j, shift = c0 // LANES, c0 % LANES
+            j, shift = c0 >> 7, c0 & (LANES - 1)
             piece = pieces[i].astype(F32)
             lines = []
             for ri in range(2):
@@ -296,7 +290,7 @@
         out_specs=pl.BlockSpec(memory_space=pltpu.VMEM),
         scratch_shapes=[
             pltpu.VMEM((columns // LANES, comps * rows, LANES), F32),
-            pltpu.SMEM((slots + 1,), jnp.int32),
+            pltpu.SMEM((slots + CAP,), jnp.int32),
         ],
         name="add",
     )(asked, pieces)
@@ -350,27 +344,46 @@
     lax.fori_loop(0, vis.shape[0] // group, step, 0)
 
 
-def adjoint_images(vis, uv):
-    count = vis.shape[0]
+def adjoint_images(vis, uv, part, parts):
+    count = vis.shape[0] // parts
     group = math.gcd(count, 4)
-    vmem = pl.BlockSpec(memory_space=pltpu.VMEM)
+    blocks = [
+        pl.BlockSpec((count,) + x.shape[1:], lambda i: (part, 0, 0)) for x in (vis, uv)
+    ]
     return pl.pallas_call(
         lambda *refs: image_kernel(group, *refs),
         out_shape=jax.ShapeDtypeStruct((count, 2 * PIX, LANES), F32),
-        in_specs=[vmem, vmem],
-        out_specs=vmem,
+        grid=(1,),
+        in_specs=blocks,
+        out_specs=pl.BlockSpec((count, 2 * PIX, LANES), lambda i: (0, 0, 0)),
         name="image",
     )(vis, uv)
 
 
-def join_halves(near, far, table, sems):
-    half = near.shape[0]
-    copies = [
-        pltpu.make_async_copy(ref, table.at[pl.ds(i * half, half)], sems.at[i])
-        for i, ref in enumerate((near, far))
-    ]
-    for copy in copies:
-        copy.start()
+def table_rows(n_bt, n_freq, me, stations, slot_time):
+    n_z = n_freq // 2
+    my_z, my_core = me[0] >> 1, me[0] & 1
+
+    def rows(which, s):
+        station, t = stations[which, s], slot_time[s]
+        bt, freq = lax.div(station, n_freq), lax.rem(station, n_freq)
+        z, core = freq >> 1, freq & 1
+        half = jnp.where(core == my_core, 0, n_bt * n_z)
+        ahead = lax.rem(z - my_z + n_z, n_z)
+        return (half + ahead * n_bt + bt) * TSLOTS + t, (half + bt * n_z + z) * TSLOTS + t
+
+    return rows
+
+
+def join_parts(parts, whole, sems, chunk):
+    copies = []
+    for p, part in enumerate(parts):
+        for c in range(0, part.shape[0], chunk):
+            at = pl.ds(p * part.shape[0] + c, chunk)
+            k = len(copies)
+            copy = pltpu.make_async_copy(part.at[pl.ds(c, chunk)], whole.at[at], sems.at[k])
+            copy.start()
+            copies.append(copy)
     return copies
 
 
@@ -388,16 +401,19 @@
 
 
 def patch_kernel(
-    group, slot, first, second, image, near, far, backward, right, spread_a, spread_b,
-    out, table, sems,
+    group, n_bt, n_freq, me, slot, stations, slot_time, image_a, image_b, near, far,
+    backward, right, spread_a, spread_b, out, table, sems, image, image_sems, stage, out_sems,
 ):
-    for copy in join_halves(near, far, table, sems):
+    copies = join_parts((near, far), table, sems, near.shape[0])
+    images = join_parts((image_a, image_b), image, image_sems, image_a.shape[0] // 2)
+    rows = table_rows(n_bt, n_freq, me, stations, slot_time)
+    for copy in copies:
         copy.wait()
 
     def step(g, carry):
         subs = [g * group + k for k in range(group)]
-        first_screens = screens_of(table, [first[s] for s in subs], spread_a)
-        second_screens = screens_of(table, [second[s] for s in subs], spread_b)
+        first_screens = screens_of(table, [rows(0, s)[0] for s in subs], spread_a)
+        second_screens = screens_of(table, [rows(1, s)[0] for s in subs], spread_b)
         backs = []
         for s, (a_re, a_im), (b_re, b_im) in zip(subs, first_screens, second_screens):
             m_re, m_im = image[s, 0:PIX], image[s, PIX:]
@@ -413,37 +429,59 @@
             grad_im = im[:, :LANES] - re[:, LANES:]
             grads.append(jnp.concatenate([grad_re, grad_im], 0).astype(BF16))
         for s, grad in zip(subs, grads):
-            out[slot[s]] = grad
-        return carry
-
-    lax.fori_loop(0, image.shape[0] // group, step, 0)
-
-
-def table_scratch(near):
+            stage[s] = grad
+        for s in subs:
+            pltpu.make_async_copy(stage.at[s], out.at[slot[s]], out_sems.at[s]).start()
+        return carry
+
+    count, ready = image.shape[0], image.shape[0] // len(images)
+    for p, copy in enumerate(images):
+        copy.wait()
+        lax.fori_loop(p * ready // group, (p + 1) * ready // group, step, 0)
+
+    def finished(s, carry):
+        pltpu.make_async_copy(stage.at[s], out.at[slot[s]], out_sems.at[s]).wait()
+        return carry
+
+    lax.fori_loop(0, count, finished, 0)
+
+
+def table_scratch(near, image):
     whole = (2 * near.shape[0],) + near.shape[1:]
-    return [pltpu.VMEM(whole, BF16), pltpu.SemaphoreType.DMA((2,))]
-
-
-def patch_gradients(slot, first, second, image, near, far, consts, slots):
+    images = (2 * image.shape[0],) + image.shape[1:]
+    return [
+        pltpu.VMEM(whole, BF16),
+        pltpu.SemaphoreType.DMA((2,)),
+        pltpu.VMEM(images, F32),
+        pltpu.SemaphoreType.DMA((4,)),
+    ]
+
+
+def patch_gradients(where, images, near, far, consts, slots, n_bt, n_freq):
     _, backward, right, spread_a, spread_b = consts
-    group = math.gcd(image.shape[0], 4)
+    count = 2 * images[0].shape[0]
+    group = math.gcd(count // 4, 4)
     vmem, smem = pl.BlockSpec(memory_space=pltpu.VMEM), pl.BlockSpec(memory_space=pltpu.SMEM)
     return pl.pallas_call(
-        lambda *refs: patch_kernel(group, *refs),
+        lambda *refs: patch_kernel(group, n_bt, n_freq, *refs),
         out_shape=jax.ShapeDtypeStruct((slots, 2 * PIX, LANES), BF16),
-        in_specs=[smem] * 3 + [vmem] + [pl.BlockSpec(memory_space=pl.ANY)] * 2 + [vmem] * 4,
-        out_specs=vmem,
-        scratch_shapes=table_scratch(near),
+        in_specs=[smem] * 4 + [pl.BlockSpec(memory_space=pl.ANY)] * 4 + [vmem] * 4,
+        out_specs=pl.BlockSpec(memory_space=pl.ANY),
+        scratch_shapes=table_scratch(near, images[0])
+        + [pltpu.VMEM((count, 2 * PIX, LANES), BF16), pltpu.SemaphoreType.DMA((count,))],
         name="patch",
-    )(slot, first, second, image, near, far, backward, right, spread_a, spread_b)
+    )(*where, *images, near, far, backward, right, spread_a, spread_b)
 
 
 def screen_kernel(
-    group, slot, first, second, first_sum, second_sum, image, patches, near, far,
-    forward, right, spread_a, spread_b, out_near, out_far, table, sems, acc,
+    group, n_bt, n_freq, me, slot, stations, slot_time, image_a, image_b, near, far,
+    patches, forward, right, spread_a, spread_b, out_near, out_far,
+    table, sems, image, image_sems, acc,
 ):
     chunk = 32
-    copies = join_halves(near, far, table, sems)
+    copies = join_parts((near, far), table, sems, near.shape[0])
+    copies += join_parts((image_a, image_b), image, image_sems, image_a.shape[0] // 2)
+    rows = table_rows(n_bt, n_freq, me, stations, slot_time)
 
     def clear(i, carry):
         acc[pl.ds(i * chunk, chunk)] = jnp.zeros((chunk, PIX, LANES), F32)
@@ -457,8 +495,9 @@
     def step(g, carry):
         terms = []
         subs = [g * group + k for k in range(group)]
-        first_screens = screens_of(table, [first[s] for s in subs], spread_a)
-        second_screens = screens_of(table, [second[s] for s in subs], spread_b)
+        first_rows, second_rows = [[rows(w, s) for s in subs] for w in (0, 1)]
+        first_screens = screens_of(table, [row for row, _ in first_rows], spread_a)
+        second_screens = screens_of(table, [row for row, _ in second_rows], spread_b)
         skies = transforms(forward, [patches[slot[s]] for s in subs], right)
         for s, (a_re, a_im), (b_re, b_im), sky in zip(subs, first_screens, second_screens, skies):
             m_re, m_im = image[s, 0:PIX], image[s, PIX:]
@@ -488,10 +527,10 @@
                 gb_re + pltpu.roll(gb_re, 2 * PIX, 1),
                 gb_im + pltpu.roll(gb_im, 2 * PIX, 1),
             )
-            terms.append((s, ta, tb))
-        for s, ta, tb in terms:
-            acc[first_sum[s]] = acc[first_sum[s]] + ta
-            acc[second_sum[s]] = acc[second_sum[s]] + tb
+            terms.append((ta, tb))
+        for (ta, tb), (_, first), (_, second) in zip(terms, first_rows, second_rows):
+            acc[first] = acc[first] + ta
+            acc[second] = acc[second] + tb
         return carry
 
     lax.fori_loop(0, image.shape[0] // group, step, 0)
@@ -505,19 +544,19 @@
         lax.fori_loop(0, out.shape[0] // chunk, give, 0)
 
 
-def screen_gradients(slot, rows, image, patches, near, far, consts):
+def screen_gradients(where, images, patches, near, far, consts, n_bt, n_freq):
     forward, _, right, spread_a, spread_b = consts
-    group = math.gcd(image.shape[0], 4)
+    group = math.gcd(images[0].shape[0], 4)
     vmem, smem = pl.BlockSpec(memory_space=pltpu.VMEM), pl.BlockSpec(memory_space=pltpu.SMEM)
-    scratch = table_scratch(near)
+    scratch = table_scratch(near, images[0])
     return pl.pallas_call(
-        lambda *refs: screen_kernel(group, *refs),
+        lambda *refs: screen_kernel(group, n_bt, n_freq, *refs),
         out_shape=(jax.ShapeDtypeStruct(near.shape, BF16),) * 2,
-        in_specs=[smem] * 5 + [vmem] * 2 + [pl.BlockSpec(memory_space=pl.ANY)] * 2 + [vmem] * 4,
+        in_specs=[smem] * 4 + [pl.BlockSpec(memory_space=pl.ANY)] * 4 + [vmem] * 5,
         out_specs=(vmem,) * 2,
         scratch_shapes=scratch + [pltpu.VMEM(scratch[0].shape, F32)],
         name="screen",
-    )(slot, *rows, image, patches, near, far, forward, right, spread_a, spread_b)
+    )(*where, *images, near, far, patches, forward, right, spread_a, spread_b)
 
 
 def exchange(x, axis, groups=None):
@@ -551,30 +590,26 @@
     swap = [(f, f ^ 1) for f in range(n_freq)]
     same_core = [[2 * z + c for z in range(n_z)] for c in range(2)]
     row = TSLOTS * PIX
-    mail, slot, first, second, first_sum, second_sum = make_mail(
-        lax.axis_index("freq").astype(jnp.int32).reshape(1),
-        owner_tile[0, :, 0],
-        row_offset[0],
-        column[0],
-        stations[0].T,
-        time_slot[0],
-        screens[:, 0],
-        n_bt,
-        n_freq,
+    mail, slot = make_mail(
+        owner_tile[0, :, 0], row_offset[0], column[0], screens[:, 0], n_bt
     )
-    image = adjoint_images(residual[0], uv_coords[0])
-    mail, image = lax.optimization_barrier((exchange(mail, "bt"), image))
+    me = lax.axis_index("freq").astype(jnp.int32).reshape(1)
+    where = (me, slot, stations[0].T, time_slot[0])
+    image_a = adjoint_images(residual[0], uv_coords[0], 0, 2)
+    image_b = adjoint_images(residual[0], uv_coords[0], 1, 2)
+    images = (image_a, image_b)
+    mail = exchange(mail, "bt")
     asked = mail[:, row].astype(jnp.int32)
     near = ring_gather(mail[:, :row], n_z).reshape(n_z * n_bt * TSLOTS, PIX, LANES)
     far = lax.ppermute(near, "freq", swap)
     cut = cut_windows(asked, uv_grid[0])
     fetched = exchange(cut.reshape(n_bt, CAP, 2 * PIX, LANES), "bt")
     fetched = fetched.reshape(slots, 2 * PIX, LANES)
-    grads = patch_gradients(slot, first, second, image, near, far, consts, slots)
+    grads = patch_gradients(where, images, near, far, consts, slots, n_bt, n_freq)
     returned = exchange(grads.reshape(n_bt, CAP, 2 * PIX, LANES), "bt")
     returned = returned.reshape(slots, 2 * PIX, LANES)
     terms, sent = screen_gradients(
-        slot, (first, second, first_sum, second_sum), image, fetched, near, far, consts
+        where, images, fetched, near, far, consts, n_bt, n_freq
     )
     came = lax.ppermute(sent, "freq", swap)
     part = (terms.astype(F32) + came.astype(F32)).astype(BF16)

time: 229 us -> 222 us (0.969)
  blocking collectives: 32 us -> 12.5 us
  waiting for transfers between devices: 70.9 us -> 87.8 us
  Pallas kernels: 78.5 us -> 73.6 us
    all_to_all x1, blocking collectives: 32 us -> 12.5 us  [exchange(): lax.all_to_all(x, axis, split_axis=0, concat_axis=0, tiled=True, axis_ind...]
    all_to_all x4, waiting for transfers between devices: 44 us -> 61.5 us  [exchange(): lax.all_to_all(x, axis, split_axis=0, concat_axis=0, tiled=True, axis_ind...]
    pallas_call x3, Pallas kernels: 34.3 us -> 30.8 us  [the longest x1 15.6 us: screen_gradients(): pl.pallas_call(lambda *refs: screen_kernel(group, n_bt, n_freq, *refs), o...]
    pallas_call x1 -> x2, Pallas kernels: 11.5 us -> 13 us  [adjoint_images(): pl.pallas_call(lambda *refs: image_kernel(group, *refs), out_shape=jax.Sh...]
  transfers between devices with their start and end apart: 13 -> 13, of which waited for: 9 -> 10; matrix products, arithmetic and copies ran while one was open for 1% -> 1% of each run, Pallas kernels for 24% -> 24%
where the time goes in v4:
time: 222 us; the launch traced here: 221 us
  waiting for transfers between devices  87.8 us (40%)
  Pallas kernels  73.6 us (33%)
  starting transfers between devices  39.9 us (18%)
  blocking collectives  12.5 us (6%)
  other arithmetic  5.32 us (2%)
    all_to_all x4, waiting for transfers between devices, exchange(): lax.all_to_all(x, axis, split_axis=0, concat_axis=0, tiled=True, axis_ind...  61.5 us
    all_to_all x4, starting transfers between devices, exchange(): lax.all_to_all(x, axis, split_axis=0, concat_axis=0, tiled=True, axis_ind...  30.7 us
    ppermute x4, waiting for transfers between devices, ring_gather(): up = lax.ppermute(up, 'freq', by(1))  20.9 us
    pallas_call x1, Pallas kernels, screen_gradients(): pl.pallas_call(lambda *refs: screen_kernel(group, n_bt, n_freq, *refs), o...  15.6 us
    pallas_call x1, Pallas kernels, add_windows(): pl.pallas_call(add_kernel, out_shape=jax.ShapeDtypeStruct((comps, rows, c...  14.3 us
    pallas_call x1, Pallas kernels, cut_windows(): pl.pallas_call(cut_kernel, out_shape=jax.ShapeDtypeStruct((slots, 2 * PIX...  13.8 us
    pallas_call x2, Pallas kernels, adjoint_images(): pl.pallas_call(lambda *refs: image_kernel(group, *refs), out_shape=jax.Sh...  13 us
    pallas_call x1, Pallas kernels, patch_gradients(): pl.pallas_call(lambda *refs: patch_kernel(group, n_bt, n_freq, *refs), ou...  12.9 us
  transfers between devices with their start and end apart: 13, of which 10 were waited for; matrix products, arithmetic and copies ran while one was open for 1% of the time, Pallas kernels for 24%

profile of v4, /device:TPU:54, one launch (start us, length us, event | category | flops | bytes accessed | tf_op | source)
XLA Modules:
  0.0 220.9 jit_solution(7642610530432467914)
XLA Ops:
  0.6 2.4 %mail.1 = (bf16[16,80,128]{2,1,0:T(8,128)(2,1)}, s32[64]{0:T(128)}) custom-call(s32[64]{0:T(128)} %bitcast.60, s32[64]{0:T(128)} %bitcast.61, s32[64]{0:T(128)} %bitcast.62, bf16[2,4,1024]{2,1,0:T(4,128)(2,1)} %bitcast.55), custom_call_target="tpu_custom_call" | custom-call | tf_op jit(solution)/shard_map/mail/pallas_call | solution.py:106
  3.0 12.5 %all_to_all.25 = bf16[16,80,128]{2,1,0:T(8,128)(2,1)S(1)} all-to-all(bf16[16,80,128]{2,1,0:T(8,128)(2,1)} %get-tuple-element.6), channel_id=1, replica_groups=mesh['bt'=16,'freq'=16] {'bt'}, dimensions={0} | all-to-all | bytes 655360 | tf_op jit(solution)/shard_map/all_to_all | solution.py:563
  15.5 2.0 collective-permute-start.3
  17.5 0.1 collective-permute-start
  17.6 4.9 %collective-permute-done.3 = bf16[16,64,128]{2,1,0:T(8,128)(2,1)S(1)} collective-permute-done((bf16[16,64,128]{2,1,0:T(8,128)(2,1)S(1)}, bf16[16,64,128]{2,1,0:T(8,128)(2,1)S(1)}, u32[]{:S(2)}, u32[]{:S(2)}) %collective-permute-start.3) | collective-permute-done | bytes 262176 | tf_op jit(solution)/shard_map/ppermute | solution.py:575
  22.5 1.9 collective-permute-start.4
  24.5 2.3 %collective-permute-start.1 = (bf16[16,64,128]{2,1,0:T(8,128)(2,1)S(1)}, bf16[16,64,128]{2,1,0:T(8,128)(2,1)S(1)}, u32[]{:S(2)}, u32[]{:S(2)}) collective-permute-start(bf16[16,64,128]{2,1,0:T(8,128)(2,1)S(1)} %collective-permute-done), channel_id=1, source_target_pairs={{0,14},{1,15},{2,0},{3,1},{4,2},{5,3},{6,4},{7,5},{8,6},{9,7},{10,... | collective-permute-start | bytes 786440 | tf_op jit(solution)/shard_map/ppermute | solution.py:578
  26.8 4.6 %collective-permute-done.4 = bf16[16,64,128]{2,1,0:T(8,128)(2,1)S(1)} collective-permute-done((bf16[16,64,128]{2,1,0:T(8,128)(2,1)S(1)}, bf16[16,64,128]{2,1,0:T(8,128)(2,1)S(1)}, u32[]{:S(2)}, u32[]{:S(2)}) %collective-permute-start.4) | collective-permute-done | bytes 262176 | tf_op jit(solution)/shard_map/ppermute | solution.py:575
  31.4 0.4 collective-permute-done.1
  31.8 2.7 %collective-permute-start.2 = (bf16[16,64,128]{2,1,0:T(8,128)(2,1)S(1)}, bf16[16,64,128]{2,1,0:T(8,128)(2,1)S(1)}, u32[]{:S(2)}, u32[]{:S(2)}) collective-permute-start(bf16[16,64,128]{2,1,0:T(8,128)(2,1)S(1)} %collective-permute-done.1), channel_id=1, source_target_pairs={{0,14},{1,15},{2,0},{3,1},{4,2},{5,3},{6,4},{7,5},{8,6},{9,7},{10,... | collective-permute-start | bytes 786440 | tf_op jit(solution)/shard_map/ppermute | solution.py:578
  34.5 4.3 %collective-permute-done.5 = bf16[16,64,128]{2,1,0:T(8,128)(2,1)S(1)} collective-permute-done((bf16[16,64,128]{2,1,0:T(8,128)(2,1)S(1)}, bf16[16,64,128]{2,1,0:T(8,128)(2,1)S(1)}, u32[]{:S(2)}, u32[]{:S(2)}) %collective-permute-start.5) | collective-permute-done | bytes 262176 | tf_op jit(solution)/shard_map/ppermute | solution.py:575
  38.9 0.5 collective-permute-done.2
  39.4 7.2 %collective-permute-done.6 = bf16[16,64,128]{2,1,0:T(8,128)(2,1)S(1)} collective-permute-done((bf16[16,64,128]{2,1,0:T(8,128)(2,1)S(1)}, bf16[16,64,128]{2,1,0:T(8,128)(2,1)S(1)}, u32[]{:S(2)}, u32[]{:S(2)}) %collective-permute-start.6) | collective-permute-done | bytes 262176 | tf_op jit(solution)/shard_map/ppermute | solution.py:575
  46.9 0.8 fusion.asked
  47.7 13.8 %cut.1 = bf16[128,64,128]{2,1,0:T(8,128)(2,1)} custom-call(s32[16,128]{1,0:T(8,128)} %fusion.asked, bf16[8,64,1024]{2,1,0:T(8,128)(2,1)} %bitcast.49), custom_call_target="tpu_custom_call" | custom-call | tf_op jit(solution)/shard_map/cut/pallas_call | solution.py:227
  61.4 6.9 %all-to-all-start.2 = ((bf16[16,8,64,128]{3,2,1,0:T(8,128)(2,1)}), bf16[16,8,64,128]{3,2,1,0:T(8,128)(2,1)}, u32[]{:S(2)}, u32[]{:S(2)}) async-start(bf16[16,8,64,128]{3,2,1,0:T(8,128)(2,1)} %bitcast.47), calls=%async_computation.2 | async-start | bytes 4194304 | tf_op jit(solution)/shard_map/all_to_all | solution.py:563
  68.4 6.6 %image.2.refs_4_ = f32[32,64,128]{2,1,0:T(8,128)} custom-call(bf16[64,8,256]{2,1,0:T(8,128)(2,1)} %bitcast.50, f32[64,2,256]{2,1,0:T(2,128)} %bitcast.52), custom_call_target="tpu_custom_call" | custom-call | tf_op jit(solution)/shard_map/image/pallas_call | solution.py:353
  74.9 6.5 %image.3.refs_5_ = f32[32,64,128]{2,1,0:T(8,128)} custom-call(bf16[64,8,256]{2,1,0:T(8,128)(2,1)} %bitcast.51, f32[64,2,256]{2,1,0:T(2,128)} %bitcast.53), custom_call_target="tpu_custom_call" | custom-call | tf_op jit(solution)/shard_map/image/pallas_call | solution.py:353
  81.4 17.3 %all-to-all-done.2 = bf16[16,8,64,128]{3,2,1,0:T(8,128)(2,1)} async-done(((bf16[16,8,64,128]{3,2,1,0:T(8,128)(2,1)}), bf16[16,8,64,128]{3,2,1,0:T(8,128)(2,1)}, u32[]{:S(2)}, u32[]{:S(2)}) %all-to-all-start.2) | async-done | bytes 2097184 | tf_op jit(solution)/shard_map/all_to_all | solution.py:563
  98.7 15.6 %screen.1 = (bf16[256,32,128]{2,1,0:T(8,128)(2,1)}, bf16[256,32,128]{2,1,0:T(8,128)(2,1)}) custom-call(s32[1]{0:T(128)} %bitcast.5.refs_0_, s32[64]{0:T(128)} %get-tuple-element.7.refs_1_, s32[2,64]{1,0:T(2,128)} %bitcast.56, s32[64]{0:T(128)} %bitcast.58, f32[32,64,128]{2,1,0:T(8,128)} %image.2.refs_4_, f32[32,64,128]{2,1,0:T(8,128)} %image.3.refs_5_, ...), custom_call_target="tpu_custom_call" | custom-call | tf_op jit(solution)/shard_map/screen/pallas_call | solution.py:552
  114.4 4.4 %collective-permute-done.8 = bf16[256,32,128]{2,1,0:T(8,128)(2,1)S(1)} collective-permute-done((bf16[256,32,128]{2,1,0:T(8,128)(2,1)}, bf16[256,32,128]{2,1,0:T(8,128)(2,1)S(1)}, u32[]{:S(2)}, u32[]{:S(2)}) %collective-permute-start.8) | collective-permute-done | bytes 2097184 | tf_op jit(solution)/shard_map/ppermute | solution.py:614
  118.8 3.5 %add_convert_fusion = bf16[256,32,128]{2,1,0:T(8,128)(2,1)} fusion(bf16[256,32,128]{2,1,0:T(8,128)(2,1)S(1)} %collective-permute-done.8, bf16[256,32,128]{2,1,0:T(8,128)(2,1)} %get-tuple-element.8), kind=kLoop, calls=%fused_computation | loop fusion | flops 4194304 | bytes 6291456 | tf_op jit(solution)/shard_map/convert_element_type | solution.py:615
  122.3 7.0 %all-to-all-start.3 = ((bf16[16,8,2,32,128]{4,3,2,1,0:T(8,128)(2,1)}), bf16[16,8,2,32,128]{4,3,2,1,0:T(8,128)(2,1)S(1)}, u32[]{:S(2)}, u32[]{:S(2)}) async-start(bf16[16,8,2,32,128]{4,3,2,1,0:T(8,128)(2,1)} %bitcast.28), calls=%async_computation.3 | async-start | bytes 4194304 | tf_op jit(solution)/shard_map/all_to_all | solution.py:563
  129.3 12.9 %patch.1 = bf16[128,64,128]{2,1,0:T(8,128)(2,1)} custom-call(s32[1]{0:T(128)} %bitcast.5.refs_0_, s32[64]{0:T(128)} %get-tuple-element.7.refs_1_, s32[2,64]{1,0:T(2,128)} %bitcast.57, s32[64]{0:T(128)} %bitcast.59, f32[32,64,128]{2,1,0:T(8,128)} %image.2.refs_4_, f32[32,64,128]{2,1,0:T(8,128)} %image.3.refs_5_, bf16[256,32,128]{2,1,0:T(8,128)(2,1)} %bitcast.45, ...), custom_call_target="tpu_custom_call" | custom-call | tf_op jit(solution)/shard_map/patch/pallas_call | solution.py:465
  142.1 17.8 %all-to-all-done.3 = bf16[16,8,2,32,128]{4,3,2,1,0:T(8,128)(2,1)S(1)} async-done(((bf16[16,8,2,32,128]{4,3,2,1,0:T(8,128)(2,1)}), bf16[16,8,2,32,128]{4,3,2,1,0:T(8,128)(2,1)S(1)}, u32[]{:S(2)}, u32[]{:S(2)}) %all-to-all-start.3) | async-done | bytes 2097184 | tf_op jit(solution)/shard_map/all_to_all | solution.py:563
  159.9 7.6 %all-to-all-start.1 = ((bf16[16,8,64,128]{3,2,1,0:T(8,128)(2,1)}), bf16[16,8,64,128]{3,2,1,0:T(8,128)(2,1)}, u32[]{:S(2)}, u32[]{:S(2)}) async-start(bf16[16,8,64,128]{3,2,1,0:T(8,128)(2,1)} %bitcast.46), calls=%async_computation.1 | async-start | bytes 4194304 | tf_op jit(solution)/shard_map/all_to_all | solution.py:563
  167.5 1.1 reduce_sum.12
  168.6 26.5 %all-to-all-done.1 = bf16[16,8,64,128]{3,2,1,0:T(8,128)(2,1)} async-done(((bf16[16,8,64,128]{3,2,1,0:T(8,128)(2,1)}), bf16[16,8,64,128]{3,2,1,0:T(8,128)(2,1)}, u32[]{:S(2)}, u32[]{:S(2)}) %all-to-all-start.1) | async-done | bytes 2097184 | tf_op jit(solution)/shard_map/all_to_all | solution.py:563
  195.1 9.2 %all-to-all-start.4 = ((bf16[8,2,32,128]{3,2,1,0:T(8,128)(2,1)}), bf16[8,2,32,128]{3,2,1,0:T(8,128)(2,1)S(1)}, u32[]{:S(2)}, u32[]{:S(2)}) async-start(bf16[8,2,32,128]{3,2,1,0:T(8,128)(2,1)} %reduce_sum.12), calls=%async_computation.4 | async-start | bytes 262144 | tf_op jit(solution)/shard_map/all_to_all | solution.py:563
  204.2 14.3 %add.6 = f32[8,64,1024]{2,1,0:T(8,128)} custom-call(s32[16,128]{1,0:T(8,128)} %fusion.asked, bf16[128,64,128]{2,1,0:T(8,128)(2,1)} %bitcast.21.pieces), custom_call_target="tpu_custom_call" | custom-call | tf_op jit(solution)/shard_map/add/pallas_call | solution.py:286
  218.5 0.7 copy-done.1
  219.2 1.7 finish.1
  (20 shorter events, 0.6 us)
Async XLA Ops:
  15.5 7.0 %collective-permute-start.3 = (bf16[16,64,128]{2,1,0:T(8,128)(2,1)S(1)}, bf16[16,64,128]{2,1,0:T(8,128)(2,1)S(1)}, u32[]{:S(2)}, u32[]{:S(2)}) collective-permute-start(bf16[16,64,128]{2,1,0:T(8,128)(2,1)S(1)} %slice.9), channel_id=1, source_target_pairs={{0,2},{1,3},{2,4},{3,5},{4,6},{5,7},{6,8},{7,9},{8,10},{9,11},{10,... | collective-permute-start | bytes 786440 | tf_op jit(solution)/shard_map/ppermute | solution.py:575
  17.5 6.9 %collective-permute-start = (bf16[16,64,128]{2,1,0:T(8,128)(2,1)S(1)}, bf16[16,64,128]{2,1,0:T(8,128)(2,1)S(1)}, u32[]{:S(2)}, u32[]{:S(2)}) collective-permute-start(bf16[16,64,128]{2,1,0:T(8,128)(2,1)S(1)} %slice.9), channel_id=1, source_target_pairs={{0,14},{1,15},{2,0},{3,1},{4,2},{5,3},{6,4},{7,5},{8,6},{9,7},{10,... | collective-permute-start | bytes 786440 | tf_op jit(solution)/shard_map/ppermute | solution.py:578
  22.5 8.8 %collective-permute-start.4 = (bf16[16,64,128]{2,1,0:T(8,128)(2,1)S(1)}, bf16[16,64,128]{2,1,0:T(8,128)(2,1)S(1)}, u32[]{:S(2)}, u32[]{:S(2)}) collective-permute-start(bf16[16,64,128]{2,1,0:T(8,128)(2,1)S(1)} %collective-permute-done.3), channel_id=1, source_target_pairs={{0,2},{1,3},{2,4},{3,5},{4,6},{5,7},{6,8},{7,9},{8,10},{9,11},{10,... | collective-permute-start | bytes 786440 | tf_op jit(solution)/shard_map/ppermute | solution.py:575
  24.5 7.4 %collective-permute-start.1 = (bf16[16,64,128]{2,1,0:T(8,128)(2,1)S(1)}, bf16[16,64,128]{2,1,0:T(8,128)(2,1)S(1)}, u32[]{:S(2)}, u32[]{:S(2)}) collective-permute-start(bf16[16,64,128]{2,1,0:T(8,128)(2,1)S(1)} %collective-permute-done), channel_id=1, source_target_pairs={{0,14},{1,15},{2,0},{3,1},{4,2},{5,3},{6,4},{7,5},{8,6},{9,7},{10,... | collective-permute-start | bytes 786440 | tf_op jit(solution)/shard_map/ppermute | solution.py:578
  31.3 7.4 %collective-permute-start.5 = (bf16[16,64,128]{2,1,0:T(8,128)(2,1)S(1)}, bf16[16,64,128]{2,1,0:T(8,128)(2,1)S(1)}, u32[]{:S(2)}, u32[]{:S(2)}) collective-permute-start(bf16[16,64,128]{2,1,0:T(8,128)(2,1)S(1)} %collective-permute-done.4), channel_id=1, source_target_pairs={{0,2},{1,3},{2,4},{3,5},{4,6},{5,7},{6,8},{7,9},{8,10},{9,11},{10,... | collective-permute-start | bytes 786440 | tf_op jit(solution)/shard_map/ppermute | solution.py:575
  31.8 7.6 %collective-permute-start.2 = (bf16[16,64,128]{2,1,0:T(8,128)(2,1)S(1)}, bf16[16,64,128]{2,1,0:T(8,128)(2,1)S(1)}, u32[]{:S(2)}, u32[]{:S(2)}) collective-permute-start(bf16[16,64,128]{2,1,0:T(8,128)(2,1)S(1)} %collective-permute-done.1), channel_id=1, source_target_pairs={{0,14},{1,15},{2,0},{3,1},{4,2},{5,3},{6,4},{7,5},{8,6},{9,7},{10,... | collective-permute-start | bytes 786440 | tf_op jit(solution)/shard_map/ppermute | solution.py:578
  38.8 7.9 %collective-permute-start.6 = (bf16[16,64,128]{2,1,0:T(8,128)(2,1)S(1)}, bf16[16,64,128]{2,1,0:T(8,128)(2,1)S(1)}, u32[]{:S(2)}, u32[]{:S(2)}) collective-permute-start(bf16[16,64,128]{2,1,0:T(8,128)(2,1)S(1)} %collective-permute-done.5), channel_id=1, source_target_pairs={{0,2},{1,3},{2,4},{3,5},{4,6},{5,7},{6,8},{7,9},{8,10},{9,11},{10,... | collective-permute-start | bytes 786440 | tf_op jit(solution)/shard_map/ppermute | solution.py:575
  46.8 14.6 %copy-start = (bf16[8,16,64,128]{3,2,1,0:T(8,128)(2,1)}, bf16[8,16,64,128]{3,2,1,0:T(8,128)(2,1)S(1)}, u32[]{:S(2)}) copy-start(bf16[8,16,64,128]{3,2,1,0:T(8,128)(2,1)S(1)} %bitcast_dynamic-update-slice_fusion) | copy-start | bytes 6291460
  46.8 51.9 %collective-permute-start.7 = (bf16[256,32,128]{2,1,0:T(8,128)(2,1)S(1)}, bf16[256,32,128]{2,1,0:T(8,128)(2,1)}, u32[]{:S(2)}, u32[]{:S(2)}) collective-permute-start(bf16[256,32,128]{2,1,0:T(8,128)(2,1)S(1)} %bitcast.43), channel_id=1, source_target_pairs={{0,1},{1,0},{2,3},{3,2},{4,5},{5,4},{6,7},{7,6},{8,9},{9,8},{10,11... | collective-permute-start | bytes 6291464 | tf_op jit(solution)/shard_map/ppermute | solution.py:604
  61.4 37.3 %all-to-all-start.2 = ((bf16[16,8,64,128]{3,2,1,0:T(8,128)(2,1)}), bf16[16,8,64,128]{3,2,1,0:T(8,128)(2,1)}, u32[]{:S(2)}, u32[]{:S(2)}) async-start(bf16[16,8,64,128]{3,2,1,0:T(8,128)(2,1)} %bitcast.47), calls=%async_computation.2 | async-start | bytes 4194304 | tf_op jit(solution)/shard_map/all_to_all | solution.py:563
  114.3 4.5 %collective-permute-start.8 = (bf16[256,32,128]{2,1,0:T(8,128)(2,1)}, bf16[256,32,128]{2,1,0:T(8,128)(2,1)S(1)}, u32[]{:S(2)}, u32[]{:S(2)}) collective-permute-start(bf16[256,32,128]{2,1,0:T(8,128)(2,1)} %get-tuple-element.9), channel_id=1, source_target_pairs={{0,1},{1,0},{2,3},{3,2},{4,5},{5,4},{6,7},{7,6},{8,9},{9,8},{10,11... | collective-permute-start | bytes 6291464 | tf_op jit(solution)/shard_map/ppermute | solution.py:614
  122.3 37.7 %all-to-all-start.3 = ((bf16[16,8,2,32,128]{4,3,2,1,0:T(8,128)(2,1)}), bf16[16,8,2,32,128]{4,3,2,1,0:T(8,128)(2,1)S(1)}, u32[]{:S(2)}, u32[]{:S(2)}) async-start(bf16[16,8,2,32,128]{4,3,2,1,0:T(8,128)(2,1)} %bitcast.28), calls=%async_computation.3 | async-start | bytes 4194304 | tf_op jit(solution)/shard_map/all_to_all | solution.py:563
  159.9 35.1 %all-to-all-start.1 = ((bf16[16,8,64,128]{3,2,1,0:T(8,128)(2,1)}), bf16[16,8,64,128]{3,2,1,0:T(8,128)(2,1)}, u32[]{:S(2)}, u32[]{:S(2)}) async-start(bf16[16,8,64,128]{3,2,1,0:T(8,128)(2,1)} %bitcast.46), calls=%async_computation.1 | async-start | bytes 4194304 | tf_op jit(solution)/shard_map/all_to_all | solution.py:563
  195.1 23.4 %all-to-all-start.4 = ((bf16[8,2,32,128]{3,2,1,0:T(8,128)(2,1)}), bf16[8,2,32,128]{3,2,1,0:T(8,128)(2,1)S(1)}, u32[]{:S(2)}, u32[]{:S(2)}) async-start(bf16[8,2,32,128]{3,2,1,0:T(8,128)(2,1)} %reduce_sum.12), calls=%async_computation.4 | async-start | bytes 262144 | tf_op jit(solution)/shard_map/all_to_all | solution.py:563
  218.5 0.7 copy-start.1

commit v5 on v4

--- a/solution.py
+++ b/solution.py
@@ -364,15 +364,14 @@
     n_z = n_freq // 2
     my_z, my_core = me[0] >> 1, me[0] & 1
 
-    def rows(which, s):
-        station, t = stations[which, s], slot_time[s]
+    def row(which, s):
+        station = stations[which, s]
         bt, freq = lax.div(station, n_freq), lax.rem(station, n_freq)
-        z, core = freq >> 1, freq & 1
-        half = jnp.where(core == my_core, 0, n_bt * n_z)
-        ahead = lax.rem(z - my_z + n_z, n_z)
-        return (half + ahead * n_bt + bt) * TSLOTS + t, (half + bt * n_z + z) * TSLOTS + t
-
-    return rows
+        half = jnp.where((freq & 1) == my_core, 0, n_bt * n_z)
+        ahead = lax.rem((freq >> 1) - my_z + n_z, n_z)
+        return (half + ahead * n_bt + bt) * TSLOTS + slot_time[s]
+
+    return row
 
 
 def join_parts(parts, whole, sems, chunk):
@@ -393,51 +392,69 @@
     return [(wide[k, :LANES], wide[k, LANES:]) for k in at]
 
 
-def transforms(left, pieces, right):
-    inner = dot(left[...], jnp.concatenate(pieces, 1)).astype(BF16)
-    lines = [inner[:, k * LANES : (k + 1) * LANES] for k in range(len(pieces))]
-    outer = dot(jnp.concatenate(lines, 0), right[...])
-    return [outer[k * 2 * PIX : (k + 1) * 2 * PIX] for k in range(len(pieces))]
+def left_side(left, pieces):
+    count = pieces.shape[1] // LANES
+    inner = dot(left[...], pieces).astype(BF16)
+    return jnp.concatenate([inner[:, k * LANES : (k + 1) * LANES] for k in range(count)], 0)
+
+
+def right_side(lines, right):
+    outer = dot(lines, right[...])
+    return [outer[k : k + 2 * PIX] for k in range(0, lines.shape[0], 2 * PIX)]
 
 
 def patch_kernel(
     group, n_bt, n_freq, me, slot, stations, slot_time, image_a, image_b, near, far,
     backward, right, spread_a, spread_b, out, table, sems, image, image_sems, stage, out_sems,
+    backs, lows,
 ):
     copies = join_parts((near, far), table, sems, near.shape[0])
     images = join_parts((image_a, image_b), image, image_sems, image_a.shape[0] // 2)
-    rows = table_rows(n_bt, n_freq, me, stations, slot_time)
-    for copy in copies:
+    row = table_rows(n_bt, n_freq, me, stations, slot_time)
+    for copy in copies + images[:1]:
         copy.wait()
-
-    def step(g, carry):
+    groups = image.shape[0] // group
+
+    def back_side(g):
         subs = [g * group + k for k in range(group)]
-        first_screens = screens_of(table, [rows(0, s)[0] for s in subs], spread_a)
-        second_screens = screens_of(table, [rows(1, s)[0] for s in subs], spread_b)
-        backs = []
+        first_screens = screens_of(table, [row(0, s) for s in subs], spread_a)
+        second_screens = screens_of(table, [row(1, s) for s in subs], spread_b)
+        pieces = []
         for s, (a_re, a_im), (b_re, b_im) in zip(subs, first_screens, second_screens):
             m_re, m_im = image[s, 0:PIX], image[s, PIX:]
             both_re = a_re * b_re + a_im * b_im
             both_im = a_re * b_im - a_im * b_re
             back_re = both_re * m_re - both_im * m_im
             back_im = both_re * m_im + both_im * m_re
-            backs.append(jnp.concatenate([back_re, back_im], 0).astype(BF16))
+            pieces.append(jnp.concatenate([back_re, back_im], 0).astype(BF16))
+        return jnp.concatenate(pieces, 1)
+
+    lows[...] = left_side(backward, back_side(0))
+    backs[...] = back_side(1)
+
+    def step(g, carry):
         grads = []
-        for grad in transforms(backward, backs, right):
+        for grad in right_side(lows[...], right):
             re, im = grad[:PIX], grad[PIX:]
             grad_re = re[:, :LANES] + im[:, LANES:]
             grad_im = im[:, :LANES] - re[:, LANES:]
             grads.append(jnp.concatenate([grad_re, grad_im], 0).astype(BF16))
+        low = left_side(backward, backs[...])
+        back = back_side(jnp.minimum(g + 2, groups - 1))
+        lows[...] = low
+        backs[...] = back
+        subs = [g * group + k for k in range(group)]
         for s, grad in zip(subs, grads):
             stage[s] = grad
         for s in subs:
             pltpu.make_async_copy(stage.at[s], out.at[slot[s]], out_sems.at[s]).start()
         return carry
 
-    count, ready = image.shape[0], image.shape[0] // len(images)
-    for p, copy in enumerate(images):
-        copy.wait()
-        lax.fori_loop(p * ready // group, (p + 1) * ready // group, step, 0)
+    count, ready = image.shape[0], groups // len(images)
+    for p in range(len(images)):
+        if p + 1 < len(images):
+            images[p + 1].wait()
+        lax.fori_loop(p * ready, (p + 1) * ready, step, 0)
 
     def finished(s, carry):
         pltpu.make_async_copy(stage.at[s], out.at[slot[s]], out_sems.at[s]).wait()
@@ -468,7 +485,12 @@
         in_specs=[smem] * 4 + [pl.BlockSpec(memory_space=pl.ANY)] * 4 + [vmem] * 4,
         out_specs=pl.BlockSpec(memory_space=pl.ANY),
         scratch_shapes=table_scratch(near, images[0])
-        + [pltpu.VMEM((count, 2 * PIX, LANES), BF16), pltpu.SemaphoreType.DMA((count,))],
+        + [
+            pltpu.VMEM((count, 2 * PIX, LANES), BF16),
+            pltpu.SemaphoreType.DMA((count,)),
+            pltpu.VMEM((2 * PIX, group * LANES), BF16),
+            pltpu.VMEM((group * 2 * PIX, LANES), BF16),
+        ],
         name="patch",
     )(*where, *images, near, far, backward, right, spread_a, spread_b)
 
@@ -476,12 +498,13 @@
 def screen_kernel(
     group, n_bt, n_freq, me, slot, stations, slot_time, image_a, image_b, near, far,
     patches, forward, right, spread_a, spread_b, out_near, out_far,
-    table, sems, image, image_sems, acc,
+    table, sems, image, image_sems, acc, mids,
 ):
     chunk = 32
     copies = join_parts((near, far), table, sems, near.shape[0])
     copies += join_parts((image_a, image_b), image, image_sems, image_a.shape[0] // 2)
-    rows = table_rows(n_bt, n_freq, me, stations, slot_time)
+    row = table_rows(n_bt, n_freq, me, stations, slot_time)
+    groups = image.shape[0] // group
 
     def clear(i, carry):
         acc[pl.ds(i * chunk, chunk)] = jnp.zeros((chunk, PIX, LANES), F32)
@@ -492,13 +515,21 @@
         copy.wait()
     block = lax.broadcasted_iota(jnp.int32, (PIX, LANES), 1) // PIX
 
+    def begin(g):
+        return left_side(
+            forward, jnp.concatenate([patches[slot[g * group + k]] for k in range(group)], 1)
+        )
+
+    mids[...] = begin(0)
+
     def step(g, carry):
         terms = []
         subs = [g * group + k for k in range(group)]
-        first_rows, second_rows = [[rows(w, s) for s in subs] for w in (0, 1)]
-        first_screens = screens_of(table, [row for row, _ in first_rows], spread_a)
-        second_screens = screens_of(table, [row for row, _ in second_rows], spread_b)
-        skies = transforms(forward, [patches[slot[s]] for s in subs], right)
+        first_rows, second_rows = [[row(w, s) for s in subs] for w in (0, 1)]
+        skies = right_side(mids[...], right)
+        first_screens = screens_of(table, first_rows, spread_a)
+        second_screens = screens_of(table, second_rows, spread_b)
+        mid = begin(jnp.minimum(g + 1, groups - 1))
         for s, (a_re, a_im), (b_re, b_im), sky in zip(subs, first_screens, second_screens, skies):
             m_re, m_im = image[s, 0:PIX], image[s, PIX:]
             re, im = sky[:PIX], sky[PIX:]
@@ -528,7 +559,8 @@
                 gb_im + pltpu.roll(gb_im, 2 * PIX, 1),
             )
             terms.append((ta, tb))
-        for (ta, tb), (_, first), (_, second) in zip(terms, first_rows, second_rows):
+        mids[...] = mid
+        for (ta, tb), first, second in zip(terms, first_rows, second_rows):
             acc[first] = acc[first] + ta
             acc[second] = acc[second] + tb
         return carry
@@ -554,30 +586,54 @@
         out_shape=(jax.ShapeDtypeStruct(near.shape, BF16),) * 2,
         in_specs=[smem] * 4 + [pl.BlockSpec(memory_space=pl.ANY)] * 4 + [vmem] * 5,
         out_specs=(vmem,) * 2,
-        scratch_shapes=scratch + [pltpu.VMEM(scratch[0].shape, F32)],
+        scratch_shapes=scratch
+        + [pltpu.VMEM(scratch[0].shape, F32), pltpu.VMEM((group * 2 * PIX, LANES), BF16)],
         name="screen",
     )(*where, *images, near, far, patches, forward, right, spread_a, spread_b)
 
 
-def exchange(x, axis, groups=None):
-    return lax.all_to_all(
-        x, axis, split_axis=0, concat_axis=0, tiled=True, axis_index_groups=groups
-    )
+def exchange(x, axis):
+    return lax.all_to_all(x, axis, split_axis=0, concat_axis=0, tiled=True)
+
+
+def z_shift(n_z, step):
+    return [(2 * z + c, 2 * ((z + step) % n_z) + c) for z in range(n_z) for c in range(2)]
 
 
 def ring_gather(x, n_z):
-    def by(step):
-        return [(2 * z + c, 2 * ((z + step) % n_z) + c) for z in range(n_z) for c in range(2)]
-
+    half = n_z // 2
     blocks = [None] * n_z
     blocks[0] = up = down = x
-    for k in range(1, n_z // 2 + 1):
-        up = lax.ppermute(up, "freq", by(1))
-        blocks[n_z - k] = up
-        if k < n_z - k:
-            down = lax.ppermute(down, "freq", by(-1))
-            blocks[k] = down
+    for k in range(1, half):
+        up = lax.ppermute(up, "freq", z_shift(n_z, 1))
+        down = lax.ppermute(down, "freq", z_shift(n_z, -1))
+        blocks[n_z - k], blocks[k] = up, down
+    cut = x.shape[0] // 2
+    up = lax.ppermute(up[:cut], "freq", z_shift(n_z, 1))
+    down = lax.ppermute(down[cut:], "freq", z_shift(n_z, -1))
+    blocks[half] = jnp.concatenate([up, down])
     return jnp.stack(blocks)
+
+
+def ring_sum(mine, came, n_z):
+    half, cut = n_z // 2, mine.shape[1] // 2
+
+    def block(k, at=slice(None)):
+        return mine[k, at].astype(F32) + came[k, at].astype(F32)
+
+    up, down = block(half, slice(0, cut)).astype(BF16), block(half, slice(cut, None)).astype(BF16)
+    up = lax.ppermute(up, "freq", z_shift(n_z, 1))
+    down = lax.ppermute(down, "freq", z_shift(n_z, -1))
+    for k in range(half - 1, 0, -1):
+        next_up, next_down = block(k), block(n_z - k)
+        if k == half - 1:
+            zeros = jnp.zeros_like(up)
+            up, down = jnp.concatenate([up, zeros]), jnp.concatenate([zeros, down])
+        next_up = (next_up + up.astype(F32)).astype(BF16)
+        next_down = (next_down + down.astype(F32)).astype(BF16)
+        up = lax.ppermute(next_up, "freq", z_shift(n_z, 1))
+        down = lax.ppermute(next_down, "freq", z_shift(n_z, -1))
+    return (block(0) + up.astype(F32) + down.astype(F32)).astype(BF16)
 
 
 def per_device(
@@ -588,7 +644,6 @@
     slots = n_bt * CAP
     consts = constant_tables()
     swap = [(f, f ^ 1) for f in range(n_freq)]
-    same_core = [[2 * z + c for z in range(n_z)] for c in range(2)]
     row = TSLOTS * PIX
     mail, slot = make_mail(
         owner_tile[0, :, 0], row_offset[0], column[0], screens[:, 0], n_bt
@@ -612,11 +667,11 @@
         where, images, fetched, near, far, consts, n_bt, n_freq
     )
     came = lax.ppermute(sent, "freq", swap)
-    part = (terms.astype(F32) + came.astype(F32)).astype(BF16)
-    part = exchange(part.reshape(n_bt, n_z, TSLOTS, PIX, LANES), "bt")
+    blocks = (n_z, n_bt, TSLOTS * PIX, LANES)
+    part = ring_sum(terms.reshape(blocks), came.reshape(blocks), n_z)
+    part = exchange(part, "bt")
     grid_grad = add_windows(asked, returned, *uv_grid.shape[1:])
-    part = jnp.sum(part.astype(F32), 0).astype(BF16)
-    screen_grad = finish(exchange(part, "freq", same_core))
+    screen_grad = finish(part.reshape(n_bt, TSLOTS, PIX, LANES))
     return grid_grad[None], screen_grad[:, None]
 
 

time: 222 us -> 193 us (0.87)
  the two profiles are of different devices: /device:TPU:54 before, /device:TPU:22 now
where the time goes in v5:
time: 193 us; the launch traced here: 192 us
  Pallas kernels  67.6 us (35%)
  waiting for transfers between devices  52.8 us (27%)
  starting transfers between devices  51.9 us (27%)
  blocking collectives  12.5 us (6%)
  other arithmetic  5.68 us (3%)
    all_to_all x3, starting transfers between devices, exchange(): return lax.all_to_all(x, axis, split_axis=0, concat_axis=0, tiled=True)  21.3 us
    all_to_all x3, waiting for transfers between devices, exchange(): return lax.all_to_all(x, axis, split_axis=0, concat_axis=0, tiled=True)  17.5 us
    ppermute x3, waiting for transfers between devices, ring_sum(): up = lax.ppermute(next_up, 'freq', z_shift(n_z, 1))  14.7 us
    pallas_call x1, Pallas kernels, add_windows(): pl.pallas_call(add_kernel, out_shape=jax.ShapeDtypeStruct((comps, rows, c...  14.1 us
    pallas_call x1, Pallas kernels, cut_windows(): pl.pallas_call(cut_kernel, out_shape=jax.ShapeDtypeStruct((slots, 2 * PIX...  13.7 us
    pallas_call x1, Pallas kernels, screen_gradients(): pl.pallas_call(lambda *refs: screen_kernel(group, n_bt, n_freq, *refs), o...  13.3 us
    ppermute x3, starting transfers between devices, ring_gather(): down = lax.ppermute(down, 'freq', z_shift(n_z, -1))  13.3 us
    pallas_call x2, Pallas kernels, adjoint_images(): pl.pallas_call(lambda *refs: image_kernel(group, *refs), out_shape=jax.Sh...  13 us
  transfers between devices with their start and end apart: 21, of which 9 were waited for; matrix products, arithmetic and copies ran while one was open for 3% of the time, Pallas kernels for 26%

profile of v5, /device:TPU:22, one launch (start us, length us, event | category | flops | bytes accessed | tf_op | source)
XLA Modules:
  0.0 192.4 jit_solution(8758855800209686116)
XLA Ops:
  0.6 2.4 %mail.1 = (bf16[16,80,128]{2,1,0:T(8,128)(2,1)}, s32[64]{0:T(128)}) custom-call(s32[64]{0:T(128)} %bitcast.115, s32[64]{0:T(128)} %bitcast.116, s32[64]{0:T(128)} %bitcast.117, bf16[2,4,1024]{2,1,0:T(4,128)(2,1)} %bitcast.110), custom_call_target="tpu_custom_call" | custom-call | tf_op jit(solution)/shard_map/mail/pallas_call | solution.py:106
  3.0 12.5 %all_to_all.20 = bf16[16,80,128]{2,1,0:T(8,128)(2,1)S(1)} all-to-all(bf16[16,80,128]{2,1,0:T(8,128)(2,1)} %get-tuple-element.6), channel_id=1, replica_groups=mesh['bt'=16,'freq'=16] {'bt'}, dimensions={0} | all-to-all | bytes 655360 | tf_op jit(solution)/shard_map/all_to_all | solution.py:596
  15.5 5.9 %collective-permute-start = (bf16[16,64,128]{2,1,0:T(8,128)(2,1)S(1)}, bf16[16,64,128]{2,1,0:T(8,128)(2,1)S(1)}, u32[]{:S(2)}, u32[]{:S(2)}) collective-permute-start(bf16[16,64,128]{2,1,0:T(8,128)(2,1)S(1)} %slice.103), channel_id=1, source_target_pairs={{0,14},{1,15},{2,0},{3,1},{4,2},{5,3},{6,4},{7,5},{8,6},{9,7},{10,... | collective-permute-start | bytes 786440 | tf_op jit(solution)/shard_map/ppermute | solution.py:609
  21.5 4.4 %collective-permute-done = bf16[16,64,128]{2,1,0:T(8,128)(2,1)S(1)} collective-permute-done((bf16[16,64,128]{2,1,0:T(8,128)(2,1)S(1)}, bf16[16,64,128]{2,1,0:T(8,128)(2,1)S(1)}, u32[]{:S(2)}, u32[]{:S(2)}) %collective-permute-start) | collective-permute-done | bytes 262176 | tf_op jit(solution)/shard_map/ppermute | solution.py:609
  25.9 3.7 %collective-permute-start.1 = (bf16[16,64,128]{2,1,0:T(8,128)(2,1)S(1)}, bf16[16,64,128]{2,1,0:T(8,128)(2,1)S(1)}, u32[]{:S(2)}, u32[]{:S(2)}) collective-permute-start(bf16[16,64,128]{2,1,0:T(8,128)(2,1)S(1)} %collective-permute-done), channel_id=1, source_target_pairs={{0,14},{1,15},{2,0},{3,1},{4,2},{5,3},{6,4},{7,5},{8,6},{9,7},{10,... | collective-permute-start | bytes 786440 | tf_op jit(solution)/shard_map/ppermute | solution.py:609
  29.6 3.8 %collective-permute-done.1 = bf16[16,64,128]{2,1,0:T(8,128)(2,1)S(1)} collective-permute-done((bf16[16,64,128]{2,1,0:T(8,128)(2,1)S(1)}, bf16[16,64,128]{2,1,0:T(8,128)(2,1)S(1)}, u32[]{:S(2)}, u32[]{:S(2)}) %collective-permute-start.1) | collective-permute-done | bytes 262176 | tf_op jit(solution)/shard_map/ppermute | solution.py:609
  33.5 3.7 %collective-permute-start.2 = (bf16[16,64,128]{2,1,0:T(8,128)(2,1)S(1)}, bf16[16,64,128]{2,1,0:T(8,128)(2,1)S(1)}, u32[]{:S(2)}, u32[]{:S(2)}) collective-permute-start(bf16[16,64,128]{2,1,0:T(8,128)(2,1)S(1)} %collective-permute-done.1), channel_id=1, source_target_pairs={{0,14},{1,15},{2,0},{3,1},{4,2},{5,3},{6,4},{7,5},{8,6},{9,7},{10,... | collective-permute-start | bytes 786440 | tf_op jit(solution)/shard_map/ppermute | solution.py:609
  37.3 8.3 %collective-permute-done.5 = bf16[16,64,128]{2,1,0:T(8,128)(2,1)S(1)} collective-permute-done((bf16[16,64,128]{2,1,0:T(8,128)(2,1)S(1)}, bf16[16,64,128]{2,1,0:T(8,128)(2,1)S(1)}, u32[]{:S(2)}, u32[]{:S(2)}) %collective-permute-start.5) | collective-permute-done | bytes 262176 | tf_op jit(solution)/shard_map/ppermute | solution.py:608
  45.7 3.3 %collective-permute-start.7 = (bf16[8,64,128]{2,1,0:T(8,128)(2,1)S(1)}, bf16[8,64,128]{2,1,0:T(8,128)(2,1)S(1)}, u32[]{:S(2)}, u32[]{:S(2)}) collective-permute-start(bf16[8,64,128]{2,1,0:T(8,128)(2,1)S(1)} %slice.105), channel_id=1, source_target_pairs={{0,14},{1,15},{2,0},{3,1},{4,2},{5,3},{6,4},{7,5},{8,6},{9,7},{10,... | collective-permute-start | bytes 393224 | tf_op jit(solution)/shard_map/ppermute | solution.py:613
  49.1 2.8 %collective-permute-done.6 = bf16[8,64,128]{2,1,0:T(8,128)(2,1)S(1)} collective-permute-done((bf16[8,64,128]{2,1,0:T(8,128)(2,1)S(1)}, bf16[8,64,128]{2,1,0:T(8,128)(2,1)S(1)}, u32[]{:S(2)}, u32[]{:S(2)}) %collective-permute-start.6) | collective-permute-done | bytes 131104 | tf_op jit(solution)/shard_map/ppermute | solution.py:612
  52.9 13.7 %cut.1 = bf16[128,64,128]{2,1,0:T(8,128)(2,1)} custom-call(s32[16,128]{1,0:T(8,128)} %fusion.11.asked, bf16[8,64,1024]{2,1,0:T(8,128)(2,1)} %bitcast.103), custom_call_target="tpu_custom_call" | custom-call | tf_op jit(solution)/shard_map/cut/pallas_call | solution.py:227
  66.7 6.9 %all-to-all-start.2 = ((bf16[16,8,64,128]{3,2,1,0:T(8,128)(2,1)}), bf16[16,8,64,128]{3,2,1,0:T(8,128)(2,1)}, u32[]{:S(2)}, u32[]{:S(2)}) async-start(bf16[16,8,64,128]{3,2,1,0:T(8,128)(2,1)} %bitcast.93), calls=%async_computation.2 | async-start | bytes 4194304 | tf_op jit(solution)/shard_map/all_to_all | solution.py:596
  73.6 6.5 %image.2.refs_4_ = f32[32,64,128]{2,1,0:T(8,128)} custom-call(bf16[64,8,256]{2,1,0:T(8,128)(2,1)} %bitcast.105, f32[64,2,256]{2,1,0:T(2,128)} %bitcast.107), custom_call_target="tpu_custom_call" | custom-call | tf_op jit(solution)/shard_map/image/pallas_call | solution.py:353
  80.1 6.5 %image.3.refs_5_ = f32[32,64,128]{2,1,0:T(8,128)} custom-call(bf16[64,8,256]{2,1,0:T(8,128)(2,1)} %bitcast.106, f32[64,2,256]{2,1,0:T(2,128)} %bitcast.108), custom_call_target="tpu_custom_call" | custom-call | tf_op jit(solution)/shard_map/image/pallas_call | solution.py:353
  86.6 17.5 %all-to-all-done.2 = bf16[16,8,64,128]{3,2,1,0:T(8,128)(2,1)} async-done(((bf16[16,8,64,128]{3,2,1,0:T(8,128)(2,1)}), bf16[16,8,64,128]{3,2,1,0:T(8,128)(2,1)}, u32[]{:S(2)}, u32[]{:S(2)}) %all-to-all-start.2) | async-done | bytes 2097184 | tf_op jit(solution)/shard_map/all_to_all | solution.py:596
  104.1 13.3 %screen.1 = (bf16[256,32,128]{2,1,0:T(8,128)(2,1)}, bf16[256,32,128]{2,1,0:T(8,128)(2,1)}) custom-call(s32[1]{0:T(128)} %bitcast.5.refs_0_, s32[64]{0:T(128)} %get-tuple-element.7.refs_1_, s32[2,64]{1,0:T(2,128)} %bitcast.111, s32[64]{0:T(128)} %bitcast.113, f32[32,64,128]{2,1,0:T(8,128)} %image.2.refs_4_, f32[32,64,128]{2,1,0:T(8,128)} %image.3.refs_5_, ...), custom_call_target="tpu_custom_call" | custom-call | tf_op jit(solution)/shard_map/screen/pallas_call | solution.py:584
  117.6 9.2 %patch.1 = bf16[128,64,128]{2,1,0:T(8,128)(2,1)} custom-call(s32[1]{0:T(128)} %bitcast.5.refs_0_, s32[64]{0:T(128)} %get-tuple-element.7.refs_1_, s32[2,64]{1,0:T(2,128)} %bitcast.112, s32[64]{0:T(128)} %bitcast.114, f32[32,64,128]{2,1,0:T(8,128)} %image.2.refs_4_, f32[32,64,128]{2,1,0:T(8,128)} %image.3.refs_5_, bf16[256,32,128]{2,1,0:T(8,128)(2,1)} %bitcast.90, ...), custom_call_target="tpu_custom_call" | custom-call | tf_op jit(solution)/shard_map/patch/pallas_call | solution.py:482
  126.8 7.1 %all-to-all-start.1 = ((bf16[16,8,64,128]{3,2,1,0:T(8,128)(2,1)}), bf16[16,8,64,128]{3,2,1,0:T(8,128)(2,1)S(1)}, u32[]{:S(2)}, u32[]{:S(2)}) async-start(bf16[16,8,64,128]{3,2,1,0:T(8,128)(2,1)} %bitcast.91), calls=%async_computation.1 | async-start | bytes 4194304 | tf_op jit(solution)/shard_map/all_to_all | solution.py:596
  134.0 1.2 fusion.9
  135.2 3.5 %collective-permute-start.14 = (bf16[8,64,128]{2,1,0:T(8,128)(2,1)S(1)}, bf16[8,64,128]{2,1,0:T(8,128)(2,1)S(1)}, u32[]{:S(2)}, u32[]{:S(2)}) collective-permute-start(bf16[8,64,128]{2,1,0:T(8,128)(2,1)S(1)} %get-tuple-element.15), channel_id=1, source_target_pairs={{0,14},{1,15},{2,0},{3,1},{4,2},{5,3},{6,4},{7,5},{8,6},{9,7},{10,... | collective-permute-start | bytes 393224 | tf_op jit(solution)/shard_map/ppermute | solution.py:626
  138.7 2.6 %convert_add_fusion.3 = (f32[32,32,128]{2,1,0:T(8,128)S(1)}, f32[32,32,128]{2,1,0:T(8,128)S(1)}, f32[32,32,128]{2,1,0:T(8,128)S(1)}, f32[32,32,128]{2,1,0:T(8,12...) fusion(bf16[256,32,128]{2,1,0:T(8,128)(2,1)} %collective-permute-done.9, ...), kind=kLoop, calls=%fused_computation.18 | loop fusion | flops 2752512 | bytes 7340032 | tf_op jit(solution)/shard_map/add | solution.py:622
  141.3 1.2 collective-permute-done.10
  142.7 3.3 %collective-permute-start.15 = (bf16[16,64,128]{2,1,0:T(8,128)(2,1)S(1)}, bf16[16,64,128]{2,1,0:T(8,128)(2,1)S(1)}, u32[]{:S(2)}, u32[]{:S(2)}) collective-permute-start(bf16[16,64,128]{2,1,0:T(8,128)(2,1)S(1)} %fusion), channel_id=1, source_target_pairs={{0,14},{1,15},{2,0},{3,1},{4,2},{5,3},{6,4},{7,5},{8,6},{9,7},{10,... | collective-permute-start | bytes 786440 | tf_op jit(solution)/shard_map/ppermute | solution.py:635
  146.0 5.7 %collective-permute-done.11 = bf16[16,64,128]{2,1,0:T(8,128)(2,1)S(1)} collective-permute-done((bf16[16,64,128]{2,1,0:T(8,128)(2,1)S(1)}, bf16[16,64,128]{2,1,0:T(8,128)(2,1)S(1)}, u32[]{:S(2)}, u32[]{:S(2)}) %collective-permute-start.11) | collective-permute-done | bytes 262176 | tf_op jit(solution)/shard_map/ppermute | solution.py:634
  151.9 3.3 %collective-permute-start.16 = (bf16[16,64,128]{2,1,0:T(8,128)(2,1)S(1)}, bf16[16,64,128]{2,1,0:T(8,128)(2,1)S(1)}, u32[]{:S(2)}, u32[]{:S(2)}) collective-permute-start(bf16[16,64,128]{2,1,0:T(8,128)(2,1)S(1)} %fusion.1), channel_id=1, source_target_pairs={{0,14},{1,15},{2,0},{3,1},{4,2},{5,3},{6,4},{7,5},{8,6},{9,7},{10,... | collective-permute-start | bytes 786440 | tf_op jit(solution)/shard_map/ppermute | solution.py:635
  155.2 4.8 %collective-permute-done.12 = bf16[16,64,128]{2,1,0:T(8,128)(2,1)S(1)} collective-permute-done((bf16[16,64,128]{2,1,0:T(8,128)(2,1)S(1)}, bf16[16,64,128]{2,1,0:T(8,128)(2,1)S(1)}, u32[]{:S(2)}, u32[]{:S(2)}) %collective-permute-start.12) | collective-permute-done | bytes 262176 | tf_op jit(solution)/shard_map/ppermute | solution.py:634
  160.3 3.3 %collective-permute-start.17 = (bf16[16,64,128]{2,1,0:T(8,128)(2,1)S(1)}, bf16[16,64,128]{2,1,0:T(8,128)(2,1)S(1)}, u32[]{:S(2)}, u32[]{:S(2)}) collective-permute-start(bf16[16,64,128]{2,1,0:T(8,128)(2,1)S(1)} %fusion.2), channel_id=1, source_target_pairs={{0,14},{1,15},{2,0},{3,1},{4,2},{5,3},{6,4},{7,5},{8,6},{9,7},{10,... | collective-permute-start | bytes 786440 | tf_op jit(solution)/shard_map/ppermute | solution.py:635
  163.6 4.2 %collective-permute-done.13 = bf16[16,64,128]{2,1,0:T(8,128)(2,1)S(1)} collective-permute-done((bf16[16,64,128]{2,1,0:T(8,128)(2,1)S(1)}, bf16[16,64,128]{2,1,0:T(8,128)(2,1)S(1)}, u32[]{:S(2)}, u32[]{:S(2)}) %collective-permute-start.13) | collective-permute-done | bytes 262176 | tf_op jit(solution)/shard_map/ppermute | solution.py:634
  167.8 0.8 fusion.7
  168.6 7.2 %all-to-all-start.3 = ((bf16[16,64,128]{2,1,0:T(8,128)(2,1)}), bf16[16,64,128]{2,1,0:T(8,128)(2,1)S(1)}, u32[]{:S(2)}, u32[]{:S(2)}) async-start(bf16[16,64,128]{2,1,0:T(8,128)(2,1)} %fusion.7), calls=%async_computation.3 | async-start | bytes 524288 | tf_op jit(solution)/shard_map/all_to_all | solution.py:596
  175.8 14.1 %add.142 = f32[8,64,1024]{2,1,0:T(8,128)} custom-call(s32[16,128]{1,0:T(8,128)} %fusion.11.asked, bf16[128,64,128]{2,1,0:T(8,128)(2,1)} %bitcast.92), custom_call_target="tpu_custom_call" | custom-call | tf_op jit(solution)/shard_map/add/pallas_call | solution.py:286
  190.6 1.8 finish.1
  (47 shorter events, 2.8 us)
Async XLA Ops:
  15.5 10.4 %collective-permute-start = (bf16[16,64,128]{2,1,0:T(8,128)(2,1)S(1)}, bf16[16,64,128]{2,1,0:T(8,128)(2,1)S(1)}, u32[]{:S(2)}, u32[]{:S(2)}) collective-permute-start(bf16[16,64,128]{2,1,0:T(8,128)(2,1)S(1)} %slice.103), channel_id=1, source_target_pairs={{0,14},{1,15},{2,0},{3,1},{4,2},{5,3},{6,4},{7,5},{8,6},{9,7},{10,... | collective-permute-start | bytes 786440 | tf_op jit(solution)/shard_map/ppermute | solution.py:609
  21.5 8.1 %collective-permute-start.3 = (bf16[16,64,128]{2,1,0:T(8,128)(2,1)S(1)}, bf16[16,64,128]{2,1,0:T(8,128)(2,1)S(1)}, u32[]{:S(2)}, u32[]{:S(2)}) collective-permute-start(bf16[16,64,128]{2,1,0:T(8,128)(2,1)S(1)} %slice.103), channel_id=1, source_target_pairs={{0,2},{1,3},{2,4},{3,5},{4,6},{5,7},{6,8},{7,9},{8,10},{9,11},{10,... | collective-permute-start | bytes 786440 | tf_op jit(solution)/shard_map/ppermute | solution.py:608
  25.9 7.6 %collective-permute-start.1 = (bf16[16,64,128]{2,1,0:T(8,128)(2,1)S(1)}, bf16[16,64,128]{2,1,0:T(8,128)(2,1)S(1)}, u32[]{:S(2)}, u32[]{:S(2)}) collective-permute-start(bf16[16,64,128]{2,1,0:T(8,128)(2,1)S(1)} %collective-permute-done), channel_id=1, source_target_pairs={{0,14},{1,15},{2,0},{3,1},{4,2},{5,3},{6,4},{7,5},{8,6},{9,7},{10,... | collective-permute-start | bytes 786440 | tf_op jit(solution)/shard_map/ppermute | solution.py:609
  29.6 7.6 %collective-permute-start.4 = (bf16[16,64,128]{2,1,0:T(8,128)(2,1)S(1)}, bf16[16,64,128]{2,1,0:T(8,128)(2,1)S(1)}, u32[]{:S(2)}, u32[]{:S(2)}) collective-permute-start(bf16[16,64,128]{2,1,0:T(8,128)(2,1)S(1)} %collective-permute-done.3), channel_id=1, source_target_pairs={{0,2},{1,3},{2,4},{3,5},{4,6},{5,7},{6,8},{7,9},{8,10},{9,11},{10,... | collective-permute-start | bytes 786440 | tf_op jit(solution)/shard_map/ppermute | solution.py:608
  33.5 12.2 %collective-permute-start.2 = (bf16[16,64,128]{2,1,0:T(8,128)(2,1)S(1)}, bf16[16,64,128]{2,1,0:T(8,128)(2,1)S(1)}, u32[]{:S(2)}, u32[]{:S(2)}) collective-permute-start(bf16[16,64,128]{2,1,0:T(8,128)(2,1)S(1)} %collective-permute-done.1), channel_id=1, source_target_pairs={{0,14},{1,15},{2,0},{3,1},{4,2},{5,3},{6,4},{7,5},{8,6},{9,7},{10,... | collective-permute-start | bytes 786440 | tf_op jit(solution)/shard_map/ppermute | solution.py:609
  37.2 8.4 %collective-permute-start.5 = (bf16[16,64,128]{2,1,0:T(8,128)(2,1)S(1)}, bf16[16,64,128]{2,1,0:T(8,128)(2,1)S(1)}, u32[]{:S(2)}, u32[]{:S(2)}) collective-permute-start(bf16[16,64,128]{2,1,0:T(8,128)(2,1)S(1)} %collective-permute-done.4), channel_id=1, source_target_pairs={{0,2},{1,3},{2,4},{3,5},{4,6},{5,7},{6,8},{7,9},{8,10},{9,11},{10,... | collective-permute-start | bytes 786440 | tf_op jit(solution)/shard_map/ppermute | solution.py:608
  45.6 6.3 %collective-permute-start.6 = (bf16[8,64,128]{2,1,0:T(8,128)(2,1)S(1)}, bf16[8,64,128]{2,1,0:T(8,128)(2,1)S(1)}, u32[]{:S(2)}, u32[]{:S(2)}) collective-permute-start(bf16[8,64,128]{2,1,0:T(8,128)(2,1)S(1)} %slice.104), channel_id=1, source_target_pairs={{0,2},{1,3},{2,4},{3,5},{4,6},{5,7},{6,8},{7,9},{8,10},{9,11},{10,... | collective-permute-start | bytes 393224 | tf_op jit(solution)/shard_map/ppermute | solution.py:612
  45.7 6.1 %collective-permute-start.7 = (bf16[8,64,128]{2,1,0:T(8,128)(2,1)S(1)}, bf16[8,64,128]{2,1,0:T(8,128)(2,1)S(1)}, u32[]{:S(2)}, u32[]{:S(2)}) collective-permute-start(bf16[8,64,128]{2,1,0:T(8,128)(2,1)S(1)} %slice.105), channel_id=1, source_target_pairs={{0,14},{1,15},{2,0},{3,1},{4,2},{5,3},{6,4},{7,5},{8,6},{9,7},{10,... | collective-permute-start | bytes 393224 | tf_op jit(solution)/shard_map/ppermute | solution.py:613
  52.1 14.6 %copy-start = (bf16[8,16,64,128]{3,2,1,0:T(8,128)(2,1)}, bf16[8,16,64,128]{3,2,1,0:T(8,128)(2,1)S(1)}, u32[]{:S(2)}) copy-start(bf16[8,16,64,128]{3,2,1,0:T(8,128)(2,1)S(1)} %bitcast_dynamic-update-slice_fusion) | copy-start | bytes 6291460
  52.1 52.1 %collective-permute-start.8 = (bf16[256,32,128]{2,1,0:T(8,128)(2,1)S(1)}, bf16[256,32,128]{2,1,0:T(8,128)(2,1)}, u32[]{:S(2)}, u32[]{:S(2)}) collective-permute-start(bf16[256,32,128]{2,1,0:T(8,128)(2,1)S(1)} %bitcast.88), channel_id=1, source_target_pairs={{0,1},{1,0},{2,3},{3,2},{4,5},{5,4},{6,7},{7,6},{8,9},{9,8},{10,11... | collective-permute-start | bytes 6291464 | tf_op jit(solution)/shard_map/ppermute | solution.py:659
  66.7 37.5 %all-to-all-start.2 = ((bf16[16,8,64,128]{3,2,1,0:T(8,128)(2,1)}), bf16[16,8,64,128]{3,2,1,0:T(8,128)(2,1)}, u32[]{:S(2)}, u32[]{:S(2)}) async-start(bf16[16,8,64,128]{3,2,1,0:T(8,128)(2,1)} %bitcast.93), calls=%async_computation.2 | async-start | bytes 4194304 | tf_op jit(solution)/shard_map/all_to_all | solution.py:596
  117.5 16.5 %collective-permute-start.9 = (bf16[256,32,128]{2,1,0:T(8,128)(2,1)}, bf16[256,32,128]{2,1,0:T(8,128)(2,1)}, u32[]{:S(2)}, u32[]{:S(2)}) collective-permute-start(bf16[256,32,128]{2,1,0:T(8,128)(2,1)} %get-tuple-element.9), channel_id=1, source_target_pairs={{0,1},{1,0},{2,3},{3,2},{4,5},{5,4},{6,7},{7,6},{8,9},{9,8},{10,11... | collective-permute-start | bytes 6291464 | tf_op jit(solution)/shard_map/ppermute | solution.py:669
  126.8 41.8 %all-to-all-start.1 = ((bf16[16,8,64,128]{3,2,1,0:T(8,128)(2,1)}), bf16[16,8,64,128]{3,2,1,0:T(8,128)(2,1)S(1)}, u32[]{:S(2)}, u32[]{:S(2)}) async-start(bf16[16,8,64,128]{3,2,1,0:T(8,128)(2,1)} %bitcast.91), calls=%async_computation.1 | async-start | bytes 4194304 | tf_op jit(solution)/shard_map/all_to_all | solution.py:596
  135.2 7.3 %collective-permute-start.10 = (bf16[8,64,128]{2,1,0:T(8,128)(2,1)S(1)}, bf16[8,64,128]{2,1,0:T(8,128)(2,1)S(1)}, u32[]{:S(2)}, u32[]{:S(2)}) collective-permute-start(bf16[8,64,128]{2,1,0:T(8,128)(2,1)S(1)} %get-tuple-element.14), channel_id=1, source_target_pairs={{0,2},{1,3},{2,4},{3,5},{4,6},{5,7},{6,8},{7,9},{8,10},{9,11},{10,... | collective-permute-start | bytes 393224 | tf_op jit(solution)/shard_map/ppermute | solution.py:625
  135.2 7.4 %collective-permute-start.14 = (bf16[8,64,128]{2,1,0:T(8,128)(2,1)S(1)}, bf16[8,64,128]{2,1,0:T(8,128)(2,1)S(1)}, u32[]{:S(2)}, u32[]{:S(2)}) collective-permute-start(bf16[8,64,128]{2,1,0:T(8,128)(2,1)S(1)} %get-tuple-element.15), channel_id=1, source_target_pairs={{0,14},{1,15},{2,0},{3,1},{4,2},{5,3},{6,4},{7,5},{8,6},{9,7},{10,... | collective-permute-start | bytes 393224 | tf_op jit(solution)/shard_map/ppermute | solution.py:626
  142.6 9.1 %collective-permute-start.11 = (bf16[16,64,128]{2,1,0:T(8,128)(2,1)S(1)}, bf16[16,64,128]{2,1,0:T(8,128)(2,1)S(1)}, u32[]{:S(2)}, u32[]{:S(2)}) collective-permute-start(bf16[16,64,128]{2,1,0:T(8,128)(2,1)S(1)} %fusion.3), channel_id=1, source_target_pairs={{0,2},{1,3},{2,4},{3,5},{4,6},{5,7},{6,8},{7,9},{8,10},{9,11},{10,... | collective-permute-start | bytes 786440 | tf_op jit(solution)/shard_map/ppermute | solution.py:634
  142.7 9.1 %collective-permute-start.15 = (bf16[16,64,128]{2,1,0:T(8,128)(2,1)S(1)}, bf16[16,64,128]{2,1,0:T(8,128)(2,1)S(1)}, u32[]{:S(2)}, u32[]{:S(2)}) collective-permute-start(bf16[16,64,128]{2,1,0:T(8,128)(2,1)S(1)} %fusion), channel_id=1, source_target_pairs={{0,14},{1,15},{2,0},{3,1},{4,2},{5,3},{6,4},{7,5},{8,6},{9,7},{10,... | collective-permute-start | bytes 786440 | tf_op jit(solution)/shard_map/ppermute | solution.py:635
  151.8 8.3 %collective-permute-start.12 = (bf16[16,64,128]{2,1,0:T(8,128)(2,1)S(1)}, bf16[16,64,128]{2,1,0:T(8,128)(2,1)S(1)}, u32[]{:S(2)}, u32[]{:S(2)}) collective-permute-start(bf16[16,64,128]{2,1,0:T(8,128)(2,1)S(1)} %fusion.4), channel_id=1, source_target_pairs={{0,2},{1,3},{2,4},{3,5},{4,6},{5,7},{6,8},{7,9},{8,10},{9,11},{10,... | collective-permute-start | bytes 786440 | tf_op jit(solution)/shard_map/ppermute | solution.py:634
  151.9 8.3 %collective-permute-start.16 = (bf16[16,64,128]{2,1,0:T(8,128)(2,1)S(1)}, bf16[16,64,128]{2,1,0:T(8,128)(2,1)S(1)}, u32[]{:S(2)}, u32[]{:S(2)}) collective-permute-start(bf16[16,64,128]{2,1,0:T(8,128)(2,1)S(1)} %fusion.1), channel_id=1, source_target_pairs={{0,14},{1,15},{2,0},{3,1},{4,2},{5,3},{6,4},{7,5},{8,6},{9,7},{10,... | collective-permute-start | bytes 786440 | tf_op jit(solution)/shard_map/ppermute | solution.py:635
  160.1 7.7 %collective-permute-start.13 = (bf16[16,64,128]{2,1,0:T(8,128)(2,1)S(1)}, bf16[16,64,128]{2,1,0:T(8,128)(2,1)S(1)}, u32[]{:S(2)}, u32[]{:S(2)}) collective-permute-start(bf16[16,64,128]{2,1,0:T(8,128)(2,1)S(1)} %fusion.5), channel_id=1, source_target_pairs={{0,2},{1,3},{2,4},{3,5},{4,6},{5,7},{6,8},{7,9},{8,10},{9,11},{10,... | collective-permute-start | bytes 786440 | tf_op jit(solution)/shard_map/ppermute | solution.py:634
  160.3 7.5 %collective-permute-start.17 = (bf16[16,64,128]{2,1,0:T(8,128)(2,1)S(1)}, bf16[16,64,128]{2,1,0:T(8,128)(2,1)S(1)}, u32[]{:S(2)}, u32[]{:S(2)}) collective-permute-start(bf16[16,64,128]{2,1,0:T(8,128)(2,1)S(1)} %fusion.2), channel_id=1, source_target_pairs={{0,14},{1,15},{2,0},{3,1},{4,2},{5,3},{6,4},{7,5},{8,6},{9,7},{10,... | collective-permute-start | bytes 786440 | tf_op jit(solution)/shard_map/ppermute | solution.py:635
  168.6 7.2 %copy-start.1 = (bf16[16,8,64,128]{3,2,1,0:T(8,128)(2,1)}, bf16[16,8,64,128]{3,2,1,0:T(8,128)(2,1)S(1)}, u32[]{:S(2)}) copy-start(bf16[16,8,64,128]{3,2,1,0:T(8,128)(2,1)S(1)} %all-to-all-done.1) | copy-start | bytes 6291460
  168.6 21.3 %all-to-all-start.3 = ((bf16[16,64,128]{2,1,0:T(8,128)(2,1)}), bf16[16,64,128]{2,1,0:T(8,128)(2,1)S(1)}, u32[]{:S(2)}, u32[]{:S(2)}) async-start(bf16[16,64,128]{2,1,0:T(8,128)(2,1)} %fusion.7), calls=%async_computation.3 | async-start | bytes 524288 | tf_op jit(solution)/shard_map/all_to_all | solution.py:596
  189.9 0.7 copy-start.2

commit v6 on v5

--- a/solution.py
+++ b/solution.py
@@ -157,25 +157,39 @@
     return asked[j, k], asked[j, CAP + k] * PIX + asked[j, 2 * CAP + k]
 
 
-def for_listed(n, group, body):
-    def whole(g, carry):
-        body([g * group + k for k in range(group)])
-        return carry
-
-    lax.fori_loop(0, n // group, whole, 0)
-
-    def rest(i, carry):
-        body([i])
-        return carry
-
-    lax.fori_loop(n // group * group, n, rest, 0)
+def for_listed(n, body):
+    done = 0
+    for group in (8, 4, 1):
+
+        def some(g, carry, group=group, done=done):
+            body([done + g * group + k for k in range(group)])
+            return carry
+
+        count = (n - done) // group
+        lax.fori_loop(0, count, some, 0)
+        done = done + count * group
+
+
+HALF = LANES // 2
+
+
+def panel_of(c0, panels):
+    p = jnp.minimum(c0 >> 6, panels - 1)
+    return p, c0 - p * HALF
 
 
 def cut_kernel(asked, tile, out, wide, order, stage, sems):
     comps, rows, columns = tile.shape
-    panels = columns // LANES
-    for j in range(panels):
-        wide[j] = tile[:, :, j * LANES : (j + 1) * LANES].astype(F32).reshape(comps * rows, LANES)
+    panels = wide.shape[0]
+    low = lax.broadcasted_iota(jnp.int32, (comps * rows, LANES), 1) < HALF
+    before = None
+    for j in range(columns // LANES):
+        whole = tile[:, :, j * LANES : (j + 1) * LANES].astype(F32).reshape(comps * rows, LANES)
+        wide[2 * j] = whole
+        turned = pltpu.roll(whole, HALF, 1)
+        if before is not None:
+            wide[2 * j - 1] = jnp.where(low, before, turned)
+        before = turned
     n = listed(asked, order)
     line = lax.broadcasted_iota(jnp.int32, (LANES, LANES), 0)
     lane = lax.broadcasted_iota(jnp.int32, (LANES, LANES), 1)
@@ -187,17 +201,11 @@
         for place in places:
             i = order[place]
             r, c0 = corner(asked, i)
-            j, shift = c0 >> 7, c0 & (LANES - 1)
-            after = jnp.minimum(j + 1, panels - 1)
-
-            def rows_of(panel):
-                return jnp.concatenate(
-                    [wide[panel, pl.ds(c * rows + r, PIX), :] for c in range(comps)], 0
-                ).astype(BF16)
-
-            both = jnp.concatenate([rows_of(j), rows_of(after)], 1)
-            pick = jnp.concatenate([ahead == shift, ahead + LANES == shift], 0)
-            moved = dot(both, jnp.where(pick, 1.0, 0.0).astype(BF16))
+            p, shift = panel_of(c0, panels)
+            lines = jnp.concatenate(
+                [wide[p, pl.ds(c * rows + r, PIX), :] for c in range(comps)], 0
+            ).astype(BF16)
+            moved = dot(lines, jnp.where(ahead == shift, 1.0, 0.0).astype(BF16))
             parts = []
             for ri in range(2):
                 part = moved[ri * 128 : ri * 128 + PIX]
@@ -211,7 +219,7 @@
         for i, piece in done:
             pltpu.make_async_copy(stage.at[i], out.at[i], sems.at[i]).start()
 
-    for_listed(n, 4, body)
+    for_listed(n, body)
 
     def finished(g, carry):
         i = order[g]
@@ -230,7 +238,7 @@
         in_specs=[pl.BlockSpec(memory_space=pltpu.SMEM), pl.BlockSpec(memory_space=pltpu.VMEM)],
         out_specs=pl.BlockSpec(memory_space=pl.ANY),
         scratch_shapes=[
-            pltpu.VMEM((columns // LANES, comps * rows, LANES), F32),
+            pltpu.VMEM((columns // HALF - 1, comps * rows, LANES), F32),
             pltpu.SMEM((slots + CAP,), jnp.int32),
             pltpu.VMEM((slots, 2 * PIX, LANES), BF16),
             pltpu.SemaphoreType.DMA((slots,)),
@@ -241,9 +249,9 @@
 
 def add_kernel(asked, pieces, out, wide, order):
     comps, rows, columns = out.shape
-    panels = columns // LANES
-    for j in range(panels):
-        wide[j] = jnp.zeros((comps * rows, LANES), F32)
+    panels = wide.shape[0]
+    for p in range(panels):
+        wide[p] = jnp.zeros((comps * rows, LANES), F32)
     n = listed(asked, order)
     line = lax.broadcasted_iota(jnp.int32, (LANES, LANES), 0)
     lane = lax.broadcasted_iota(jnp.int32, (LANES, LANES), 1)
@@ -255,30 +263,33 @@
         for place in places:
             i = order[place]
             r, c0 = corner(asked, i)
-            j, shift = c0 >> 7, c0 & (LANES - 1)
+            p, shift = panel_of(c0, panels)
             piece = pieces[i].astype(F32)
             lines = []
             for ri in range(2):
                 for m in range(4):
                     lines.append(jnp.where(block == m, piece[ri * PIX : (ri + 1) * PIX], 0.0))
             lines = jnp.concatenate(lines, 0).astype(BF16)
-            pick = jnp.concatenate([ahead == shift, ahead + LANES == shift], 1)
-            spread.append((r, j, shift, dot(lines, jnp.where(pick, 1.0, 0.0).astype(BF16))))
-        for r, j, shift, moved in spread:
+            spread.append((r, p, dot(lines, jnp.where(ahead == shift, 1.0, 0.0).astype(BF16))))
+        for r, p, moved in spread:
+            sums = []
             for c in range(comps):
                 at = pl.ds(c * rows + r, PIX)
-                wide[j, at, :] = wide[j, at, :] + moved[c * PIX : (c + 1) * PIX, :LANES]
-        for r, j, shift, moved in spread:
-
-            @pl.when(shift > LANES - PIX)
-            def _(r=r, j=j, moved=moved):
-                for c in range(comps):
-                    at = pl.ds(c * rows + r, PIX)
-                    wide[j + 1, at, :] = wide[j + 1, at, :] + moved[c * PIX : (c + 1) * PIX, LANES:]
-
-    for_listed(n, 4, body)
-    for j in range(panels):
-        out[:, :, j * LANES : (j + 1) * LANES] = wide[j].reshape(comps, rows, LANES)
+                sums.append((at, wide[p, at, :] + moved[c * PIX : (c + 1) * PIX]))
+            for at, total in sums:
+                wide[p, at, :] = total
+
+    for_listed(n, body)
+    low = lax.broadcasted_iota(jnp.int32, (comps * rows, LANES), 1) < HALF
+    before = jnp.zeros((comps * rows, LANES), F32)
+    for j in range(columns // LANES):
+        if 2 * j + 1 < panels:
+            turned = pltpu.roll(wide[2 * j + 1], HALF, 1)
+        else:
+            turned = jnp.zeros((comps * rows, LANES), F32)
+        total = wide[2 * j] + jnp.where(low, before, turned)
+        out[:, :, j * LANES : (j + 1) * LANES] = total.reshape(comps, rows, LANES)
+        before = turned
 
 
 def add_windows(asked, pieces, comps, rows, columns):
@@ -289,7 +300,7 @@
         in_specs=[pl.BlockSpec(memory_space=pltpu.SMEM), pl.BlockSpec(memory_space=pltpu.VMEM)],
         out_specs=pl.BlockSpec(memory_space=pltpu.VMEM),
         scratch_shapes=[
-            pltpu.VMEM((columns // LANES, comps * rows, LANES), F32),
+            pltpu.VMEM((columns // HALF - 1, comps * rows, LANES), F32),
             pltpu.SMEM((slots + CAP,), jnp.int32),
         ],
         name="add",
@@ -386,9 +397,9 @@
     return copies
 
 
-def screens_of(table, rows, spread):
-    wide = dot(jnp.concatenate([table[row] for row in rows], 0), spread[...])
-    at = [slice(k * PIX, (k + 1) * PIX) for k in range(len(rows))]
+def screens_of(lines, spread):
+    wide = dot(jnp.concatenate(lines, 0), spread[...])
+    at = [slice(k * PIX, (k + 1) * PIX) for k in range(len(lines))]
     return [(wide[k, :LANES], wide[k, LANES:]) for k in at]
 
 
@@ -405,8 +416,8 @@
 
 def patch_kernel(
     group, n_bt, n_freq, me, slot, stations, slot_time, image_a, image_b, near, far,
-    backward, right, spread_a, spread_b, out, table, sems, image, image_sems, stage, out_sems,
-    backs, lows,
+    backward, right, spread_a, spread_b, out, used, table, sems, image, image_sems,
+    stage, out_sems, backs, lows, lines, line_sems,
 ):
     copies = join_parts((near, far), table, sems, near.shape[0])
     images = join_parts((image_a, image_b), image, image_sems, image_a.shape[0] // 2)
@@ -417,8 +428,10 @@
 
     def back_side(g):
         subs = [g * group + k for k in range(group)]
-        first_screens = screens_of(table, [row(0, s) for s in subs], spread_a)
-        second_screens = screens_of(table, [row(1, s) for s in subs], spread_b)
+        first_lines = [table[row(0, s)] for s in subs]
+        second_lines = [table[row(1, s)] for s in subs]
+        first_screens = screens_of(first_lines, spread_a)
+        second_screens = screens_of(second_lines, spread_b)
         pieces = []
         for s, (a_re, a_im), (b_re, b_im) in zip(subs, first_screens, second_screens):
             m_re, m_im = image[s, 0:PIX], image[s, PIX:]
@@ -427,7 +440,13 @@
             back_re = both_re * m_re - both_im * m_im
             back_im = both_re * m_im + both_im * m_re
             pieces.append(jnp.concatenate([back_re, back_im], 0).astype(BF16))
+        for s, a, b in zip(subs, first_lines, second_lines):
+            lines[s] = jnp.concatenate([a, b], 0)
         return jnp.concatenate(pieces, 1)
+
+    def hand_on(g):
+        at = pl.ds(g * group, group)
+        return pltpu.make_async_copy(lines.at[at], used.at[at], line_sems.at[g])
 
     lows[...] = left_side(backward, back_side(0))
     backs[...] = back_side(1)
@@ -448,6 +467,7 @@
             stage[s] = grad
         for s in subs:
             pltpu.make_async_copy(stage.at[s], out.at[slot[s]], out_sems.at[s]).start()
+        hand_on(g).start()
         return carry
 
     count, ready = image.shape[0], groups // len(images)
@@ -461,17 +481,8 @@
         return carry
 
     lax.fori_loop(0, count, finished, 0)
-
-
-def table_scratch(near, image):
-    whole = (2 * near.shape[0],) + near.shape[1:]
-    images = (2 * image.shape[0],) + image.shape[1:]
-    return [
-        pltpu.VMEM(whole, BF16),
-        pltpu.SemaphoreType.DMA((2,)),
-        pltpu.VMEM(images, F32),
-        pltpu.SemaphoreType.DMA((4,)),
-    ]
+    for g in range(groups):
+        hand_on(g).wait()
 
 
 def patch_gradients(where, images, near, far, consts, slots, n_bt, n_freq):
@@ -479,45 +490,74 @@
     count = 2 * images[0].shape[0]
     group = math.gcd(count // 4, 4)
     vmem, smem = pl.BlockSpec(memory_space=pltpu.VMEM), pl.BlockSpec(memory_space=pltpu.SMEM)
+    half = near.shape[0]
     return pl.pallas_call(
         lambda *refs: patch_kernel(group, n_bt, n_freq, *refs),
-        out_shape=jax.ShapeDtypeStruct((slots, 2 * PIX, LANES), BF16),
+        out_shape=(
+            jax.ShapeDtypeStruct((slots, 2 * PIX, LANES), BF16),
+            jax.ShapeDtypeStruct((count, 2 * PIX, LANES), BF16),
+        ),
         in_specs=[smem] * 4 + [pl.BlockSpec(memory_space=pl.ANY)] * 4 + [vmem] * 4,
-        out_specs=pl.BlockSpec(memory_space=pl.ANY),
-        scratch_shapes=table_scratch(near, images[0])
-        + [
+        out_specs=(pl.BlockSpec(memory_space=pl.ANY),) * 2,
+        scratch_shapes=[
+            pltpu.VMEM((2 * half,) + near.shape[1:], BF16),
+            pltpu.SemaphoreType.DMA((2,)),
+            pltpu.VMEM((count, 2 * PIX, LANES), F32),
+            pltpu.SemaphoreType.DMA((4,)),
             pltpu.VMEM((count, 2 * PIX, LANES), BF16),
             pltpu.SemaphoreType.DMA((count,)),
             pltpu.VMEM((2 * PIX, group * LANES), BF16),
             pltpu.VMEM((group * 2 * PIX, LANES), BF16),
+            pltpu.VMEM((count, 2 * PIX, LANES), BF16),
+            pltpu.SemaphoreType.DMA((count // group,)),
         ],
         name="patch",
     )(*where, *images, near, far, backward, right, spread_a, spread_b)
 
 
 def screen_kernel(
-    group, n_bt, n_freq, me, slot, stations, slot_time, image_a, image_b, near, far,
+    group, n_bt, n_freq, me, slot, stations, slot_time, image_a, image_b, used,
     patches, forward, right, spread_a, spread_b, out_near, out_far,
-    table, sems, image, image_sems, acc, mids,
+    lines, line_sems, image, image_sems, window, window_sems, acc, mids, stage, out_sems,
 ):
     chunk = 32
-    copies = join_parts((near, far), table, sems, near.shape[0])
-    copies += join_parts((image_a, image_b), image, image_sems, image_a.shape[0] // 2)
+    count = image.shape[0]
+    line_copies = join_parts((used,), lines, line_sems, count // 4)
+    image_copies = join_parts((image_a, image_b), image, image_sems, count // 4)
+
+    def window_copy(s):
+        return pltpu.make_async_copy(patches.at[slot[s]], window.at[s], window_sems.at[s])
+
+    def ask(s, carry):
+        window_copy(s).start()
+        return carry
+
+    lax.fori_loop(0, count, ask, 0)
+
+    def ready(p):
+        line_copies[p].wait()
+        image_copies[p].wait()
+
+        def have(s, carry):
+            window_copy(s).wait()
+            return carry
+
+        lax.fori_loop(p * count // 4, (p + 1) * count // 4, have, 0)
+
     row = table_rows(n_bt, n_freq, me, stations, slot_time)
-    groups = image.shape[0] // group
+    groups = count // group
 
     def clear(i, carry):
         acc[pl.ds(i * chunk, chunk)] = jnp.zeros((chunk, PIX, LANES), F32)
         return carry
 
     lax.fori_loop(0, acc.shape[0] // chunk, clear, 0)
-    for copy in copies:
-        copy.wait()
+    ready(0)
     block = lax.broadcasted_iota(jnp.int32, (PIX, LANES), 1) // PIX
 
     def begin(g):
         return left_side(
-            forward, jnp.concatenate([patches[slot[g * group + k]] for k in range(group)], 1)
+            forward, jnp.concatenate([window[g * group + k] for k in range(group)], 1)
         )
 
     mids[...] = begin(0)
@@ -527,8 +567,8 @@
         subs = [g * group + k for k in range(group)]
         first_rows, second_rows = [[row(w, s) for s in subs] for w in (0, 1)]
         skies = right_side(mids[...], right)
-        first_screens = screens_of(table, first_rows, spread_a)
-        second_screens = screens_of(table, second_rows, spread_b)
+        first_screens = screens_of([lines[s, 0:PIX] for s in subs], spread_a)
+        second_screens = screens_of([lines[s, PIX:] for s in subs], spread_b)
         mid = begin(jnp.minimum(g + 1, groups - 1))
         for s, (a_re, a_im), (b_re, b_im), sky in zip(subs, first_screens, second_screens, skies):
             m_re, m_im = image[s, 0:PIX], image[s, PIX:]
@@ -565,31 +605,50 @@
             acc[second] = acc[second] + tb
         return carry
 
-    lax.fori_loop(0, image.shape[0] // group, step, 0)
-
-    for start, out in ((0, out_near), (out_near.shape[0], out_far)):
-
-        def give(i, carry, start=start, out=out):
-            out[pl.ds(i * chunk, chunk)] = acc[pl.ds(start + i * chunk, chunk)].astype(BF16)
-            return carry
-
-        lax.fori_loop(0, out.shape[0] // chunk, give, 0)
-
-
-def screen_gradients(where, images, patches, near, far, consts, n_bt, n_freq):
+    for p in range(4):
+        if p + 1 < 4:
+            ready(p + 1)
+        lax.fori_loop(p * groups // 4, (p + 1) * groups // 4, step, 0)
+    copies = []
+    half = out_far.shape[0]
+    for start, out in ((half, out_far), (0, out_near)):
+        for i in range(0, half, chunk):
+            at = pl.ds(start + i, chunk)
+            stage[at] = acc[at].astype(BF16)
+            copy = pltpu.make_async_copy(
+                stage.at[at], out.at[pl.ds(i, chunk)], out_sems.at[len(copies)]
+            )
+            copy.start()
+            copies.append(copy)
+    for copy in copies:
+        copy.wait()
+
+
+def screen_gradients(where, images, patches, used, rows, consts, n_bt, n_freq):
     forward, _, right, spread_a, spread_b = consts
-    group = math.gcd(images[0].shape[0], 4)
+    count = used.shape[0]
+    group = math.gcd(count // 4, 4)
     vmem, smem = pl.BlockSpec(memory_space=pltpu.VMEM), pl.BlockSpec(memory_space=pltpu.SMEM)
-    scratch = table_scratch(near, images[0])
+    sums = jax.ShapeDtypeStruct((rows, PIX, LANES), BF16)
     return pl.pallas_call(
         lambda *refs: screen_kernel(group, n_bt, n_freq, *refs),
-        out_shape=(jax.ShapeDtypeStruct(near.shape, BF16),) * 2,
-        in_specs=[smem] * 4 + [pl.BlockSpec(memory_space=pl.ANY)] * 4 + [vmem] * 5,
-        out_specs=(vmem,) * 2,
-        scratch_shapes=scratch
-        + [pltpu.VMEM(scratch[0].shape, F32), pltpu.VMEM((group * 2 * PIX, LANES), BF16)],
+        out_shape=(sums, sums),
+        in_specs=[smem] * 4 + [pl.BlockSpec(memory_space=pl.ANY)] * 4 + [vmem] * 4,
+        out_specs=(pl.BlockSpec(memory_space=pl.ANY),) * 2,
+        scratch_shapes=[
+            pltpu.VMEM((count, 2 * PIX, LANES), BF16),
+            pltpu.SemaphoreType.DMA((4,)),
+            pltpu.VMEM((count, 2 * PIX, LANES), F32),
+            pltpu.SemaphoreType.DMA((4,)),
+            pltpu.VMEM((count, 2 * PIX, LANES), BF16),
+            pltpu.SemaphoreType.DMA((count,)),
+            pltpu.VMEM((2 * rows, PIX, LANES), F32),
+            pltpu.VMEM((group * 2 * PIX, LANES), BF16),
+            pltpu.VMEM((2 * rows, PIX, LANES), BF16),
+            pltpu.SemaphoreType.DMA((2 * rows // 32,)),
+        ],
         name="screen",
-    )(*where, *images, near, far, patches, forward, right, spread_a, spread_b)
+    )(*where, *images, used, patches, forward, right, spread_a, spread_b)
 
 
 def exchange(x, axis):
@@ -660,11 +719,11 @@
     cut = cut_windows(asked, uv_grid[0])
     fetched = exchange(cut.reshape(n_bt, CAP, 2 * PIX, LANES), "bt")
     fetched = fetched.reshape(slots, 2 * PIX, LANES)
-    grads = patch_gradients(where, images, near, far, consts, slots, n_bt, n_freq)
+    grads, used = patch_gradients(where, images, near, far, consts, slots, n_bt, n_freq)
     returned = exchange(grads.reshape(n_bt, CAP, 2 * PIX, LANES), "bt")
     returned = returned.reshape(slots, 2 * PIX, LANES)
     terms, sent = screen_gradients(
-        where, images, fetched, near, far, consts, n_bt, n_freq
+        where, images, fetched, used, near.shape[0], consts, n_bt, n_freq
     )
     came = lax.ppermute(sent, "freq", swap)
     blocks = (n_z, n_bt, TSLOTS * PIX, LANES)

time: 193 us -> 177 us (0.917)
  the two profiles are of different devices: /device:TPU:22 before, /device:TPU:14 now
where the time goes in v6:
time: 177 us
  Pallas kernels  57.5 us (32%)
  starting transfers between devices  50.3 us (28%)
  waiting for transfers between devices  41.5 us (23%)
  blocking collectives  13.2 us (7%)
  local copies, waits for them, and re-layouts  7.12 us (4%)
  other arithmetic  6.21 us (4%)
    all_to_all x3, starting transfers between devices, exchange(): return lax.all_to_all(x, axis, split_axis=0, concat_axis=0, tiled=True)  21.8 us
    ppermute x3, waiting for transfers between devices, ring_sum(): down = lax.ppermute(next_down, 'freq', z_shift(n_z, -1))  13.4 us
    ppermute x3, starting transfers between devices, ring_gather(): down = lax.ppermute(down, 'freq', z_shift(n_z, -1))  13.3 us
    all_to_all x1, blocking collectives, exchange(): return lax.all_to_all(x, axis, split_axis=0, concat_axis=0, tiled=True)  13.2 us
    pallas_call x2, Pallas kernels, adjoint_images(): pl.pallas_call(lambda *refs: image_kernel(group, *refs), out_shape=jax.Sh...  13 us
    pallas_call x1, Pallas kernels, screen_gradients(): pl.pallas_call(lambda *refs: screen_kernel(group, n_bt, n_freq, *refs), o...  12.2 us
    ppermute x3, waiting for transfers between devices, ring_gather(): down = lax.ppermute(down, 'freq', z_shift(n_z, -1))  10.3 us
    pallas_call x1, Pallas kernels, cut_windows(): pl.pallas_call(cut_kernel, out_shape=jax.ShapeDtypeStruct((slots, 2 * PIX...  9.67 us
  transfers between devices with their start and end apart: 21, of which 13 were waited for; matrix products, arithmetic and copies ran while one was open for 5% of the time, Pallas kernels for 23%

profile of v6, /device:TPU:14, one launch (start us, length us, event | category | flops | bytes accessed | tf_op | source)
XLA Modules:
  0.0 176.8 jit_solution(11137204493111163454)
XLA Ops:
  0.6 2.4 %mail.1 = (bf16[16,80,128]{2,1,0:T(8,128)(2,1)}, s32[64]{0:T(128)}) custom-call(s32[64]{0:T(128)} %bitcast.113, s32[64]{0:T(128)} %bitcast.114, s32[64]{0:T(128)} %bitcast.115, bf16[2,4,1024]{2,1,0:T(4,128)(2,1)} %bitcast.108), custom_call_target="tpu_custom_call" | custom-call | tf_op jit(solution)/shard_map/mail/pallas_call | solution.py:106
  3.0 13.2 %all_to_all.20 = bf16[16,80,128]{2,1,0:T(8,128)(2,1)S(1)} all-to-all(bf16[16,80,128]{2,1,0:T(8,128)(2,1)} %get-tuple-element.8), channel_id=1, replica_groups=mesh['bt'=16,'freq'=16] {'bt'}, dimensions={0} | all-to-all | bytes 655360 | tf_op jit(solution)/shard_map/all_to_all | solution.py:655
  16.3 5.9 %collective-permute-start = (bf16[16,64,128]{2,1,0:T(8,128)(2,1)S(1)}, bf16[16,64,128]{2,1,0:T(8,128)(2,1)S(1)}, u32[]{:S(2)}, u32[]{:S(2)}) collective-permute-start(bf16[16,64,128]{2,1,0:T(8,128)(2,1)S(1)} %slice.103), channel_id=1, source_target_pairs={{0,14},{1,15},{2,0},{3,1},{4,2},{5,3},{6,4},{7,5},{8,6},{9,7},{10,... | collective-permute-start | bytes 786440 | tf_op jit(solution)/shard_map/ppermute | solution.py:668
  22.2 3.9 %collective-permute-done = bf16[16,64,128]{2,1,0:T(8,128)(2,1)S(1)} collective-permute-done((bf16[16,64,128]{2,1,0:T(8,128)(2,1)S(1)}, bf16[16,64,128]{2,1,0:T(8,128)(2,1)S(1)}, u32[]{:S(2)}, u32[]{:S(2)}) %collective-permute-start) | collective-permute-done | bytes 262176 | tf_op jit(solution)/shard_map/ppermute | solution.py:668
  26.1 3.7 %collective-permute-start.1 = (bf16[16,64,128]{2,1,0:T(8,128)(2,1)S(1)}, bf16[16,64,128]{2,1,0:T(8,128)(2,1)S(1)}, u32[]{:S(2)}, u32[]{:S(2)}) collective-permute-start(bf16[16,64,128]{2,1,0:T(8,128)(2,1)S(1)} %collective-permute-done), channel_id=1, source_target_pairs={{0,14},{1,15},{2,0},{3,1},{4,2},{5,3},{6,4},{7,5},{8,6},{9,7},{10,... | collective-permute-start | bytes 786440 | tf_op jit(solution)/shard_map/ppermute | solution.py:668
  30.6 3.1 %collective-permute-done.1 = bf16[16,64,128]{2,1,0:T(8,128)(2,1)S(1)} collective-permute-done((bf16[16,64,128]{2,1,0:T(8,128)(2,1)S(1)}, bf16[16,64,128]{2,1,0:T(8,128)(2,1)S(1)}, u32[]{:S(2)}, u32[]{:S(2)}) %collective-permute-start.1) | collective-permute-done | bytes 262176 | tf_op jit(solution)/shard_map/ppermute | solution.py:668
  33.7 3.7 %collective-permute-start.2 = (bf16[16,64,128]{2,1,0:T(8,128)(2,1)S(1)}, bf16[16,64,128]{2,1,0:T(8,128)(2,1)S(1)}, u32[]{:S(2)}, u32[]{:S(2)}) collective-permute-start(bf16[16,64,128]{2,1,0:T(8,128)(2,1)S(1)} %collective-permute-done.1), channel_id=1, source_target_pairs={{0,14},{1,15},{2,0},{3,1},{4,2},{5,3},{6,4},{7,5},{8,6},{9,7},{10,... | collective-permute-start | bytes 786440 | tf_op jit(solution)/shard_map/ppermute | solution.py:668
  39.2 3.2 %collective-permute-done.2 = bf16[16,64,128]{2,1,0:T(8,128)(2,1)S(1)} collective-permute-done((bf16[16,64,128]{2,1,0:T(8,128)(2,1)S(1)}, bf16[16,64,128]{2,1,0:T(8,128)(2,1)S(1)}, u32[]{:S(2)}, u32[]{:S(2)}) %collective-permute-start.2) | collective-permute-done | bytes 262176 | tf_op jit(solution)/shard_map/ppermute | solution.py:668
  42.4 3.8 %collective-permute-start.7 = (bf16[8,64,128]{2,1,0:T(8,128)(2,1)S(1)}, bf16[8,64,128]{2,1,0:T(8,128)(2,1)S(1)}, u32[]{:S(2)}, u32[]{:S(2)}) collective-permute-start(bf16[8,64,128]{2,1,0:T(8,128)(2,1)S(1)} %slice.105), channel_id=1, source_target_pairs={{0,14},{1,15},{2,0},{3,1},{4,2},{5,3},{6,4},{7,5},{8,6},{9,7},{10,... | collective-permute-start | bytes 393224 | tf_op jit(solution)/shard_map/ppermute | solution.py:672
  47.5 1.2 collective-permute-done.7
  48.7 4.2 %collective-permute-done.6 = bf16[8,64,128]{2,1,0:T(8,128)(2,1)S(1)} collective-permute-done((bf16[8,64,128]{2,1,0:T(8,128)(2,1)S(1)}, bf16[8,64,128]{2,1,0:T(8,128)(2,1)S(1)}, u32[]{:S(2)}, u32[]{:S(2)}) %collective-permute-start.6) | collective-permute-done | bytes 131104 | tf_op jit(solution)/shard_map/ppermute | solution.py:671
  56.4 9.7 %cut.1 = bf16[128,64,128]{2,1,0:T(8,128)(2,1)} custom-call(s32[16,128]{1,0:T(8,128)} %fusion.11.asked, bf16[8,64,1024]{2,1,0:T(8,128)(2,1)} %bitcast.101), custom_call_target="tpu_custom_call" | custom-call | tf_op jit(solution)/shard_map/cut/pallas_call | solution.py:235
  66.1 6.0 %all-to-all-start.2 = ((bf16[16,8,64,128]{3,2,1,0:T(8,128)(2,1)}), bf16[16,8,64,128]{3,2,1,0:T(8,128)(2,1)S(1)}, u32[]{:S(2)}, u32[]{:S(2)}) async-start(bf16[16,8,64,128]{3,2,1,0:T(8,128)(2,1)} %bitcast.90), calls=%async_computation.2 | async-start | bytes 4194304 | tf_op jit(solution)/shard_map/all_to_all | solution.py:655
  72.1 6.5 %image.2.refs_4_ = f32[32,64,128]{2,1,0:T(8,128)} custom-call(bf16[64,8,256]{2,1,0:T(8,128)(2,1)} %bitcast.103, f32[64,2,256]{2,1,0:T(2,128)} %bitcast.105), custom_call_target="tpu_custom_call" | custom-call | tf_op jit(solution)/shard_map/image/pallas_call | solution.py:364
  78.6 6.6 %image.3.refs_5_ = f32[32,64,128]{2,1,0:T(8,128)} custom-call(bf16[64,8,256]{2,1,0:T(8,128)(2,1)} %bitcast.104, f32[64,2,256]{2,1,0:T(2,128)} %bitcast.106), custom_call_target="tpu_custom_call" | custom-call | tf_op jit(solution)/shard_map/image/pallas_call | solution.py:364
  85.2 9.4 %patch.1 = (bf16[128,64,128]{2,1,0:T(8,128)(2,1)}, bf16[64,64,128]{2,1,0:T(8,128)(2,1)}) custom-call(s32[1]{0:T(128)} %bitcast.5.refs_0_, s32[64]{0:T(128)} %get-tuple-element.9.refs_1_, s32[2,64]{1,0:T(2,128)} %bitcast.109, s32[64]{0:T(128)} %bitcast.111, f32[32,64,128]{2,1,0:T(8,128)} %image.2.refs_4_, f32[32,64,128]{2,1,0:T(8,128)} %image.3.refs_5_, ...), custom_call_target="tpu_custom_call" | custom-call | tf_op jit(solution)/shard_map/patch/pallas_call | solution.py:494
  94.6 6.9 %all-to-all-done.2 = bf16[16,8,64,128]{3,2,1,0:T(8,128)(2,1)S(1)} async-done(((bf16[16,8,64,128]{3,2,1,0:T(8,128)(2,1)}), bf16[16,8,64,128]{3,2,1,0:T(8,128)(2,1)S(1)}, u32[]{:S(2)}, u32[]{:S(2)}) %all-to-all-start.2) | async-done | bytes 2097184 | tf_op jit(solution)/shard_map/all_to_all | solution.py:655
  101.5 1.3 copy-done.1
  102.8 12.2 %screen.1 = (bf16[256,32,128]{2,1,0:T(8,128)(2,1)}, bf16[256,32,128]{2,1,0:T(8,128)(2,1)}) custom-call(s32[1]{0:T(128)} %bitcast.5.refs_0_, s32[64]{0:T(128)} %get-tuple-element.9.refs_1_, s32[2,64]{1,0:T(2,128)} %bitcast.110, s32[64]{0:T(128)} %bitcast.112, f32[32,64,128]{2,1,0:T(8,128)} %image.2.refs_4_, f32[32,64,128]{2,1,0:T(8,128)} %image.3.refs_5_, ...), custom_call_target="tpu_custom_call" | custom-call | tf_op jit(solution)/shard_map/screen/pallas_call | solution.py:633
  115.2 8.5 %all-to-all-start.1 = ((bf16[16,8,64,128]{3,2,1,0:T(8,128)(2,1)}), bf16[16,8,64,128]{3,2,1,0:T(8,128)(2,1)S(1)}, u32[]{:S(2)}, u32[]{:S(2)}) async-start(bf16[16,8,64,128]{3,2,1,0:T(8,128)(2,1)} %bitcast.99), calls=%async_computation.1 | async-start | bytes 4194304 | tf_op jit(solution)/shard_map/all_to_all | solution.py:655
  124.9 2.0 %collective-permute-start.10 = (bf16[8,64,128]{2,1,0:T(8,128)(2,1)S(1)}, bf16[8,64,128]{2,1,0:T(8,128)(2,1)S(1)}, u32[]{:S(2)}, u32[]{:S(2)}) collective-permute-start(bf16[8,64,128]{2,1,0:T(8,128)(2,1)S(1)} %get-tuple-element.20), channel_id=1, source_target_pairs={{0,2},{1,3},{2,4},{3,5},{4,6},{5,7},{6,8},{7,9},{8,10},{9,11},{10,... | collective-permute-start | bytes 393224 | tf_op jit(solution)/shard_map/ppermute | solution.py:684
  126.9 2.6 %convert_add_fusion.3 = (f32[32,32,128]{2,1,0:T(8,128)S(1)}, f32[32,32,128]{2,1,0:T(8,128)S(1)}, f32[32,32,128]{2,1,0:T(8,128)S(1)}, f32[32,32,128]{2,1,0:T(8,12...) fusion(bf16[256,32,128]{2,1,0:T(8,128)(2,1)} %collective-permute-done.9, ...), kind=kLoop, calls=%fused_computation.18 | loop fusion | flops 2752512 | bytes 7340032 | tf_op jit(solution)/shard_map/add | solution.py:681
  130.5 1.6 collective-permute-start.15
  132.7 5.3 %collective-permute-done.15 = bf16[16,64,128]{2,1,0:T(8,128)(2,1)S(1)} collective-permute-done((bf16[16,64,128]{2,1,0:T(8,128)(2,1)S(1)}, bf16[16,64,128]{2,1,0:T(8,128)(2,1)S(1)}, u32[]{:S(2)}, u32[]{:S(2)}) %collective-permute-start.15) | collective-permute-done | bytes 262176 | tf_op jit(solution)/shard_map/ppermute | solution.py:694
  138.2 3.1 %collective-permute-start.16 = (bf16[16,64,128]{2,1,0:T(8,128)(2,1)S(1)}, bf16[16,64,128]{2,1,0:T(8,128)(2,1)S(1)}, u32[]{:S(2)}, u32[]{:S(2)}) collective-permute-start(bf16[16,64,128]{2,1,0:T(8,128)(2,1)S(1)} %fusion.1), channel_id=1, source_target_pairs={{0,14},{1,15},{2,0},{3,1},{4,2},{5,3},{6,4},{7,5},{8,6},{9,7},{10,... | collective-permute-start | bytes 786440 | tf_op jit(solution)/shard_map/ppermute | solution.py:694
  141.4 4.3 %collective-permute-done.16 = bf16[16,64,128]{2,1,0:T(8,128)(2,1)S(1)} collective-permute-done((bf16[16,64,128]{2,1,0:T(8,128)(2,1)S(1)}, bf16[16,64,128]{2,1,0:T(8,128)(2,1)S(1)}, u32[]{:S(2)}, u32[]{:S(2)}) %collective-permute-start.16) | collective-permute-done | bytes 262176 | tf_op jit(solution)/shard_map/ppermute | solution.py:694
  145.8 3.8 %collective-permute-start.17 = (bf16[16,64,128]{2,1,0:T(8,128)(2,1)S(1)}, bf16[16,64,128]{2,1,0:T(8,128)(2,1)S(1)}, u32[]{:S(2)}, u32[]{:S(2)}) collective-permute-start(bf16[16,64,128]{2,1,0:T(8,128)(2,1)S(1)} %fusion.2), channel_id=1, source_target_pairs={{0,14},{1,15},{2,0},{3,1},{4,2},{5,3},{6,4},{7,5},{8,6},{9,7},{10,... | collective-permute-start | bytes 786440 | tf_op jit(solution)/shard_map/ppermute | solution.py:694
  149.7 3.7 %collective-permute-done.17 = bf16[16,64,128]{2,1,0:T(8,128)(2,1)S(1)} collective-permute-done((bf16[16,64,128]{2,1,0:T(8,128)(2,1)S(1)}, bf16[16,64,128]{2,1,0:T(8,128)(2,1)S(1)}, u32[]{:S(2)}, u32[]{:S(2)}) %collective-permute-start.17) | collective-permute-done | bytes 262176 | tf_op jit(solution)/shard_map/ppermute | solution.py:694
  153.4 3.8 %collective-permute-done.13 = bf16[16,64,128]{2,1,0:T(8,128)(2,1)S(1)} collective-permute-done((bf16[16,64,128]{2,1,0:T(8,128)(2,1)S(1)}, bf16[16,64,128]{2,1,0:T(8,128)(2,1)S(1)}, u32[]{:S(2)}, u32[]{:S(2)}) %collective-permute-start.13) | collective-permute-done | bytes 262176 | tf_op jit(solution)/shard_map/ppermute | solution.py:693
  158.1 7.3 %all-to-all-start.3 = ((bf16[16,64,128]{2,1,0:T(8,128)(2,1)}), bf16[16,64,128]{2,1,0:T(8,128)(2,1)S(1)}, u32[]{:S(2)}, u32[]{:S(2)}) async-start(bf16[16,64,128]{2,1,0:T(8,128)(2,1)} %fusion.7), calls=%async_computation.3 | async-start | bytes 524288 | tf_op jit(solution)/shard_map/all_to_all | solution.py:655
  165.4 8.9 %add.142 = f32[8,64,1024]{2,1,0:T(8,128)} custom-call(s32[16,128]{1,0:T(8,128)} %fusion.11.asked, bf16[128,64,128]{2,1,0:T(8,128)(2,1)} %bitcast.88), custom_call_target="tpu_custom_call" | custom-call | tf_op jit(solution)/shard_map/add/pallas_call | solution.py:297
  175.0 1.8 %finish.1 = f32[2,4,1024]{2,1,0:T(4,128)} custom-call(bf16[16,2,32,128]{3,2,1,0:T(8,128)(2,1)} %bitcast.102), custom_call_target="tpu_custom_call" | custom-call | tf_op jit(solution)/shard_map/finish/pallas_call | solution.py:137
  (47 shorter events, 12.2 us)
Async XLA Ops:
  16.3 9.9 %collective-permute-start = (bf16[16,64,128]{2,1,0:T(8,128)(2,1)S(1)}, bf16[16,64,128]{2,1,0:T(8,128)(2,1)S(1)}, u32[]{:S(2)}, u32[]{:S(2)}) collective-permute-start(bf16[16,64,128]{2,1,0:T(8,128)(2,1)S(1)} %slice.103), channel_id=1, source_target_pairs={{0,14},{1,15},{2,0},{3,1},{4,2},{5,3},{6,4},{7,5},{8,6},{9,7},{10,... | collective-permute-start | bytes 786440 | tf_op jit(solution)/shard_map/ppermute | solution.py:668
  22.2 7.6 %collective-permute-start.3 = (bf16[16,64,128]{2,1,0:T(8,128)(2,1)S(1)}, bf16[16,64,128]{2,1,0:T(8,128)(2,1)S(1)}, u32[]{:S(2)}, u32[]{:S(2)}) collective-permute-start(bf16[16,64,128]{2,1,0:T(8,128)(2,1)S(1)} %slice.103), channel_id=1, source_target_pairs={{0,2},{1,3},{2,4},{3,5},{4,6},{5,7},{6,8},{7,9},{8,10},{9,11},{10,... | collective-permute-start | bytes 786440 | tf_op jit(solution)/shard_map/ppermute | solution.py:667
  26.1 7.6 %collective-permute-start.1 = (bf16[16,64,128]{2,1,0:T(8,128)(2,1)S(1)}, bf16[16,64,128]{2,1,0:T(8,128)(2,1)S(1)}, u32[]{:S(2)}, u32[]{:S(2)}) collective-permute-start(bf16[16,64,128]{2,1,0:T(8,128)(2,1)S(1)} %collective-permute-done), channel_id=1, source_target_pairs={{0,14},{1,15},{2,0},{3,1},{4,2},{5,3},{6,4},{7,5},{8,6},{9,7},{10,... | collective-permute-start | bytes 786440 | tf_op jit(solution)/shard_map/ppermute | solution.py:668
  29.8 7.9 %collective-permute-start.4 = (bf16[16,64,128]{2,1,0:T(8,128)(2,1)S(1)}, bf16[16,64,128]{2,1,0:T(8,128)(2,1)S(1)}, u32[]{:S(2)}, u32[]{:S(2)}) collective-permute-start(bf16[16,64,128]{2,1,0:T(8,128)(2,1)S(1)} %collective-permute-done.3), channel_id=1, source_target_pairs={{0,2},{1,3},{2,4},{3,5},{4,6},{5,7},{6,8},{7,9},{8,10},{9,11},{10,... | collective-permute-start | bytes 786440 | tf_op jit(solution)/shard_map/ppermute | solution.py:667
  33.7 8.7 %collective-permute-start.2 = (bf16[16,64,128]{2,1,0:T(8,128)(2,1)S(1)}, bf16[16,64,128]{2,1,0:T(8,128)(2,1)S(1)}, u32[]{:S(2)}, u32[]{:S(2)}) collective-permute-start(bf16[16,64,128]{2,1,0:T(8,128)(2,1)S(1)} %collective-permute-done.1), channel_id=1, source_target_pairs={{0,14},{1,15},{2,0},{3,1},{4,2},{5,3},{6,4},{7,5},{8,6},{9,7},{10,... | collective-permute-start | bytes 786440 | tf_op jit(solution)/shard_map/ppermute | solution.py:668
  37.7 8.9 %collective-permute-start.5 = (bf16[16,64,128]{2,1,0:T(8,128)(2,1)S(1)}, bf16[16,64,128]{2,1,0:T(8,128)(2,1)S(1)}, u32[]{:S(2)}, u32[]{:S(2)}) collective-permute-start(bf16[16,64,128]{2,1,0:T(8,128)(2,1)S(1)} %collective-permute-done.4), channel_id=1, source_target_pairs={{0,2},{1,3},{2,4},{3,5},{4,6},{5,7},{6,8},{7,9},{8,10},{9,11},{10,... | collective-permute-start | bytes 786440 | tf_op jit(solution)/shard_map/ppermute | solution.py:667
  42.4 6.3 %collective-permute-start.7 = (bf16[8,64,128]{2,1,0:T(8,128)(2,1)S(1)}, bf16[8,64,128]{2,1,0:T(8,128)(2,1)S(1)}, u32[]{:S(2)}, u32[]{:S(2)}) collective-permute-start(bf16[8,64,128]{2,1,0:T(8,128)(2,1)S(1)} %slice.105), channel_id=1, source_target_pairs={{0,14},{1,15},{2,0},{3,1},{4,2},{5,3},{6,4},{7,5},{8,6},{9,7},{10,... | collective-permute-start | bytes 393224 | tf_op jit(solution)/shard_map/ppermute | solution.py:672
  46.7 6.3 %collective-permute-start.6 = (bf16[8,64,128]{2,1,0:T(8,128)(2,1)S(1)}, bf16[8,64,128]{2,1,0:T(8,128)(2,1)S(1)}, u32[]{:S(2)}, u32[]{:S(2)}) collective-permute-start(bf16[8,64,128]{2,1,0:T(8,128)(2,1)S(1)} %slice.104), channel_id=1, source_target_pairs={{0,2},{1,3},{2,4},{3,5},{4,6},{5,7},{6,8},{7,9},{8,10},{9,11},{10,... | collective-permute-start | bytes 393224 | tf_op jit(solution)/shard_map/ppermute | solution.py:671
  55.8 29.4 %collective-permute-start.8 = (bf16[256,32,128]{2,1,0:T(8,128)(2,1)}, bf16[256,32,128]{2,1,0:T(8,128)(2,1)}, u32[]{:S(2)}, u32[]{:S(2)}) collective-permute-start(bf16[256,32,128]{2,1,0:T(8,128)(2,1)} %bitcast.19.refs_6_), channel_id=1, source_target_pairs={{0,1},{1,0},{2,3},{3,2},{4,5},{5,4},{6,7},{7,6},{8,9},{9,8},{10,11... | collective-permute-start | bytes 6291464 | tf_op jit(solution)/shard_map/ppermute | solution.py:718
  66.1 35.4 %all-to-all-start.2 = ((bf16[16,8,64,128]{3,2,1,0:T(8,128)(2,1)}), bf16[16,8,64,128]{3,2,1,0:T(8,128)(2,1)S(1)}, u32[]{:S(2)}, u32[]{:S(2)}) async-start(bf16[16,8,64,128]{3,2,1,0:T(8,128)(2,1)} %bitcast.90), calls=%async_computation.2 | async-start | bytes 4194304 | tf_op jit(solution)/shard_map/all_to_all | solution.py:655
  101.5 1.3 copy-start.1
  115.1 8.6 %collective-permute-start.9 = (bf16[256,32,128]{2,1,0:T(8,128)(2,1)}, bf16[256,32,128]{2,1,0:T(8,128)(2,1)}, u32[]{:S(2)}, u32[]{:S(2)}) collective-permute-start(bf16[256,32,128]{2,1,0:T(8,128)(2,1)} %get-tuple-element.13), channel_id=1, source_target_pairs={{0,1},{1,0},{2,3},{3,2},{4,5},{5,4},{6,7},{7,6},{8,9},{9,8},{10,11... | collective-permute-start | bytes 6291464 | tf_op jit(solution)/shard_map/ppermute | solution.py:728
  115.2 42.9 %all-to-all-start.1 = ((bf16[16,8,64,128]{3,2,1,0:T(8,128)(2,1)}), bf16[16,8,64,128]{3,2,1,0:T(8,128)(2,1)S(1)}, u32[]{:S(2)}, u32[]{:S(2)}) async-start(bf16[16,8,64,128]{3,2,1,0:T(8,128)(2,1)} %bitcast.99), calls=%async_computation.1 | async-start | bytes 4194304 | tf_op jit(solution)/shard_map/all_to_all | solution.py:655
  124.8 5.6 %collective-permute-start.14 = (bf16[8,64,128]{2,1,0:T(8,128)(2,1)S(1)}, bf16[8,64,128]{2,1,0:T(8,128)(2,1)S(1)}, u32[]{:S(2)}, u32[]{:S(2)}) collective-permute-start(bf16[8,64,128]{2,1,0:T(8,128)(2,1)S(1)} %get-tuple-element.21), channel_id=1, source_target_pairs={{0,14},{1,15},{2,0},{3,1},{4,2},{5,3},{6,4},{7,5},{8,6},{9,7},{10,... | collective-permute-start | bytes 393224 | tf_op jit(solution)/shard_map/ppermute | solution.py:685
  124.9 7.2 %collective-permute-start.10 = (bf16[8,64,128]{2,1,0:T(8,128)(2,1)S(1)}, bf16[8,64,128]{2,1,0:T(8,128)(2,1)S(1)}, u32[]{:S(2)}, u32[]{:S(2)}) collective-permute-start(bf16[8,64,128]{2,1,0:T(8,128)(2,1)S(1)} %get-tuple-element.20), channel_id=1, source_target_pairs={{0,2},{1,3},{2,4},{3,5},{4,6},{5,7},{6,8},{7,9},{8,10},{9,11},{10,... | collective-permute-start | bytes 393224 | tf_op jit(solution)/shard_map/ppermute | solution.py:684
  130.5 7.6 %collective-permute-start.15 = (bf16[16,64,128]{2,1,0:T(8,128)(2,1)S(1)}, bf16[16,64,128]{2,1,0:T(8,128)(2,1)S(1)}, u32[]{:S(2)}, u32[]{:S(2)}) collective-permute-start(bf16[16,64,128]{2,1,0:T(8,128)(2,1)S(1)} %fusion), channel_id=1, source_target_pairs={{0,14},{1,15},{2,0},{3,1},{4,2},{5,3},{6,4},{7,5},{8,6},{9,7},{10,... | collective-permute-start | bytes 786440 | tf_op jit(solution)/shard_map/ppermute | solution.py:694
  132.1 9.1 %collective-permute-start.11 = (bf16[16,64,128]{2,1,0:T(8,128)(2,1)S(1)}, bf16[16,64,128]{2,1,0:T(8,128)(2,1)S(1)}, u32[]{:S(2)}, u32[]{:S(2)}) collective-permute-start(bf16[16,64,128]{2,1,0:T(8,128)(2,1)S(1)} %fusion.3), channel_id=1, source_target_pairs={{0,2},{1,3},{2,4},{3,5},{4,6},{5,7},{6,8},{7,9},{8,10},{9,11},{10,... | collective-permute-start | bytes 786440 | tf_op jit(solution)/shard_map/ppermute | solution.py:693
  138.2 7.5 %collective-permute-start.16 = (bf16[16,64,128]{2,1,0:T(8,128)(2,1)S(1)}, bf16[16,64,128]{2,1,0:T(8,128)(2,1)S(1)}, u32[]{:S(2)}, u32[]{:S(2)}) collective-permute-start(bf16[16,64,128]{2,1,0:T(8,128)(2,1)S(1)} %fusion.1), channel_id=1, source_target_pairs={{0,14},{1,15},{2,0},{3,1},{4,2},{5,3},{6,4},{7,5},{8,6},{9,7},{10,... | collective-permute-start | bytes 786440 | tf_op jit(solution)/shard_map/ppermute | solution.py:694
  141.3 8.2 %collective-permute-start.12 = (bf16[16,64,128]{2,1,0:T(8,128)(2,1)S(1)}, bf16[16,64,128]{2,1,0:T(8,128)(2,1)S(1)}, u32[]{:S(2)}, u32[]{:S(2)}) collective-permute-start(bf16[16,64,128]{2,1,0:T(8,128)(2,1)S(1)} %fusion.4), channel_id=1, source_target_pairs={{0,2},{1,3},{2,4},{3,5},{4,6},{5,7},{6,8},{7,9},{8,10},{9,11},{10,... | collective-permute-start | bytes 786440 | tf_op jit(solution)/shard_map/ppermute | solution.py:693
  145.8 7.7 %collective-permute-start.17 = (bf16[16,64,128]{2,1,0:T(8,128)(2,1)S(1)}, bf16[16,64,128]{2,1,0:T(8,128)(2,1)S(1)}, u32[]{:S(2)}, u32[]{:S(2)}) collective-permute-start(bf16[16,64,128]{2,1,0:T(8,128)(2,1)S(1)} %fusion.2), channel_id=1, source_target_pairs={{0,14},{1,15},{2,0},{3,1},{4,2},{5,3},{6,4},{7,5},{8,6},{9,7},{10,... | collective-permute-start | bytes 786440 | tf_op jit(solution)/shard_map/ppermute | solution.py:694
  149.6 7.7 %collective-permute-start.13 = (bf16[16,64,128]{2,1,0:T(8,128)(2,1)S(1)}, bf16[16,64,128]{2,1,0:T(8,128)(2,1)S(1)}, u32[]{:S(2)}, u32[]{:S(2)}) collective-permute-start(bf16[16,64,128]{2,1,0:T(8,128)(2,1)S(1)} %fusion.5), channel_id=1, source_target_pairs={{0,2},{1,3},{2,4},{3,5},{4,6},{5,7},{6,8},{7,9},{8,10},{9,11},{10,... | collective-permute-start | bytes 786440 | tf_op jit(solution)/shard_map/ppermute | solution.py:693
  158.1 7.3 %copy-start = (bf16[16,8,64,128]{3,2,1,0:T(8,128)(2,1)}, bf16[16,8,64,128]{3,2,1,0:T(8,128)(2,1)S(1)}, u32[]{:S(2)}) copy-start(bf16[16,8,64,128]{3,2,1,0:T(8,128)(2,1)S(1)} %all-to-all-done.1) | copy-start | bytes 6291460
  158.1 16.2 %all-to-all-start.3 = ((bf16[16,64,128]{2,1,0:T(8,128)(2,1)}), bf16[16,64,128]{2,1,0:T(8,128)(2,1)S(1)}, u32[]{:S(2)}, u32[]{:S(2)}) async-start(bf16[16,64,128]{2,1,0:T(8,128)(2,1)} %fusion.7), calls=%async_computation.3 | async-start | bytes 524288 | tf_op jit(solution)/shard_map/all_to_all | solution.py:655
  174.3 0.7 copy-start.2

commit v7 on v6

--- a/solution.py
+++ b/solution.py
@@ -140,6 +140,7 @@
         in_specs=[vmem],
         out_specs=vmem,
         name="finish",
+        compiler_params=pltpu.CompilerParams(vmem_limit_bytes=4 << 20),
     )(parts)
 
 
@@ -304,6 +305,7 @@
             pltpu.SMEM((slots + CAP,), jnp.int32),
         ],
         name="add",
+        compiler_params=pltpu.CompilerParams(vmem_limit_bytes=14 << 20),
     )(asked, pieces)
 
 
@@ -355,12 +357,10 @@
     lax.fori_loop(0, vis.shape[0] // group, step, 0)
 
 
-def adjoint_images(vis, uv, part, parts):
-    count = vis.shape[0] // parts
+def adjoint_images(vis, uv, first, count):
     group = math.gcd(count, 4)
-    blocks = [
-        pl.BlockSpec((count,) + x.shape[1:], lambda i: (part, 0, 0)) for x in (vis, uv)
-    ]
+    at = first // count
+    blocks = [pl.BlockSpec((count,) + x.shape[1:], lambda i: (at, 0, 0)) for x in (vis, uv)]
     return pl.pallas_call(
         lambda *refs: image_kernel(group, *refs),
         out_shape=jax.ShapeDtypeStruct((count, 2 * PIX, LANES), F32),
@@ -387,16 +387,32 @@
 
 def join_parts(parts, whole, sems, chunk):
     copies = []
-    for p, part in enumerate(parts):
+    for part in parts:
         for c in range(0, part.shape[0], chunk):
-            at = pl.ds(p * part.shape[0] + c, chunk)
             k = len(copies)
+            at = pl.ds(k * chunk, chunk)
             copy = pltpu.make_async_copy(part.at[pl.ds(c, chunk)], whole.at[at], sems.at[k])
             copy.start()
             copies.append(copy)
     return copies
 
 
+def join_rings(halves, table, sems):
+    copies, at = [], 0
+    for early, late in halves:
+        block = (early.shape[0] + late.shape[0]) // 8
+        for part, start, count in ((early, 0, 3), (late, 0, 3), (early, 3, 2)):
+            copy = pltpu.make_async_copy(
+                part.at[pl.ds(start * block, count * block)],
+                table.at[pl.ds(at, count * block)],
+                sems.at[len(copies)],
+            )
+            copy.start()
+            copies.append(copy)
+            at += count * block
+    return copies
+
+
 def screens_of(lines, spread):
     wide = dot(jnp.concatenate(lines, 0), spread[...])
     at = [slice(k * PIX, (k + 1) * PIX) for k in range(len(lines))]
@@ -415,12 +431,12 @@
 
 
 def patch_kernel(
-    group, n_bt, n_freq, me, slot, stations, slot_time, image_a, image_b, near, far,
-    backward, right, spread_a, spread_b, out, used, table, sems, image, image_sems,
+    group, n_bt, n_freq, me, slot, stations, slot_time, image_a, image_b, image_c,
+    near_a, near_b, far_a, far_b, backward, right, spread_a, spread_b, out, used, table, sems, image, image_sems,
     stage, out_sems, backs, lows, lines, line_sems,
 ):
-    copies = join_parts((near, far), table, sems, near.shape[0])
-    images = join_parts((image_a, image_b), image, image_sems, image_a.shape[0] // 2)
+    copies = join_rings(((near_a, near_b), (far_a, far_b)), table, sems)
+    images = join_parts((image_a, image_b, image_c), image, image_sems, image_c.shape[0])
     row = table_rows(n_bt, n_freq, me, stations, slot_time)
     for copy in copies + images[:1]:
         copy.wait()
@@ -485,23 +501,23 @@
         hand_on(g).wait()
 
 
-def patch_gradients(where, images, near, far, consts, slots, n_bt, n_freq):
+def patch_gradients(where, images, rings, consts, slots, n_bt, n_freq):
     _, backward, right, spread_a, spread_b = consts
-    count = 2 * images[0].shape[0]
+    count = 4 * images[-1].shape[0]
     group = math.gcd(count // 4, 4)
     vmem, smem = pl.BlockSpec(memory_space=pltpu.VMEM), pl.BlockSpec(memory_space=pltpu.SMEM)
-    half = near.shape[0]
+    half = rings[0].shape[0] + rings[1].shape[0]
     return pl.pallas_call(
         lambda *refs: patch_kernel(group, n_bt, n_freq, *refs),
         out_shape=(
             jax.ShapeDtypeStruct((slots, 2 * PIX, LANES), BF16),
             jax.ShapeDtypeStruct((count, 2 * PIX, LANES), BF16),
         ),
-        in_specs=[smem] * 4 + [pl.BlockSpec(memory_space=pl.ANY)] * 4 + [vmem] * 4,
+        in_specs=[smem] * 4 + [pl.BlockSpec(memory_space=pl.ANY)] * 7 + [vmem] * 4,
         out_specs=(pl.BlockSpec(memory_space=pl.ANY),) * 2,
         scratch_shapes=[
-            pltpu.VMEM((2 * half,) + near.shape[1:], BF16),
-            pltpu.SemaphoreType.DMA((2,)),
+            pltpu.VMEM((2 * half, PIX, LANES), BF16),
+            pltpu.SemaphoreType.DMA((6,)),
             pltpu.VMEM((count, 2 * PIX, LANES), F32),
             pltpu.SemaphoreType.DMA((4,)),
             pltpu.VMEM((count, 2 * PIX, LANES), BF16),
@@ -512,18 +528,19 @@
             pltpu.SemaphoreType.DMA((count // group,)),
         ],
         name="patch",
-    )(*where, *images, near, far, backward, right, spread_a, spread_b)
+        compiler_params=pltpu.CompilerParams(vmem_limit_bytes=64 << 20),
+    )(*where, *images, *rings, backward, right, spread_a, spread_b)
 
 
 def screen_kernel(
-    group, n_bt, n_freq, me, slot, stations, slot_time, image_a, image_b, used,
+    group, n_bt, n_freq, me, slot, stations, slot_time, image_a, image_b, image_c, used,
     patches, forward, right, spread_a, spread_b, out_near, out_far,
     lines, line_sems, image, image_sems, window, window_sems, acc, mids, stage, out_sems,
 ):
     chunk = 32
     count = image.shape[0]
     line_copies = join_parts((used,), lines, line_sems, count // 4)
-    image_copies = join_parts((image_a, image_b), image, image_sems, count // 4)
+    image_copies = join_parts((image_a, image_b, image_c), image, image_sems, count // 4)
 
     def window_copy(s):
         return pltpu.make_async_copy(patches.at[slot[s]], window.at[s], window_sems.at[s])
@@ -633,7 +650,7 @@
     return pl.pallas_call(
         lambda *refs: screen_kernel(group, n_bt, n_freq, *refs),
         out_shape=(sums, sums),
-        in_specs=[smem] * 4 + [pl.BlockSpec(memory_space=pl.ANY)] * 4 + [vmem] * 4,
+        in_specs=[smem] * 4 + [pl.BlockSpec(memory_space=pl.ANY)] * 5 + [vmem] * 4,
         out_specs=(pl.BlockSpec(memory_space=pl.ANY),) * 2,
         scratch_shapes=[
             pltpu.VMEM((count, 2 * PIX, LANES), BF16),
@@ -671,7 +688,8 @@
     up = lax.ppermute(up[:cut], "freq", z_shift(n_z, 1))
     down = lax.ppermute(down[cut:], "freq", z_shift(n_z, -1))
     blocks[half] = jnp.concatenate([up, down])
-    return jnp.stack(blocks)
+    early = jnp.stack(blocks[:3] + blocks[6:])
+    return early, jnp.stack(blocks[3:6])
 
 
 def ring_sum(mine, came, n_z):
@@ -709,21 +727,24 @@
     )
     me = lax.axis_index("freq").astype(jnp.int32).reshape(1)
     where = (me, slot, stations[0].T, time_slot[0])
-    image_a = adjoint_images(residual[0], uv_coords[0], 0, 2)
-    image_b = adjoint_images(residual[0], uv_coords[0], 1, 2)
-    images = (image_a, image_b)
+    quarter = residual.shape[1] // 4
+    images = []
+    for part, (begin, count) in enumerate(((0, 2), (2, 1), (3, 1))):
+        images.append(adjoint_images(residual[0], uv_coords[0], begin * quarter, count * quarter))
     mail = exchange(mail, "bt")
     asked = mail[:, row].astype(jnp.int32)
-    near = ring_gather(mail[:, :row], n_z).reshape(n_z * n_bt * TSLOTS, PIX, LANES)
-    far = lax.ppermute(near, "freq", swap)
+    near = [x.reshape(-1, PIX, LANES) for x in ring_gather(mail[:, :row], n_z)]
+    far_early = lax.ppermute(near[0], "freq", swap)
+    far_late = lax.ppermute(near[1], "freq", swap)
+    rings = (*near, far_early, far_late)
     cut = cut_windows(asked, uv_grid[0])
     fetched = exchange(cut.reshape(n_bt, CAP, 2 * PIX, LANES), "bt")
     fetched = fetched.reshape(slots, 2 * PIX, LANES)
-    grads, used = patch_gradients(where, images, near, far, consts, slots, n_bt, n_freq)
+    grads, used = patch_gradients(where, images, rings, consts, slots, n_bt, n_freq)
     returned = exchange(grads.reshape(n_bt, CAP, 2 * PIX, LANES), "bt")
     returned = returned.reshape(slots, 2 * PIX, LANES)
     terms, sent = screen_gradients(
-        where, images, fetched, used, near.shape[0], consts, n_bt, n_freq
+        where, images, fetched, used, n_z * n_bt * TSLOTS, consts, n_bt, n_freq
     )
     came = lax.ppermute(sent, "freq", swap)
     blocks = (n_z, n_bt, TSLOTS * PIX, LANES)

time: 177 us -> 161 us (0.910)
  waiting for transfers between devices: 41.5 us -> 28.9 us
  local copies, waits for them, and re-layouts: 7.12 us -> 1.32 us
  starting transfers between devices: 50.3 us -> 53.4 us
    all_to_all x3, waiting for transfers between devices: 6.86 us -> 0.01 us  [exchange(): return lax.all_to_all(x, axis, split_axis=0, concat_axis=0, tiled=True)]
    unnamed x12, local copies, waits for them, and re-layouts: 6.36 us -> 1.24 us
    ppermute x1, starting transfers between devices: 0.08 us -> 3.22 us  [ring_sum(): down = lax.ppermute(down, 'freq', z_shift(n_z, -1))]
    ppermute x3, waiting for transfers between devices: 10.3 us -> 7.46 us  [ring_gather(): down = lax.ppermute(down, 'freq', z_shift(n_z, -1))]
    ppermute x3, starting transfers between devices: 8.4 us -> 11.2 us  [ring_sum(): down = lax.ppermute(next_down, 'freq', z_shift(n_z, -1))]
    ppermute x3, waiting for transfers between devices: 13.4 us -> 11.4 us  [ring_sum(): down = lax.ppermute(next_down, 'freq', z_shift(n_z, -1))]
    ppermute x1, starting transfers between devices: 2.01 us -> 0.08 us  [ring_sum(): up = lax.ppermute(up, 'freq', z_shift(n_z, 1))]
    pallas_call x2 -> x3, Pallas kernels: 13 us -> 14.4 us  [adjoint_images(): pl.pallas_call(lambda *refs: image_kernel(group, *refs), out_shape=jax.Sh...]
  transfers between devices with their start and end apart: 21 -> 22, of which waited for: 13 -> 8; matrix products, arithmetic and copies ran while one was open for 5% -> 4% of each run, Pallas kernels for 23% -> 26%
where the time goes in v7:
time: 161 us; the launch traced here: 160 us
  Pallas kernels  56.8 us (35%)
  starting transfers between devices  53.4 us (33%)
  waiting for transfers between devices  28.9 us (18%)
  blocking collectives  13.2 us (8%)
  other arithmetic  5.59 us (3%)
    all_to_all x3, starting transfers between devices, exchange(): return lax.all_to_all(x, axis, split_axis=0, concat_axis=0, tiled=True)  20.9 us
    pallas_call x3, Pallas kernels, adjoint_images(): pl.pallas_call(lambda *refs: image_kernel(group, *refs), out_shape=jax.Sh...  14.4 us
    all_to_all x1, blocking collectives, exchange(): return lax.all_to_all(x, axis, split_axis=0, concat_axis=0, tiled=True)  13.2 us
    ppermute x3, starting transfers between devices, ring_gather(): down = lax.ppermute(down, 'freq', z_shift(n_z, -1))  12.9 us
    pallas_call x1, Pallas kernels, screen_gradients(): pl.pallas_call(lambda *refs: screen_kernel(group, n_bt, n_freq, *refs), o...  12.2 us
    ppermute x3, waiting for transfers between devices, ring_sum(): down = lax.ppermute(next_down, 'freq', z_shift(n_z, -1))  11.4 us
    ppermute x3, starting transfers between devices, ring_sum(): down = lax.ppermute(next_down, 'freq', z_shift(n_z, -1))  11.2 us
    pallas_call x1, Pallas kernels, cut_windows(): pl.pallas_call(cut_kernel, out_shape=jax.ShapeDtypeStruct((slots, 2 * PIX...  9.68 us
  transfers between devices with their start and end apart: 22, of which 8 were waited for; matrix products, arithmetic and copies ran while one was open for 4% of the time, Pallas kernels for 26%

profile of v7, /device:TPU:14, one launch (start us, length us, event | category | flops | bytes accessed | tf_op | source)
XLA Modules:
  0.0 160.2 jit_solution(8320229406995133464)
XLA Ops:
  0.6 2.4 %mail.1 = (bf16[16,80,128]{2,1,0:T(8,128)(2,1)}, s32[64]{0:T(128)}) custom-call(s32[64]{0:T(128)} %bitcast.117, s32[64]{0:T(128)} %bitcast.118, s32[64]{0:T(128)} %bitcast.119, bf16[2,4,1024]{2,1,0:T(4,128)(2,1)} %bitcast.112), custom_call_target="tpu_custom_call" | custom-call | tf_op jit(solution)/shard_map/mail/pallas_call | solution.py:106
  3.0 13.2 %all_to_all.20 = bf16[16,80,128]{2,1,0:T(8,128)(2,1)S(1)} all-to-all(bf16[16,80,128]{2,1,0:T(8,128)(2,1)} %get-tuple-element.8), channel_id=1, replica_groups=mesh['bt'=16,'freq'=16] {'bt'}, dimensions={0} | all-to-all | bytes 655360 | tf_op jit(solution)/shard_map/all_to_all | solution.py:672
  16.3 5.9 %collective-permute-start = (bf16[16,64,128]{2,1,0:T(8,128)(2,1)S(1)}, bf16[16,64,128]{2,1,0:T(8,128)(2,1)S(1)}, u32[]{:S(2)}, u32[]{:S(2)}) collective-permute-start(bf16[16,64,128]{2,1,0:T(8,128)(2,1)S(1)} %slice.103), channel_id=1, source_target_pairs={{0,14},{1,15},{2,0},{3,1},{4,2},{5,3},{6,4},{7,5},{8,6},{9,7},{10,... | collective-permute-start | bytes 786440 | tf_op jit(solution)/shard_map/ppermute | solution.py:685
  22.8 9.7 %cut.1 = bf16[128,64,128]{2,1,0:T(8,128)(2,1)} custom-call(s32[16,128]{1,0:T(8,128)} %fusion.10.asked, bf16[8,64,1024]{2,1,0:T(8,128)(2,1)} %bitcast.108), custom_call_target="tpu_custom_call" | custom-call | tf_op jit(solution)/shard_map/cut/pallas_call | solution.py:236
  32.5 6.4 %all-to-all-start.2 = ((bf16[16,8,64,128]{3,2,1,0:T(8,128)(2,1)}), bf16[16,8,64,128]{3,2,1,0:T(8,128)(2,1)}, u32[]{:S(2)}, u32[]{:S(2)}) async-start(bf16[16,8,64,128]{3,2,1,0:T(8,128)(2,1)} %bitcast.87), calls=%async_computation.2 | async-start | bytes 4194304 | tf_op jit(solution)/shard_map/all_to_all | solution.py:672
  39.0 3.3 %collective-permute-start.1 = (bf16[16,64,128]{2,1,0:T(8,128)(2,1)S(1)}, bf16[16,64,128]{2,1,0:T(8,128)(2,1)S(1)}, u32[]{:S(2)}, u32[]{:S(2)}) collective-permute-start(bf16[16,64,128]{2,1,0:T(8,128)(2,1)S(1)} %collective-permute-done), channel_id=1, source_target_pairs={{0,14},{1,15},{2,0},{3,1},{4,2},{5,3},{6,4},{7,5},{8,6},{9,7},{10,... | collective-permute-start | bytes 786440 | tf_op jit(solution)/shard_map/ppermute | solution.py:685
  42.3 3.8 %collective-permute-done.1 = bf16[16,64,128]{2,1,0:T(8,128)(2,1)S(1)} collective-permute-done((bf16[16,64,128]{2,1,0:T(8,128)(2,1)S(1)}, bf16[16,64,128]{2,1,0:T(8,128)(2,1)S(1)}, u32[]{:S(2)}, u32[]{:S(2)}) %collective-permute-start.1) | collective-permute-done | bytes 262176 | tf_op jit(solution)/shard_map/ppermute | solution.py:685
  46.1 3.7 %collective-permute-start.4 = (bf16[16,64,128]{2,1,0:T(8,128)(2,1)S(1)}, bf16[16,64,128]{2,1,0:T(8,128)(2,1)S(1)}, u32[]{:S(2)}, u32[]{:S(2)}) collective-permute-start(bf16[16,64,128]{2,1,0:T(8,128)(2,1)S(1)} %collective-permute-done.1), channel_id=1, source_target_pairs={{0,14},{1,15},{2,0},{3,1},{4,2},{5,3},{6,4},{7,5},{8,6},{9,7},{10,... | collective-permute-start | bytes 786440 | tf_op jit(solution)/shard_map/ppermute | solution.py:685
  50.1 3.6 %collective-permute-done.4 = bf16[16,64,128]{2,1,0:T(8,128)(2,1)S(1)} collective-permute-done((bf16[16,64,128]{2,1,0:T(8,128)(2,1)S(1)}, bf16[16,64,128]{2,1,0:T(8,128)(2,1)S(1)}, u32[]{:S(2)}, u32[]{:S(2)}) %collective-permute-start.4) | collective-permute-done | bytes 262176 | tf_op jit(solution)/shard_map/ppermute | solution.py:685
  53.7 3.8 %collective-permute-start.7 = (bf16[8,64,128]{2,1,0:T(8,128)(2,1)S(1)}, bf16[8,64,128]{2,1,0:T(8,128)(2,1)S(1)}, u32[]{:S(2)}, u32[]{:S(2)}) collective-permute-start(bf16[8,64,128]{2,1,0:T(8,128)(2,1)S(1)} %slice.105), channel_id=1, source_target_pairs={{0,14},{1,15},{2,0},{3,1},{4,2},{5,3},{6,4},{7,5},{8,6},{9,7},{10,... | collective-permute-start | bytes 393224 | tf_op jit(solution)/shard_map/ppermute | solution.py:689
  57.6 2.4 %collective-permute-done.7 = bf16[8,64,128]{2,1,0:T(8,128)(2,1)S(1)} collective-permute-done((bf16[8,64,128]{2,1,0:T(8,128)(2,1)S(1)}, bf16[8,64,128]{2,1,0:T(8,128)(2,1)S(1)}, u32[]{:S(2)}, u32[]{:S(2)}) %collective-permute-start.7) | collective-permute-done | bytes 131104 | tf_op jit(solution)/shard_map/ppermute | solution.py:689
  60.0 3.8 %collective-permute-done.6 = bf16[8,64,128]{2,1,0:T(8,128)(2,1)S(1)} collective-permute-done((bf16[8,64,128]{2,1,0:T(8,128)(2,1)S(1)}, bf16[8,64,128]{2,1,0:T(8,128)(2,1)S(1)}, u32[]{:S(2)}, u32[]{:S(2)}) %collective-permute-start.6) | collective-permute-done | bytes 131104 | tf_op jit(solution)/shard_map/ppermute | solution.py:688
  64.2 3.9 %image.5.refs_6_ = f32[16,64,128]{2,1,0:T(8,128)} custom-call(bf16[64,8,256]{2,1,0:T(8,128)(2,1)} %bitcast.90, f32[64,2,256]{2,1,0:T(2,128)} %bitcast.105), custom_call_target="tpu_custom_call" | custom-call | tf_op jit(solution)/shard_map/image/pallas_call | solution.py:364
  68.1 3.9 %image.4.refs_5_ = f32[16,64,128]{2,1,0:T(8,128)} custom-call(bf16[64,8,256]{2,1,0:T(8,128)(2,1)} %bitcast.91, f32[64,2,256]{2,1,0:T(2,128)} %bitcast.106), custom_call_target="tpu_custom_call" | custom-call | tf_op jit(solution)/shard_map/image/pallas_call | solution.py:364
  72.1 6.5 %image.3.refs_4_ = f32[32,64,128]{2,1,0:T(8,128)} custom-call(bf16[64,8,256]{2,1,0:T(8,128)(2,1)} %bitcast.92, f32[64,2,256]{2,1,0:T(2,128)} %bitcast.107), custom_call_target="tpu_custom_call" | custom-call | tf_op jit(solution)/shard_map/image/pallas_call | solution.py:364
  78.6 1.1 copy-done.3
  79.7 9.4 %patch.1 = (bf16[128,64,128]{2,1,0:T(8,128)(2,1)}, bf16[64,64,128]{2,1,0:T(8,128)(2,1)}) custom-call(s32[1]{0:T(128)} %bitcast.5.refs_0_, s32[64]{0:T(128)} %get-tuple-element.9.refs_1_, s32[2,64]{1,0:T(2,128)} %bitcast.113, s32[64]{0:T(128)} %bitcast.115, f32[32,64,128]{2,1,0:T(8,128)} %image.3.refs_4_, f32[16,64,128]{2,1,0:T(8,128)} %image.4.refs_5_, ...), custom_call_target="tpu_custom_call" | custom-call | tf_op jit(solution)/shard_map/patch/pallas_call | solution.py:510
  89.1 12.2 %screen.1 = (bf16[256,32,128]{2,1,0:T(8,128)(2,1)}, bf16[256,32,128]{2,1,0:T(8,128)(2,1)}) custom-call(s32[1]{0:T(128)} %bitcast.5.refs_0_, s32[64]{0:T(128)} %get-tuple-element.9.refs_1_, s32[2,64]{1,0:T(2,128)} %bitcast.114, s32[64]{0:T(128)} %bitcast.116, f32[32,64,128]{2,1,0:T(8,128)} %image.3.refs_4_, f32[16,64,128]{2,1,0:T(8,128)} %image.4.refs_5_, ...), custom_call_target="tpu_custom_call" | custom-call | tf_op jit(solution)/shard_map/screen/pallas_call | solution.py:650
  101.9 7.2 %all-to-all-start.1 = ((bf16[16,8,64,128]{3,2,1,0:T(8,128)(2,1)}), bf16[16,8,64,128]{3,2,1,0:T(8,128)(2,1)S(1)}, u32[]{:S(2)}, u32[]{:S(2)}) async-start(bf16[16,8,64,128]{3,2,1,0:T(8,128)(2,1)} %bitcast.101), calls=%async_computation.1 | async-start | bytes 4194304 | tf_op jit(solution)/shard_map/all_to_all | solution.py:672
  109.1 1.2 fusion.8
  110.4 3.2 %collective-permute-start.15 = (bf16[8,64,128]{2,1,0:T(8,128)(2,1)S(1)}, bf16[8,64,128]{2,1,0:T(8,128)(2,1)S(1)}, u32[]{:S(2)}, u32[]{:S(2)}) collective-permute-start(bf16[8,64,128]{2,1,0:T(8,128)(2,1)S(1)} %get-tuple-element.21), channel_id=1, source_target_pairs={{0,14},{1,15},{2,0},{3,1},{4,2},{5,3},{6,4},{7,5},{8,6},{9,7},{10,... | collective-permute-start | bytes 393224 | tf_op jit(solution)/shard_map/ppermute | solution.py:703
  113.6 2.6 %convert_add_fusion.3 = (f32[32,32,128]{2,1,0:T(8,128)S(1)}, f32[32,32,128]{2,1,0:T(8,128)S(1)}, f32[32,32,128]{2,1,0:T(8,128)S(1)}, f32[32,32,128]{2,1,0:T(8,12...) fusion(bf16[256,32,128]{2,1,0:T(8,128)(2,1)} %collective-permute-done.10, ...), kind=kLoop, calls=%fused_computation.19 | loop fusion | flops 2752512 | bytes 7340032 | tf_op jit(solution)/shard_map/add | solution.py:699
  116.3 3.7 %collective-permute-start.16 = (bf16[16,64,128]{2,1,0:T(8,128)(2,1)S(1)}, bf16[16,64,128]{2,1,0:T(8,128)(2,1)S(1)}, u32[]{:S(2)}, u32[]{:S(2)}) collective-permute-start(bf16[16,64,128]{2,1,0:T(8,128)(2,1)S(1)} %fusion), channel_id=1, source_target_pairs={{0,14},{1,15},{2,0},{3,1},{4,2},{5,3},{6,4},{7,5},{8,6},{9,7},{10,... | collective-permute-start | bytes 786440 | tf_op jit(solution)/shard_map/ppermute | solution.py:712
  120.1 3.9 %collective-permute-done.16 = bf16[16,64,128]{2,1,0:T(8,128)(2,1)S(1)} collective-permute-done((bf16[16,64,128]{2,1,0:T(8,128)(2,1)S(1)}, bf16[16,64,128]{2,1,0:T(8,128)(2,1)S(1)}, u32[]{:S(2)}, u32[]{:S(2)}) %collective-permute-start.16) | collective-permute-done | bytes 262176 | tf_op jit(solution)/shard_map/ppermute | solution.py:712
  124.1 3.8 %collective-permute-start.17 = (bf16[16,64,128]{2,1,0:T(8,128)(2,1)S(1)}, bf16[16,64,128]{2,1,0:T(8,128)(2,1)S(1)}, u32[]{:S(2)}, u32[]{:S(2)}) collective-permute-start(bf16[16,64,128]{2,1,0:T(8,128)(2,1)S(1)} %fusion.1), channel_id=1, source_target_pairs={{0,14},{1,15},{2,0},{3,1},{4,2},{5,3},{6,4},{7,5},{8,6},{9,7},{10,... | collective-permute-start | bytes 786440 | tf_op jit(solution)/shard_map/ppermute | solution.py:712
  128.0 3.7 %collective-permute-done.17 = bf16[16,64,128]{2,1,0:T(8,128)(2,1)S(1)} collective-permute-done((bf16[16,64,128]{2,1,0:T(8,128)(2,1)S(1)}, bf16[16,64,128]{2,1,0:T(8,128)(2,1)S(1)}, u32[]{:S(2)}, u32[]{:S(2)}) %collective-permute-start.17) | collective-permute-done | bytes 262176 | tf_op jit(solution)/shard_map/ppermute | solution.py:712
  131.8 3.8 %collective-permute-start.18 = (bf16[16,64,128]{2,1,0:T(8,128)(2,1)S(1)}, bf16[16,64,128]{2,1,0:T(8,128)(2,1)S(1)}, u32[]{:S(2)}, u32[]{:S(2)}) collective-permute-start(bf16[16,64,128]{2,1,0:T(8,128)(2,1)S(1)} %fusion.2), channel_id=1, source_target_pairs={{0,14},{1,15},{2,0},{3,1},{4,2},{5,3},{6,4},{7,5},{8,6},{9,7},{10,... | collective-permute-start | bytes 786440 | tf_op jit(solution)/shard_map/ppermute | solution.py:712
  135.7 3.7 %collective-permute-done.18 = bf16[16,64,128]{2,1,0:T(8,128)(2,1)S(1)} collective-permute-done((bf16[16,64,128]{2,1,0:T(8,128)(2,1)S(1)}, bf16[16,64,128]{2,1,0:T(8,128)(2,1)S(1)}, u32[]{:S(2)}, u32[]{:S(2)}) %collective-permute-start.18) | collective-permute-done | bytes 262176 | tf_op jit(solution)/shard_map/ppermute | solution.py:712
  139.5 3.8 %collective-permute-done.14 = bf16[16,64,128]{2,1,0:T(8,128)(2,1)S(1)} collective-permute-done((bf16[16,64,128]{2,1,0:T(8,128)(2,1)S(1)}, bf16[16,64,128]{2,1,0:T(8,128)(2,1)S(1)}, u32[]{:S(2)}, u32[]{:S(2)}) %collective-permute-start.14) | collective-permute-done | bytes 262176 | tf_op jit(solution)/shard_map/ppermute | solution.py:711
  144.1 7.2 %all-to-all-start.3 = ((bf16[16,64,128]{2,1,0:T(8,128)(2,1)}), bf16[16,64,128]{2,1,0:T(8,128)(2,1)S(1)}, u32[]{:S(2)}, u32[]{:S(2)}) async-start(bf16[16,64,128]{2,1,0:T(8,128)(2,1)} %fusion.7), calls=%async_computation.3 | async-start | bytes 524288 | tf_op jit(solution)/shard_map/all_to_all | solution.py:672
  151.3 8.0 %add.142 = f32[8,64,1024]{2,1,0:T(8,128)} custom-call(s32[16,128]{1,0:T(8,128)S(1)} %copy-done, bf16[128,64,128]{2,1,0:T(8,128)(2,1)S(1)} %bitcast.85), custom_call_target="tpu_custom_call" | custom-call | tf_op jit(solution)/shard_map/add/pallas_call | solution.py:298
  159.3 0.8 finish.1
  (51 shorter events, 3.5 us)
Async XLA Ops:
  16.3 22.7 %collective-permute-start = (bf16[16,64,128]{2,1,0:T(8,128)(2,1)S(1)}, bf16[16,64,128]{2,1,0:T(8,128)(2,1)S(1)}, u32[]{:S(2)}, u32[]{:S(2)}) collective-permute-start(bf16[16,64,128]{2,1,0:T(8,128)(2,1)S(1)} %slice.103), channel_id=1, source_target_pairs={{0,14},{1,15},{2,0},{3,1},{4,2},{5,3},{6,4},{7,5},{8,6},{9,7},{10,... | collective-permute-start | bytes 786440 | tf_op jit(solution)/shard_map/ppermute | solution.py:685
  22.2 20.0 %collective-permute-start.2 = (bf16[16,64,128]{2,1,0:T(8,128)(2,1)S(1)}, bf16[16,64,128]{2,1,0:T(8,128)(2,1)S(1)}, u32[]{:S(2)}, u32[]{:S(2)}) collective-permute-start(bf16[16,64,128]{2,1,0:T(8,128)(2,1)S(1)} %slice.103), channel_id=1, source_target_pairs={{0,2},{1,3},{2,4},{3,5},{4,6},{5,7},{6,8},{7,9},{8,10},{9,11},{10,... | collective-permute-start | bytes 786440 | tf_op jit(solution)/shard_map/ppermute | solution.py:684
  32.5 56.5 %all-to-all-start.2 = ((bf16[16,8,64,128]{3,2,1,0:T(8,128)(2,1)}), bf16[16,8,64,128]{3,2,1,0:T(8,128)(2,1)}, u32[]{:S(2)}, u32[]{:S(2)}) async-start(bf16[16,8,64,128]{3,2,1,0:T(8,128)(2,1)} %bitcast.87), calls=%async_computation.2 | async-start | bytes 4194304 | tf_op jit(solution)/shard_map/all_to_all | solution.py:672
  39.0 7.2 %collective-permute-start.1 = (bf16[16,64,128]{2,1,0:T(8,128)(2,1)S(1)}, bf16[16,64,128]{2,1,0:T(8,128)(2,1)S(1)}, u32[]{:S(2)}, u32[]{:S(2)}) collective-permute-start(bf16[16,64,128]{2,1,0:T(8,128)(2,1)S(1)} %collective-permute-done), channel_id=1, source_target_pairs={{0,14},{1,15},{2,0},{3,1},{4,2},{5,3},{6,4},{7,5},{8,6},{9,7},{10,... | collective-permute-start | bytes 786440 | tf_op jit(solution)/shard_map/ppermute | solution.py:685
  42.2 7.6 %collective-permute-start.3 = (bf16[16,64,128]{2,1,0:T(8,128)(2,1)S(1)}, bf16[16,64,128]{2,1,0:T(8,128)(2,1)S(1)}, u32[]{:S(2)}, u32[]{:S(2)}) collective-permute-start(bf16[16,64,128]{2,1,0:T(8,128)(2,1)S(1)} %collective-permute-done.2), channel_id=1, source_target_pairs={{0,2},{1,3},{2,4},{3,5},{4,6},{5,7},{6,8},{7,9},{8,10},{9,11},{10,... | collective-permute-start | bytes 786440 | tf_op jit(solution)/shard_map/ppermute | solution.py:684
  46.1 7.6 %collective-permute-start.4 = (bf16[16,64,128]{2,1,0:T(8,128)(2,1)S(1)}, bf16[16,64,128]{2,1,0:T(8,128)(2,1)S(1)}, u32[]{:S(2)}, u32[]{:S(2)}) collective-permute-start(bf16[16,64,128]{2,1,0:T(8,128)(2,1)S(1)} %collective-permute-done.1), channel_id=1, source_target_pairs={{0,14},{1,15},{2,0},{3,1},{4,2},{5,3},{6,4},{7,5},{8,6},{9,7},{10,... | collective-permute-start | bytes 786440 | tf_op jit(solution)/shard_map/ppermute | solution.py:685
  49.8 7.7 %collective-permute-start.5 = (bf16[16,64,128]{2,1,0:T(8,128)(2,1)S(1)}, bf16[16,64,128]{2,1,0:T(8,128)(2,1)S(1)}, u32[]{:S(2)}, u32[]{:S(2)}) collective-permute-start(bf16[16,64,128]{2,1,0:T(8,128)(2,1)S(1)} %collective-permute-done.3), channel_id=1, source_target_pairs={{0,2},{1,3},{2,4},{3,5},{4,6},{5,7},{6,8},{7,9},{8,10},{9,11},{10,... | collective-permute-start | bytes 786440 | tf_op jit(solution)/shard_map/ppermute | solution.py:684
  50.0 13.9 %copy-start.2 = (bf16[5,16,64,128]{3,2,1,0:T(8,128)(2,1)}, bf16[5,16,64,128]{3,2,1,0:T(8,128)(2,1)S(1)}, u32[]{:S(2)}) copy-start(bf16[5,16,64,128]{3,2,1,0:T(8,128)(2,1)S(1)} %bitcast_dynamic-update-slice_fusion) | copy-start | bytes 3932164
  50.0 28.6 %collective-permute-start.8 = (bf16[160,32,128]{2,1,0:T(8,128)(2,1)S(1)}, bf16[160,32,128]{2,1,0:T(8,128)(2,1)S(1)}, u32[]{:S(2)}, u32[]{:S(2)}) collective-permute-start(bf16[160,32,128]{2,1,0:T(8,128)(2,1)S(1)} %bitcast.103), channel_id=1, source_target_pairs={{0,1},{1,0},{2,3},{3,2},{4,5},{5,4},{6,7},{7,6},{8,9},{9,8},{10,11... | collective-permute-start | bytes 3932168 | tf_op jit(solution)/shard_map/ppermute | solution.py:737
  53.7 6.3 %collective-permute-start.7 = (bf16[8,64,128]{2,1,0:T(8,128)(2,1)S(1)}, bf16[8,64,128]{2,1,0:T(8,128)(2,1)S(1)}, u32[]{:S(2)}, u32[]{:S(2)}) collective-permute-start(bf16[8,64,128]{2,1,0:T(8,128)(2,1)S(1)} %slice.105), channel_id=1, source_target_pairs={{0,14},{1,15},{2,0},{3,1},{4,2},{5,3},{6,4},{7,5},{8,6},{9,7},{10,... | collective-permute-start | bytes 393224 | tf_op jit(solution)/shard_map/ppermute | solution.py:689
  57.5 6.3 %collective-permute-start.6 = (bf16[8,64,128]{2,1,0:T(8,128)(2,1)S(1)}, bf16[8,64,128]{2,1,0:T(8,128)(2,1)S(1)}, u32[]{:S(2)}, u32[]{:S(2)}) collective-permute-start(bf16[8,64,128]{2,1,0:T(8,128)(2,1)S(1)} %slice.104), channel_id=1, source_target_pairs={{0,2},{1,3},{2,4},{3,5},{4,6},{5,7},{6,8},{7,9},{8,10},{9,11},{10,... | collective-permute-start | bytes 393224 | tf_op jit(solution)/shard_map/ppermute | solution.py:688
  63.9 14.7 %copy-start.1 = (bf16[3,16,64,128]{3,2,1,0:T(8,128)(2,1)}, bf16[3,16,64,128]{3,2,1,0:T(8,128)(2,1)S(1)}, u32[]{:S(2)}) copy-start(bf16[3,16,64,128]{3,2,1,0:T(8,128)(2,1)S(1)} %pad_maximum_fusion) | copy-start | bytes 2359300
  63.9 14.7 %collective-permute-start.9 = (bf16[96,32,128]{2,1,0:T(8,128)(2,1)S(1)}, bf16[96,32,128]{2,1,0:T(8,128)(2,1)}, u32[]{:S(2)}, u32[]{:S(2)}) collective-permute-start(bf16[96,32,128]{2,1,0:T(8,128)(2,1)S(1)} %bitcast.88), channel_id=1, source_target_pairs={{0,1},{1,0},{2,3},{3,2},{4,5},{5,4},{6,7},{7,6},{8,9},{9,8},{10,11... | collective-permute-start | bytes 2359304 | tf_op jit(solution)/shard_map/ppermute | solution.py:738
  78.6 1.1 copy-start.3
  101.3 7.8 %collective-permute-start.10 = (bf16[256,32,128]{2,1,0:T(8,128)(2,1)}, bf16[256,32,128]{2,1,0:T(8,128)(2,1)}, u32[]{:S(2)}, u32[]{:S(2)}) collective-permute-start(bf16[256,32,128]{2,1,0:T(8,128)(2,1)} %get-tuple-element.13), channel_id=1, source_target_pairs={{0,1},{1,0},{2,3},{3,2},{4,5},{5,4},{6,7},{7,6},{8,9},{9,8},{10,11... | collective-permute-start | bytes 6291464 | tf_op jit(solution)/shard_map/ppermute | solution.py:749
  101.9 42.2 %all-to-all-start.1 = ((bf16[16,8,64,128]{3,2,1,0:T(8,128)(2,1)}), bf16[16,8,64,128]{3,2,1,0:T(8,128)(2,1)S(1)}, u32[]{:S(2)}, u32[]{:S(2)}) async-start(bf16[16,8,64,128]{3,2,1,0:T(8,128)(2,1)} %bitcast.101), calls=%async_computation.1 | async-start | bytes 4194304 | tf_op jit(solution)/shard_map/all_to_all | solution.py:672
  110.3 9.6 %collective-permute-start.11 = (bf16[8,64,128]{2,1,0:T(8,128)(2,1)S(1)}, bf16[8,64,128]{2,1,0:T(8,128)(2,1)S(1)}, u32[]{:S(2)}, u32[]{:S(2)}) collective-permute-start(bf16[8,64,128]{2,1,0:T(8,128)(2,1)S(1)} %get-tuple-element.20), channel_id=1, source_target_pairs={{0,2},{1,3},{2,4},{3,5},{4,6},{5,7},{6,8},{7,9},{8,10},{9,11},{10,... | collective-permute-start | bytes 393224 | tf_op jit(solution)/shard_map/ppermute | solution.py:702
  110.4 5.8 %collective-permute-start.15 = (bf16[8,64,128]{2,1,0:T(8,128)(2,1)S(1)}, bf16[8,64,128]{2,1,0:T(8,128)(2,1)S(1)}, u32[]{:S(2)}, u32[]{:S(2)}) collective-permute-start(bf16[8,64,128]{2,1,0:T(8,128)(2,1)S(1)} %get-tuple-element.21), channel_id=1, source_target_pairs={{0,14},{1,15},{2,0},{3,1},{4,2},{5,3},{6,4},{7,5},{8,6},{9,7},{10,... | collective-permute-start | bytes 393224 | tf_op jit(solution)/shard_map/ppermute | solution.py:703
  116.3 7.7 %collective-permute-start.16 = (bf16[16,64,128]{2,1,0:T(8,128)(2,1)S(1)}, bf16[16,64,128]{2,1,0:T(8,128)(2,1)S(1)}, u32[]{:S(2)}, u32[]{:S(2)}) collective-permute-start(bf16[16,64,128]{2,1,0:T(8,128)(2,1)S(1)} %fusion), channel_id=1, source_target_pairs={{0,14},{1,15},{2,0},{3,1},{4,2},{5,3},{6,4},{7,5},{8,6},{9,7},{10,... | collective-permute-start | bytes 786440 | tf_op jit(solution)/shard_map/ppermute | solution.py:712
  120.0 7.8 %collective-permute-start.12 = (bf16[16,64,128]{2,1,0:T(8,128)(2,1)S(1)}, bf16[16,64,128]{2,1,0:T(8,128)(2,1)S(1)}, u32[]{:S(2)}, u32[]{:S(2)}) collective-permute-start(bf16[16,64,128]{2,1,0:T(8,128)(2,1)S(1)} %fusion.3), channel_id=1, source_target_pairs={{0,2},{1,3},{2,4},{3,5},{4,6},{5,7},{6,8},{7,9},{8,10},{9,11},{10,... | collective-permute-start | bytes 786440 | tf_op jit(solution)/shard_map/ppermute | solution.py:711
  124.1 7.7 %collective-permute-start.17 = (bf16[16,64,128]{2,1,0:T(8,128)(2,1)S(1)}, bf16[16,64,128]{2,1,0:T(8,128)(2,1)S(1)}, u32[]{:S(2)}, u32[]{:S(2)}) collective-permute-start(bf16[16,64,128]{2,1,0:T(8,128)(2,1)S(1)} %fusion.1), channel_id=1, source_target_pairs={{0,14},{1,15},{2,0},{3,1},{4,2},{5,3},{6,4},{7,5},{8,6},{9,7},{10,... | collective-permute-start | bytes 786440 | tf_op jit(solution)/shard_map/ppermute | solution.py:712
  127.9 7.7 %collective-permute-start.13 = (bf16[16,64,128]{2,1,0:T(8,128)(2,1)S(1)}, bf16[16,64,128]{2,1,0:T(8,128)(2,1)S(1)}, u32[]{:S(2)}, u32[]{:S(2)}) collective-permute-start(bf16[16,64,128]{2,1,0:T(8,128)(2,1)S(1)} %fusion.4), channel_id=1, source_target_pairs={{0,2},{1,3},{2,4},{3,5},{4,6},{5,7},{6,8},{7,9},{8,10},{9,11},{10,... | collective-permute-start | bytes 786440 | tf_op jit(solution)/shard_map/ppermute | solution.py:711
  131.8 7.7 %collective-permute-start.18 = (bf16[16,64,128]{2,1,0:T(8,128)(2,1)S(1)}, bf16[16,64,128]{2,1,0:T(8,128)(2,1)S(1)}, u32[]{:S(2)}, u32[]{:S(2)}) collective-permute-start(bf16[16,64,128]{2,1,0:T(8,128)(2,1)S(1)} %fusion.2), channel_id=1, source_target_pairs={{0,14},{1,15},{2,0},{3,1},{4,2},{5,3},{6,4},{7,5},{8,6},{9,7},{10,... | collective-permute-start | bytes 786440 | tf_op jit(solution)/shard_map/ppermute | solution.py:712
  135.6 15.8 %copy-start = (s32[16,128]{1,0:T(8,128)S(1)}, s32[16,128]{1,0:T(8,128)}, u32[]{:S(2)}) copy-start(s32[16,128]{1,0:T(8,128)} %fusion.10.asked) | copy-start | bytes 24580
  135.6 7.7 %collective-permute-start.14 = (bf16[16,64,128]{2,1,0:T(8,128)(2,1)S(1)}, bf16[16,64,128]{2,1,0:T(8,128)(2,1)S(1)}, u32[]{:S(2)}, u32[]{:S(2)}) collective-permute-start(bf16[16,64,128]{2,1,0:T(8,128)(2,1)S(1)} %fusion.5), channel_id=1, source_target_pairs={{0,2},{1,3},{2,4},{3,5},{4,6},{5,7},{6,8},{7,9},{8,10},{9,11},{10,... | collective-permute-start | bytes 786440 | tf_op jit(solution)/shard_map/ppermute | solution.py:711
  144.1 15.2 %all-to-all-start.3 = ((bf16[16,64,128]{2,1,0:T(8,128)(2,1)}), bf16[16,64,128]{2,1,0:T(8,128)(2,1)S(1)}, u32[]{:S(2)}, u32[]{:S(2)}) async-start(bf16[16,64,128]{2,1,0:T(8,128)(2,1)} %fusion.7), calls=%async_computation.3 | async-start | bytes 524288 | tf_op jit(solution)/shard_map/all_to_all | solution.py:672
